TPU v7x, 32 devices: a whole 2x2x4 slice. The times are simulated.
32 devices in a mesh: section: 2 (over core), expert: 16 (over z, y, x).
Axes of the slice: x: 2, y: 2, z: 4, core: 2. Of those that a mesh axis runs over, the one named last changes fastest.
Arguments:
- tokens: bfloat16 [2, 2048, 2048], P('section', 'expert'), may hold values from -6 to 6
- routes: int32 [2, 2048, 2], P('section', 'expert'), may hold values from 0 to 7, all different within a row; in each aligned block of 128 rows (0 to 127, 128 to 255, ..., all dimensions but the last counted through in order) at most 64 rows name the same one
- probs: bfloat16 [2, 2048, 2], P('section', 'expert'), may hold values from 0.099609375 to 1
- cotangent: bfloat16 [2, 2048, 2048], P('section', 'expert'), may hold values from -6 to 6
- w_gate: bfloat16 [2, 2048, 6144], P('section', None, 'expert'), may hold values from -0.125 to 0.125
- w_up: bfloat16 [2, 2048, 6144], P('section', None, 'expert'), may hold values from -0.125 to 0.125
- w_down: bfloat16 [2, 6144, 2048], P('section', 'expert'), may hold values from -0.21875 to 0.21875
Outputs:
- upstream: bfloat16 [2, 2048, 2048], P('section', 'expert')
- route_grad: bfloat16 [2, 2048, 2], P('section', 'expert')
- grad_gate: bfloat16 [2, 2048, 6144], P('section', None, 'expert')
- grad_up: bfloat16 [2, 2048, 6144], P('section', None, 'expert')
- grad_down: bfloat16 [2, 6144, 2048], P('section', 'expert')
Inputs may be any that keep to these rules, and one draw needn't show every extreme that they name: `routes`: each token names 2 different experts. In each aligned block of 128 rows (the tokens of one device) no expert is named by more than 64 rows, and in some blocks one expert is named by exactly 64 rows.
All inputs are finite; a program needn't handle non-finite values.
Results may differ from a plain program's by a relative error of at most 0.008.
Values may be sent and summed in bfloat16 or wider, within the bound.
No kernel may reach another device: no remote copies, remote signals or barrier semaphores. Data moves between devices by JAX's collectives and lax.ppermute only.
A program may use at most 128 MiB of HBM per device.

v0:
```python
import functools

import jax
import jax.numpy as jnp
from jax import lax
from jax.experimental import pallas as pl
from jax.experimental.pallas import tpu as pltpu
from jax.sharding import PartitionSpec as P


AXES = ("section", "expert")
HALF, FULL = jnp.bfloat16, jnp.float32
LINE = 4
VMEM = pl.BlockSpec(memory_space=pltpu.VMEM)
SMEM = pl.BlockSpec(memory_space=pltpu.SMEM)
ANY = pl.BlockSpec(memory_space=pl.ANY)


def moved(value, target, first=0, down=0):
    sections, units = lax.axis_size("section"), lax.axis_size("expert")
    pairs = [
        (s * units + i, (s - down) * units + target(i))
        for s in range(first, sections)
        for i in range(units)
        if target(i) is not None
    ]
    return lax.ppermute(value, AXES, pairs)


def shifted(value, mask, first=0, down=0):
    return moved(value, lambda i: i ^ mask, first, down)


def groups_of(experts):
    ring = experts // LINE
    size = min(2, ring)
    head = [list(range(i, i + size)) for i in range(0, experts - size, size)]
    return head + [[o] for o in range(experts - size, experts)]


def dot(a, b, ca, cb):
    return lax.dot_general(a, b, (((ca,), (cb,)), ((), ())), preferred_element_type=FULL)


def picks(code, home, offsets, cap):
    top, rows = code.shape[0] // 2, code.shape[1]
    near = [code[k : k + 1].astype(jnp.int32) ^ home for k in range(top)]
    hits = [[n == o for n in near] for o in offsets]
    named = jnp.concatenate(
        [functools.reduce(jnp.logical_or, h).astype(FULL) for h in hits], axis=0
    )
    weight = [
        functools.reduce(
            jnp.add, [jnp.where(h[k], code[top + k : top + k + 1], 0.0) for k in range(top)]
        )
        for h in hits
    ]
    earlier = (
        lax.broadcasted_iota(jnp.int32, (rows, rows), 0)
        < lax.broadcasted_iota(jnp.int32, (rows, rows), 1)
    )
    place = dot(named.astype(HALF), earlier.astype(FULL).astype(HALF), 1, 0)
    place = jnp.where(named > 0, place, -1.0)
    slot = lax.broadcasted_iota(jnp.int32, (cap, rows), 0).astype(FULL)
    return [slot == place[i : i + 1] for i in range(len(offsets))], weight


def select_kernel(sources, ring, cap, where_ref, code_ref, *refs):
    source, out, (held, sem) = refs[:sources], refs[sources : sources + ring], refs[-2:]
    for i in range(sources):

        @pl.when(where_ref[1] == i)
        def _():
            pltpu.make_async_copy(source[i], held, sem).start()

    pick, weight = picks(code_ref[...], where_ref[0], range(ring), cap)
    pltpu.make_async_copy(source[0], held, sem).wait()
    for d in range(ring):
        rows_x = jnp.where(pick[d], 1.0, 0.0).astype(HALF)
        rows_g = jnp.where(pick[d], weight[d], 0.0).astype(HALF)
        out[d][0] = dot(rows_x, held[0], 1, 0).astype(HALF)
        out[d][1] = dot(rows_g, held[1], 1, 0).astype(HALF)


def select(where, code, sources, ring, cap):
    two, rows, width = sources[0].shape
    return pl.pallas_call(
        functools.partial(select_kernel, len(sources), ring, cap),
        out_shape=[jax.ShapeDtypeStruct((two, cap, width), HALF)] * ring,
        in_specs=[SMEM, VMEM] + [ANY] * len(sources),
        out_specs=[VMEM] * ring,
        scratch_shapes=[pltpu.VMEM((two, rows, width), HALF), pltpu.SemaphoreType.DMA],
        name="select",
    )(where, code, *sources)


def phase_kernel(size, *refs):
    near, far, (wg, wu, wd) = refs[:size], refs[size : 2 * size], refs[2 * size : 2 * size + 3]
    da_ref, db_ref, h_ref, rg_ref, *parts = refs[2 * size + 3 :]
    cap = near[0].shape[1]
    x = jnp.concatenate([r[0] for r in near + far], axis=0)
    g = jnp.concatenate([r[1] for r in near + far], axis=0)
    a = dot(x, wg[...], 1, 0)
    b = dot(x, wu[...], 1, 0)
    q = dot(g, wd[...], 1, 1)
    sig = jax.nn.sigmoid(a)
    act = a * sig
    h = (act * b).astype(HALF)
    rg_ref[...] = jnp.sum(q * h.astype(FULL), axis=1, keepdims=True)
    da = (q * b * sig * (1.0 + a * (1.0 - sig))).astype(HALF)
    db = (q * act).astype(HALF)
    h_ref[...], da_ref[...], db_ref[...] = h, da, db
    part = (dot(da, wg[...], 1, 1) + dot(db, wu[...], 1, 1)).astype(HALF)
    for i in range(size):
        for side in range(2):
            start = (side * size + i) * cap
            parts[i][side] = part[start : start + cap]


def phase(near, far, wg, wu, wd):
    size = len(near)
    _, cap, width = near[0].shape
    rows, hidden = 2 * size * cap, wg.shape[1]
    flat = jax.ShapeDtypeStruct((rows, hidden), HALF)
    da, db, h, rg, *parts = pl.pallas_call(
        functools.partial(phase_kernel, size),
        out_shape=[flat, flat, flat, jax.ShapeDtypeStruct((rows, 1), FULL)]
        + [jax.ShapeDtypeStruct((2, cap, width), HALF)] * size,
        in_specs=[VMEM] * (2 * size + 3),
        out_specs=[VMEM] * (4 + size),
        name="phase",
    )(*near, *far, wg, wu, wd)
    return da, db, h, rg.reshape(2, size, cap), parts


def grads_kernel(count, chunks, *refs):
    blocks = refs[:count]
    das, dbs, hs = (refs[count + i * chunks : count + (i + 1) * chunks] for i in range(3))
    gate_ref, up_ref, down_ref = refs[-3:]
    x = jnp.concatenate([r[0] for r in blocks], axis=0)
    g = jnp.concatenate([r[1] for r in blocks], axis=0)
    da, db, h = (jnp.concatenate([r[...] for r in refs_], axis=0) for refs_ in (das, dbs, hs))
    gate_ref[...] = dot(x, da, 0, 0).astype(HALF)
    up_ref[...] = dot(x, db, 0, 0).astype(HALF)
    down_ref[...] = dot(h, g, 0, 0).astype(HALF)


def grads(blocks, das, dbs, hs, hidden, tile=512):
    _, cap, width = blocks[0].shape
    flat = list(das) + list(dbs) + list(hs)
    return pl.pallas_call(
        functools.partial(grads_kernel, len(blocks), len(das)),
        grid=(width // tile,),
        out_shape=[
            jax.ShapeDtypeStruct((width, hidden), HALF),
            jax.ShapeDtypeStruct((width, hidden), HALF),
            jax.ShapeDtypeStruct((hidden, width), HALF),
        ],
        in_specs=[pl.BlockSpec((2, cap, tile), lambda i: (0, 0, i))] * len(blocks)
        + [pl.BlockSpec(v.shape, lambda i: (0, 0)) for v in flat],
        out_specs=[
            pl.BlockSpec((tile, hidden), lambda i: (i, 0)),
            pl.BlockSpec((tile, hidden), lambda i: (i, 0)),
            pl.BlockSpec((hidden, tile), lambda i: (0, i)),
        ],
        name="grads",
    )(*blocks, *flat)


def combine_kernel(experts, cap, where_ref, mine_ref, other_ref, *refs):
    got, (near_ref, far_ref) = refs[:experts], refs[experts:]
    for side, code_ref, out in ((0, mine_ref, near_ref), (1, other_ref, far_ref)):
        pick, _ = picks(code_ref[...], where_ref[0], range(experts), cap)
        rows = jnp.concatenate([jnp.where(p, 1.0, 0.0).astype(HALF) for p in pick], axis=0)
        back = jnp.concatenate([r[side] for r in got], axis=0)
        out[...] = dot(rows, back, 0, 0).astype(HALF)


def combine(where, mine, other, got, tile=1024):
    _, cap, width = got[0].shape
    rows = mine.shape[1]
    code = pl.BlockSpec(mine.shape, lambda i: (0, 0))
    return pl.pallas_call(
        functools.partial(combine_kernel, len(got), cap),
        grid=(width // tile,),
        out_shape=[jax.ShapeDtypeStruct((rows, width), HALF)] * 2,
        in_specs=[SMEM, code, code]
        + [pl.BlockSpec((2, cap, tile), lambda i: (0, 0, i))] * len(got),
        out_specs=[pl.BlockSpec((rows, tile), lambda i: (0, i))] * 2,
        name="combine",
    )(where, mine, other, *got)


def body(tokens, routes, probs, cotangent, w_gate, w_up, w_down):
    units = lax.axis_size("expert")
    experts = units // 2
    ring = experts // LINE
    rows, top = routes.shape[1:]
    cap = 2 * rows * top // experts
    home = lax.axis_index("expert") // 2
    line = home // ring
    wg, wu, wd = w_gate[0], w_up[0], w_down[0]
    hidden = wg.shape[1]
    inner = ((line == 1) | (line == 2)).astype(jnp.int32)
    where_one = jnp.stack([home, jnp.zeros_like(home)]).astype(jnp.int32)
    where_two = jnp.stack([home, 1 - inner]).astype(jnp.int32)

    def along(value, hops):
        step = 2 * ring

        def target(i):
            return hops[i // step] * step + i % step if i // step in hops else None

        return moved(value, target)

    own = jnp.stack([tokens[0], cotangent[0]])
    code = jnp.concatenate([routes[0].astype(FULL).T, probs[0].astype(FULL).T], axis=0)
    side1 = along(own, {0: 1, 1: 0, 2: 3, 3: 2})
    side2 = along(own, {1: 2, 2: 1})
    side3 = along(side1, {1: 2, 2: 1})
    side4 = along(side2, {1: 0, 2: 3})
    side5 = along(side3, {1: 0, 2: 3})
    codes = [code] + [shifted(code, 2 * ring * j) for j in range(1, LINE)]
    mirror = shifted(code, 1)

    sources = [(where_one, [own]), (where_one, [side1])]
    sources += [(where_two, [side3, side4]), (where_two, [side2, side5])]
    near, far = {}, {}
    for j, (where, source) in enumerate(sources):
        for d, block in enumerate(select(where, codes[j], source, ring, cap)):
            o = j * ring + d
            near[o] = block if d == 0 else shifted(block, 2 * d)
            far[o] = shifted(near[o], 1)

    das, dbs, hs, blocks, near_rg, far_rg, got = [], [], [], [], {}, {}, {}
    for group in groups_of(experts):
        near_group, far_group = [near[o] for o in group], [far[o] for o in group]
        da, db, h, rg, parts = phase(near_group, far_group, wg, wu, wd)
        das, dbs, hs = das + [da], dbs + [db], hs + [h]
        blocks += near_group + far_group
        for i, o in enumerate(group):
            near_rg[o], far_rg[o] = rg[0, i], rg[1, i]
            got[o] = parts[i] if o == 0 else shifted(parts[i], 2 * o, 1)

    g_gate, g_up, g_down = grads(blocks, das, dbs, hs, hidden)

    slots = jnp.stack([near_rg[o] for o in range(experts)])
    slots += shifted(jnp.stack([far_rg[o] for o in range(experts)]), 1)
    for bit in range(experts.bit_length() - 1):
        high = [o for o in range(experts) if o >> bit & 1]
        taken = shifted(jnp.stack([slots[o] for o in high]), 2 << bit)
        slots = jnp.stack(
            [taken[high.index(o)] if o in high else slots[o] for o in range(experts)]
        )
    near_expert = routes[0] ^ home
    names = near_expert[:, :, None] == jnp.arange(experts, dtype=jnp.int32)
    named = jnp.sum(names.astype(FULL), axis=1)
    earlier = (
        lax.broadcasted_iota(jnp.int32, (rows, rows), 1)
        < lax.broadcasted_iota(jnp.int32, (rows, rows), 0)
    )
    place = dot(earlier.astype(HALF), named.astype(HALF), 1, 0)
    place = jnp.where(named > 0, place, -1.0).T
    pick = place[:, None, :] == jnp.arange(cap, dtype=FULL)[None, :, None]
    rg_named = jnp.sum(jnp.where(pick, slots[:, :, None], 0.0), axis=1).T
    rg_token = jnp.sum(jnp.where(names, rg_named[:, None, :], 0.0), axis=2)
    route_grad = (rg_token / probs[0].astype(FULL)).astype(HALF)

    dx_near, dx_far = combine(where_one, code, mirror, [got[o] for o in range(experts)])
    below = shifted(dx_near, 0, 1, 1)
    across = shifted(dx_far, 1, 1, 1)
    upstream = (below.astype(FULL) + across.astype(FULL)).astype(HALF)
    return (upstream[None], route_grad[None], g_gate[None], g_up[None], g_down[None])


def solution(mesh):
    rows, columns = P("section", "expert", None), P("section", None, "expert")
    in_specs = (rows, rows, rows, rows, columns, columns, rows)
    out_specs = (rows, rows, columns, columns, rows)

    return jax.shard_map(body, mesh=mesh, in_specs=in_specs, out_specs=out_specs, check_vma=False)
```

profile of v0, /device:TPU:10, one launch (start us, length us, event | category | flops | bytes accessed | tf_op | source)
XLA Modules:
  0.0 253.5 jit_solution(10384088977349134924)
XLA Ops:
  0.7 1.1 constant_dynamic-update-slice_fusion.1
  1.7 1.1 constant_dynamic-update-slice_fusion.refs_0_
  3.4 4.6 %collective-permute-start.14 = (bf16[2,128,2048]{2,1,0:T(8,128)(2,1)S(1)}, bf16[2,128,2048]{2,1,0:T(8,128)(2,1)}, u32[]{:S(2)}, u32[]{:S(2)}) collective-permute-start(bf16[2,128,2048]{2,1,0:T(8,128)(2,1)S(1)} %constant_dynamic-update-slice_fusion.refs_0_), channel_id=1, source_target_pairs={{4,8},{5,9},{6,10},{7,11},{8,4},{9,5},{10,6},{11,7},{20,24},{21,25... | collective-permute-start | bytes 3145736 | tf_op jit(solution)/shard_map/ppermute | solution.py:27
  8.0 19.8 %collective-permute-done.6.refs_0_ = bf16[2,128,2048]{2,1,0:T(8,128)(2,1)S(1)} collective-permute-done((bf16[2,128,2048]{2,1,0:T(8,128)(2,1)S(1)}, bf16[2,128,2048]{2,1,0:T(8,128)(2,1)S(1)}, u32[]{:S(2)}, u32[]{:S(2)}) %collective-permute-start.6) | collective-permute-done | bytes 1048608 | tf_op jit(solution)/shard_map/ppermute | solution.py:27
  27.8 3.5 %collective-permute-start.13 = (bf16[2,128,2048]{2,1,0:T(8,128)(2,1)S(1)}, bf16[2,128,2048]{2,1,0:T(8,128)(2,1)}, u32[]{:S(2)}, u32[]{:S(2)}) collective-permute-start(bf16[2,128,2048]{2,1,0:T(8,128)(2,1)S(1)} %collective-permute-done.6.refs_0_), channel_id=1, source_target_pairs={{4,8},{5,9},{6,10},{7,11},{8,4},{9,5},{10,6},{11,7},{20,24},{21,25... | collective-permute-start | bytes 3145736 | tf_op jit(solution)/shard_map/ppermute | solution.py:27
  31.9 2.3 collective-permute-start.15
  34.2 19.8 %collective-permute-done.13.refs_0_ = bf16[2,128,2048]{2,1,0:T(8,128)(2,1)} collective-permute-done((bf16[2,128,2048]{2,1,0:T(8,128)(2,1)S(1)}, bf16[2,128,2048]{2,1,0:T(8,128)(2,1)}, u32[]{:S(2)}, u32[]{:S(2)}) %collective-permute-start.13) | collective-permute-done | bytes 1048608 | tf_op jit(solution)/shard_map/ppermute | solution.py:27
  53.9 2.3 collective-permute-start.22
  56.8 3.2 %select.12 = (bf16[2,64,2048]{2,1,0:T(8,128)(2,1)}, bf16[2,64,2048]{2,1,0:T(8,128)(2,1)}) custom-call(s32[2]{0:T(128)} %pad_add_fusion.where_ref, f32[4,128]{1,0:T(4,128)} %pad_maximum_fusion.1.code_ref.mine_ref, bf16[2,128,2048]{2,1,0:T(8,128)(2,1)} %copy-done), custom_call_target="tpu_custom_call" | custom-call | tf_op jit(solution)/shard_map/select/pallas_call | solution.py:87
  60.0 1.6 collective-permute-start.1
  62.1 15.5 %collective-permute-done.5.code_ref = f32[4,128]{1,0:T(4,128)S(1)} collective-permute-done((f32[4,128]{1,0:T(4,128)}, f32[4,128]{1,0:T(4,128)S(1)}, u32[]{:S(2)}, u32[]{:S(2)}) %collective-permute-start.5) | collective-permute-done | bytes 2080 | tf_op jit(solution)/shard_map/ppermute | solution.py:27
  77.6 3.7 %collective-permute-start.12 = (f32[4,128]{1,0:T(4,128)}, f32[4,128]{1,0:T(4,128)S(1)}, u32[]{:S(2)}, u32[]{:S(2)}) collective-permute-start(f32[4,128]{1,0:T(4,128)} %pad_maximum_fusion.1.code_ref.mine_ref), channel_id=1, source_target_pairs={{0,8},{1,9},{2,10},{3,11},{4,12},{5,13},{6,14},{7,15},{8,0},{9,1},... | collective-permute-start | bytes 6152 | tf_op jit(solution)/shard_map/ppermute | solution.py:27
  81.4 1.8 collective-permute-done.12.code_ref
  83.1 1.0 collective-permute-start.21
  84.7 3.2 %select.13 = (bf16[2,64,2048]{2,1,0:T(8,128)(2,1)}, bf16[2,64,2048]{2,1,0:T(8,128)(2,1)}) custom-call(s32[2]{0:T(128)} %pad_add_fusion.where_ref, f32[4,128]{1,0:T(4,128)} %copy-done.19, bf16[2,128,2048]{2,1,0:T(8,128)(2,1)} %copy-done.10), custom_call_target="tpu_custom_call" | custom-call | tf_op jit(solution)/shard_map/select/pallas_call | solution.py:87
  87.9 1.6 collective-permute-start.7
  90.0 3.2 %select.14 = (bf16[2,64,2048]{2,1,0:T(8,128)(2,1)}, bf16[2,64,2048]{2,1,0:T(8,128)(2,1)}) custom-call(s32[2]{0:T(128)} %pad_add_fusion.1.where_ref, f32[4,128]{1,0:T(4,128)} %copy-done.20, bf16[2,128,2048]{2,1,0:T(8,128)(2,1)} %collective-permute-done.13.refs_0_, bf16[2,128,2048]{2,1,0:T(8,128)(2,1)} %collective-permute-done.15.refs_1_), custom_call_target="tpu_custom_call" | custom-call | tf_op jit(solution)/shard_map/select/pallas_call | solution.py:87
  93.8 1.5 collective-permute-start.8
  95.3 3.2 %select.15 = (bf16[2,64,2048]{2,1,0:T(8,128)(2,1)}, bf16[2,64,2048]{2,1,0:T(8,128)(2,1)}) custom-call(s32[2]{0:T(128)} %pad_add_fusion.1.where_ref, f32[4,128]{1,0:T(4,128)} %copy-done.21, bf16[2,128,2048]{2,1,0:T(8,128)(2,1)} %collective-permute-done.14.refs_0_, bf16[2,128,2048]{2,1,0:T(8,128)(2,1)} %collective-permute-done.22.refs_1_), custom_call_target="tpu_custom_call" | custom-call | tf_op jit(solution)/shard_map/select/pallas_call | solution.py:87
  98.5 1.6 collective-permute-start.25
  100.1 2.9 %collective-permute-done.7.refs_1_.refs_5_ = bf16[2,64,2048]{2,1,0:T(8,128)(2,1)S(1)} collective-permute-done((bf16[2,64,2048]{2,1,0:T(8,128)(2,1)}, bf16[2,64,2048]{2,1,0:T(8,128)(2,1)S(1)}, u32[]{:S(2)}, u32[]{:S(2)}) %collective-permute-start.7) | collective-permute-done | bytes 524320 | tf_op jit(solution)/shard_map/ppermute | solution.py:27
  105.1 9.2 %collective-permute-done.16.refs_1_.refs_9_ = bf16[2,64,2048]{2,1,0:T(8,128)(2,1)} collective-permute-done((bf16[2,64,2048]{2,1,0:T(8,128)(2,1)}, bf16[2,64,2048]{2,1,0:T(8,128)(2,1)}, u32[]{:S(2)}, u32[]{:S(2)}) %collective-permute-start.16) | collective-permute-done | bytes 524320 | tf_op jit(solution)/shard_map/ppermute | solution.py:27
  116.4 7.0 %phase.5 = (bf16[256,384]{1,0:T(8,128)(2,1)}, bf16[256,384]{1,0:T(8,128)(2,1)}, bf16[256,384]{1,0:T(8,128)(2,1)}, f32[256,1]{1,0:T(8,128)}, bf16[2,64,2048]{2,1,0:T(8,128)(2,1)}, /*index=5*/bf16[2,64,2048]{2,1,0:T(8,128)(2,1)}) custom-call(bf16[2,64,2048]{2,1,0:T(8,128)(2,1)} %get-tuple-element.46.refs_0_, bf16[2,64,2048]{2,1,0:T(8,128)(2,1)} %copy-done.1, ...), custom_call_target="tpu_custom_call" | custom-call | tf_op jit(solution)/shard_map/phase/pallas_call | solution.py:125
  123.3 1.0 reduce
  124.4 1.3 collective-permute-start.26
  125.8 1.1 collective-permute-done.9.refs_3_.refs_7_
  126.9 7.0 %phase.6 = (bf16[256,384]{1,0:T(8,128)(2,1)}, bf16[256,384]{1,0:T(8,128)(2,1)}, bf16[256,384]{1,0:T(8,128)(2,1)}, f32[256,1]{1,0:T(8,128)}, bf16[2,64,2048]{2,1,0:T(8,128)(2,1)}, /*index=5*/bf16[2,64,2048]{2,1,0:T(8,128)(2,1)}) custom-call(bf16[2,64,2048]{2,1,0:T(8,128)(2,1)} %get-tuple-element.50.refs_0_.refs_4_, bf16[2,64,2048]{2,1,0:T(8,128)(2,1)} %copy-done.4, ...), custom_call_target="tpu_custom_call" | custom-call | tf_op jit(solution)/shard_map/phase/pallas_call | solution.py:125
  133.8 1.0 reduce.1
  134.9 3.1 %collective-permute-done.17.refs_2_.refs_10_ = bf16[2,64,2048]{2,1,0:T(8,128)(2,1)S(1)} collective-permute-done((bf16[2,64,2048]{2,1,0:T(8,128)(2,1)S(1)}, bf16[2,64,2048]{2,1,0:T(8,128)(2,1)S(1)}, u32[]{:S(2)}, u32[]{:S(2)}) %collective-permute-start.17) | collective-permute-done | bytes 524320 | tf_op jit(solution)/shard_map/ppermute | solution.py:27
  138.0 11.3 %collective-permute-done.18.refs_3_.refs_11_ = bf16[2,64,2048]{2,1,0:T(8,128)(2,1)} collective-permute-done((bf16[2,64,2048]{2,1,0:T(8,128)(2,1)}, bf16[2,64,2048]{2,1,0:T(8,128)(2,1)}, u32[]{:S(2)}, u32[]{:S(2)}) %collective-permute-start.18) | collective-permute-done | bytes 524320 | tf_op jit(solution)/shard_map/ppermute | solution.py:27
  149.3 7.0 %phase.7 = (bf16[256,384]{1,0:T(8,128)(2,1)}, bf16[256,384]{1,0:T(8,128)(2,1)}, bf16[256,384]{1,0:T(8,128)(2,1)}, f32[256,1]{1,0:T(8,128)}, bf16[2,64,2048]{2,1,0:T(8,128)(2,1)}, /*index=5*/bf16[2,64,2048]{2,1,0:T(8,128)(2,1)}) custom-call(bf16[2,64,2048]{2,1,0:T(8,128)(2,1)} %get-tuple-element.54.refs_0_.refs_8_, ...), custom_call_target="tpu_custom_call" | custom-call | tf_op jit(solution)/shard_map/phase/pallas_call | solution.py:125
  156.3 1.0 reduce.2
  157.4 3.0 %collective-permute-done.23.refs_1_.refs_13_ = bf16[2,64,2048]{2,1,0:T(8,128)(2,1)S(1)} collective-permute-done((bf16[2,64,2048]{2,1,0:T(8,128)(2,1)}, bf16[2,64,2048]{2,1,0:T(8,128)(2,1)S(1)}, u32[]{:S(2)}, u32[]{:S(2)}) %collective-permute-start.23) | collective-permute-done | bytes 524320 | tf_op jit(solution)/shard_map/ppermute | solution.py:27
  161.3 6.0 %phase.8 = (bf16[128,384]{1,0:T(8,128)(2,1)}, bf16[128,384]{1,0:T(8,128)(2,1)}, bf16[128,384]{1,0:T(8,128)(2,1)}, f32[128,1]{1,0:T(8,128)}, bf16[2,64,2048]{2,1,0:T(8,128)(2,1)}) custom-call(bf16[2,64,2048]{2,1,0:T(8,128)(2,1)} %get-tuple-element.58.refs_0_.refs_12_, bf16[2,64,2048]{2,1,0:T(8,128)(2,1)} %copy-done.8, bf16[2048,384]{1,0:T(8,128)(2,1)} %bitcast.58, ...), custom_call_target="tpu_custom_call" | custom-call | tf_op jit(solution)/shard_map/phase/pallas_call | solution.py:125
  167.3 0.9 slice_reduce_fusion.1
  168.2 0.8 copy-done.9
  169.0 5.8 %phase.9 = (bf16[128,384]{1,0:T(8,128)(2,1)}, bf16[128,384]{1,0:T(8,128)(2,1)}, bf16[128,384]{1,0:T(8,128)(2,1)}, f32[128,1]{1,0:T(8,128)}, bf16[2,64,2048]{2,1,0:T(8,128)(2,1)}) custom-call(bf16[2,64,2048]{2,1,0:T(8,128)(2,1)} %collective-permute-done.25.refs_0_.refs_14_, bf16[2,64,2048]{2,1,0:T(8,128)(2,1)} %copy-done.9, bf16[2048,384]{1,0:T(8,128)(2,1)} %bitcast.59, ...), custom_call_target="tpu_custom_call" | custom-call | tf_op jit(solution)/shard_map/phase/pallas_call | solution.py:125
  174.8 0.9 slice_reduce_fusion
  177.7 1.6 collective-permute-done.30
  180.5 2.5 collective-permute-done.31
  183.1 3.5 %collective-permute-start.32 = (f32[4,64]{1,0:T(4,128)S(1)}, f32[4,64]{1,0:T(4,128)S(1)}, u32[]{:S(2)}, u32[]{:S(2)}) collective-permute-start(f32[4,64]{1,0:T(4,128)S(1)} %pad_maximum_fusion.3), channel_id=1, source_target_pairs={{0,4},{1,5},{2,6},{3,7},{4,0},{5,1},{6,2},{7,3},{8,12},{9,13},{10,... | collective-permute-start | bytes 3080 | tf_op jit(solution)/shard_map/ppermute | solution.py:27
  189.4 1.5 collective-permute-start.27
  191.5 10.1 %grads.1 = (bf16[2048,384]{1,0:T(8,128)(2,1)}, bf16[2048,384]{1,0:T(8,128)(2,1)}, bf16[384,2048]{1,0:T(8,128)(2,1)}) custom-call(bf16[2,64,2048]{2,1,0:T(8,128)(2,1)} %get-tuple-element.46.refs_0_, bf16[2,64,2048]{2,1,0:T(8,128)(2,1)} %copy-done.1, bf16[2,64,2048]{2,1,0:T(8,128)(2,1)} %copy-done.2, bf16[2,64,2048]{2,1,0:T(8,128)(2,1)} %copy-done.5, ...), custom_call_target="tpu_custom_call" | custom-call | tf_op jit(solution)/shard_map/grads/pallas_call | solution.py:151
  202.9 4.1 %combine.1 = (bf16[128,2048]{1,0:T(8,128)(2,1)}, bf16[128,2048]{1,0:T(8,128)(2,1)}) custom-call(s32[2]{0:T(128)} %pad_add_fusion.where_ref, f32[4,128]{1,0:T(4,128)} %pad_maximum_fusion.1.code_ref.mine_ref, f32[4,128]{1,0:T(4,128)} %copy-done.18, bf16[2,64,2048]{2,1,0:T(8,128)(2,1)} %get-tuple-element.48.refs_0_, bf16[2,64,2048]{2,1,0:T(8,128)(2,1)} %copy-done.11, ...), custom_call_target="tpu_custom_call" | custom-call | tf_op jit(solution)/shard_map/combine/pallas_call | solution.py:183
  207.0 1.3 collective-permute-start.29
  208.3 1.3 collective-permute-start.28
  210.3 42.3 %collective-permute-done.29 = bf16[128,2048]{1,0:T(8,128)(2,1)S(1)} collective-permute-done((bf16[128,2048]{1,0:T(8,128)(2,1)}, bf16[128,2048]{1,0:T(8,128)(2,1)S(1)}, u32[]{:S(2)}, u32[]{:S(2)}) %collective-permute-start.29) | collective-permute-done | bytes 524320 | tf_op jit(solution)/shard_map/ppermute | solution.py:27
  252.6 0.9 fusion
  (114 shorter events, 17.6 us)
Async XLA Ops:
  0.6 33.5 %copy-start.22 = (s32[1,128,2]{1,2,0:T(2,128)S(1)}, s32[1,128,2]{1,2,0:T(2,128)}, u32[]{:S(2)}) copy-start(s32[1,128,2]{1,2,0:T(2,128)} %param.8) | copy-start | bytes 3076
  0.6 55.6 %copy-start.23 = (bf16[1,128,2]{1,2,0:T(2,128)(2,1)S(1)}, bf16[1,128,2]{1,2,0:T(2,128)(2,1)}, u32[]{:S(2)}) copy-start(bf16[1,128,2]{1,2,0:T(2,128)(2,1)} %param.9) | copy-start | bytes 1540
  2.8 54.0 %copy-start = (bf16[2,128,2048]{2,1,0:T(8,128)(2,1)}, bf16[2,128,2048]{2,1,0:T(8,128)(2,1)S(1)}, u32[]{:S(2)}) copy-start(bf16[2,128,2048]{2,1,0:T(8,128)(2,1)S(1)} %constant_dynamic-update-slice_fusion.refs_0_) | copy-start | bytes 3145732
  2.8 25.0 %collective-permute-start.6 = (bf16[2,128,2048]{2,1,0:T(8,128)(2,1)S(1)}, bf16[2,128,2048]{2,1,0:T(8,128)(2,1)S(1)}, u32[]{:S(2)}, u32[]{:S(2)}) collective-permute-start(bf16[2,128,2048]{2,1,0:T(8,128)(2,1)S(1)} %constant_dynamic-update-slice_fusion.refs_0_), channel_id=1, source_target_pairs={{0,4},{1,5},{2,6},{3,7},{4,0},{5,1},{6,2},{7,3},{8,12},{9,13},{10,... | collective-permute-start | bytes 3145736 | tf_op jit(solution)/shard_map/ppermute | solution.py:27
  3.4 28.5 %collective-permute-start.14 = (bf16[2,128,2048]{2,1,0:T(8,128)(2,1)S(1)}, bf16[2,128,2048]{2,1,0:T(8,128)(2,1)}, u32[]{:S(2)}, u32[]{:S(2)}) collective-permute-start(bf16[2,128,2048]{2,1,0:T(8,128)(2,1)S(1)} %constant_dynamic-update-slice_fusion.refs_0_), channel_id=1, source_target_pairs={{4,8},{5,9},{6,10},{7,11},{8,4},{9,5},{10,6},{11,7},{20,24},{21,25... | collective-permute-start | bytes 3145736 | tf_op jit(solution)/shard_map/ppermute | solution.py:27
  27.8 56.9 %copy-start.10 = (bf16[2,128,2048]{2,1,0:T(8,128)(2,1)}, bf16[2,128,2048]{2,1,0:T(8,128)(2,1)S(1)}, u32[]{:S(2)}) copy-start(bf16[2,128,2048]{2,1,0:T(8,128)(2,1)S(1)} %collective-permute-done.6.refs_0_) | copy-start | bytes 3145732
  27.8 26.1 %collective-permute-start.13 = (bf16[2,128,2048]{2,1,0:T(8,128)(2,1)S(1)}, bf16[2,128,2048]{2,1,0:T(8,128)(2,1)}, u32[]{:S(2)}, u32[]{:S(2)}) collective-permute-start(bf16[2,128,2048]{2,1,0:T(8,128)(2,1)S(1)} %collective-permute-done.6.refs_0_), channel_id=1, source_target_pairs={{4,8},{5,9},{6,10},{7,11},{8,4},{9,5},{10,6},{11,7},{20,24},{21,25... | collective-permute-start | bytes 3145736 | tf_op jit(solution)/shard_map/ppermute | solution.py:27
  31.9 57.6 %collective-permute-start.15 = (bf16[2,128,2048]{2,1,0:T(8,128)(2,1)}, bf16[2,128,2048]{2,1,0:T(8,128)(2,1)}, u32[]{:S(2)}, u32[]{:S(2)}) collective-permute-start(bf16[2,128,2048]{2,1,0:T(8,128)(2,1)} %collective-permute-done.14.refs_0_), channel_id=1, source_target_pairs={{4,0},{5,1},{6,2},{7,3},{8,12},{9,13},{10,14},{11,15},{20,16},{21,... | collective-permute-start | bytes 3145736 | tf_op jit(solution)/shard_map/ppermute | solution.py:27
  53.9 39.9 %collective-permute-start.22 = (bf16[2,128,2048]{2,1,0:T(8,128)(2,1)}, bf16[2,128,2048]{2,1,0:T(8,128)(2,1)}, u32[]{:S(2)}, u32[]{:S(2)}) collective-permute-start(bf16[2,128,2048]{2,1,0:T(8,128)(2,1)} %collective-permute-done.13.refs_0_), channel_id=1, source_target_pairs={{4,0},{5,1},{6,2},{7,3},{8,12},{9,13},{10,14},{11,15},{20,16},{21,... | collective-permute-start | bytes 3145736 | tf_op jit(solution)/shard_map/ppermute | solution.py:27
  60.0 27.9 %collective-permute-start.1 = (bf16[2,64,2048]{2,1,0:T(8,128)(2,1)}, bf16[2,64,2048]{2,1,0:T(8,128)(2,1)S(1)}, u32[]{:S(2)}, u32[]{:S(2)}) collective-permute-start(bf16[2,64,2048]{2,1,0:T(8,128)(2,1)} %get-tuple-element.47), channel_id=1, source_target_pairs={{0,2},{1,3},{2,0},{3,1},{4,6},{5,7},{6,4},{7,5},{8,10},{9,11},{10,... | collective-permute-start | bytes 1572872 | tf_op jit(solution)/shard_map/ppermute | solution.py:27
  61.6 36.9 %collective-permute-start.2 = (bf16[2,64,2048]{2,1,0:T(8,128)(2,1)}, bf16[2,64,2048]{2,1,0:T(8,128)(2,1)S(1)}, u32[]{:S(2)}, u32[]{:S(2)}) collective-permute-start(bf16[2,64,2048]{2,1,0:T(8,128)(2,1)} %get-tuple-element.46.refs_0_), channel_id=1, source_target_pairs={{0,1},{1,0},{2,3},{3,2},{4,5},{5,4},{6,7},{7,6},{8,9},{9,8},{10,11... | collective-permute-start | bytes 1572872 | tf_op jit(solution)/shard_map/ppermute | solution.py:27
  62.1 15.5 %collective-permute-start.5 = (f32[4,128]{1,0:T(4,128)}, f32[4,128]{1,0:T(4,128)S(1)}, u32[]{:S(2)}, u32[]{:S(2)}) collective-permute-start(f32[4,128]{1,0:T(4,128)} %pad_maximum_fusion.1.code_ref.mine_ref), channel_id=1, source_target_pairs={{0,4},{1,5},{2,6},{3,7},{4,0},{5,1},{6,2},{7,3},{8,12},{9,13},{10,... | collective-permute-start | bytes 6152 | tf_op jit(solution)/shard_map/ppermute | solution.py:27
  77.6 5.5 %collective-permute-start.12 = (f32[4,128]{1,0:T(4,128)}, f32[4,128]{1,0:T(4,128)S(1)}, u32[]{:S(2)}, u32[]{:S(2)}) collective-permute-start(f32[4,128]{1,0:T(4,128)} %pad_maximum_fusion.1.code_ref.mine_ref), channel_id=1, source_target_pairs={{0,8},{1,9},{2,10},{3,11},{4,12},{5,13},{6,14},{7,15},{8,0},{9,1},... | collective-permute-start | bytes 6152 | tf_op jit(solution)/shard_map/ppermute | solution.py:27
  83.1 10.1 %collective-permute-start.21 = (f32[4,128]{1,0:T(4,128)}, f32[4,128]{1,0:T(4,128)S(1)}, u32[]{:S(2)}, u32[]{:S(2)}) collective-permute-start(f32[4,128]{1,0:T(4,128)} %pad_maximum_fusion.1.code_ref.mine_ref), channel_id=1, source_target_pairs={{0,12},{1,13},{2,14},{3,15},{4,8},{5,9},{6,10},{7,11},{8,4},{9,5},... | collective-permute-start | bytes 6152 | tf_op jit(solution)/shard_map/ppermute | solution.py:27
  87.9 15.1 %collective-permute-start.7 = (bf16[2,64,2048]{2,1,0:T(8,128)(2,1)}, bf16[2,64,2048]{2,1,0:T(8,128)(2,1)S(1)}, u32[]{:S(2)}, u32[]{:S(2)}) collective-permute-start(bf16[2,64,2048]{2,1,0:T(8,128)(2,1)} %get-tuple-element.51), channel_id=1, source_target_pairs={{0,2},{1,3},{2,0},{3,1},{4,6},{5,7},{6,4},{7,5},{8,10},{9,11},{10,... | collective-permute-start | bytes 1572872 | tf_op jit(solution)/shard_map/ppermute | solution.py:27
  89.5 14.8 %collective-permute-start.3 = (bf16[2,64,2048]{2,1,0:T(8,128)(2,1)S(1)}, bf16[2,64,2048]{2,1,0:T(8,128)(2,1)S(1)}, u32[]{:S(2)}, u32[]{:S(2)}) collective-permute-start(bf16[2,64,2048]{2,1,0:T(8,128)(2,1)S(1)} %collective-permute-done.1.refs_1_), channel_id=1, source_target_pairs={{0,1},{1,0},{2,3},{3,2},{4,5},{5,4},{6,7},{7,6},{8,9},{9,8},{10,11... | collective-permute-start | bytes 1572872 | tf_op jit(solution)/shard_map/ppermute | solution.py:27
  93.2 11.1 %copy-start.6 = (bf16[2,64,2048]{2,1,0:T(8,128)(2,1)S(1)}, bf16[2,64,2048]{2,1,0:T(8,128)(2,1)}, u32[]{:S(2)}) copy-start(bf16[2,64,2048]{2,1,0:T(8,128)(2,1)} %get-tuple-element.54.refs_0_.refs_8_) | copy-start | bytes 1572868
  93.2 21.1 %collective-permute-start.16 = (bf16[2,64,2048]{2,1,0:T(8,128)(2,1)}, bf16[2,64,2048]{2,1,0:T(8,128)(2,1)}, u32[]{:S(2)}, u32[]{:S(2)}) collective-permute-start(bf16[2,64,2048]{2,1,0:T(8,128)(2,1)} %get-tuple-element.55), channel_id=1, source_target_pairs={{0,2},{1,3},{2,0},{3,1},{4,6},{5,7},{6,4},{7,5},{8,10},{9,11},{10,... | collective-permute-start | bytes 1572872 | tf_op jit(solution)/shard_map/ppermute | solution.py:27
  93.8 21.8 %collective-permute-start.8 = (bf16[2,64,2048]{2,1,0:T(8,128)(2,1)S(1)}, bf16[2,64,2048]{2,1,0:T(8,128)(2,1)}, u32[]{:S(2)}, u32[]{:S(2)}) collective-permute-start(bf16[2,64,2048]{2,1,0:T(8,128)(2,1)S(1)} %copy-done.3), channel_id=1, source_target_pairs={{0,1},{1,0},{2,3},{3,2},{4,5},{5,4},{6,7},{7,6},{8,9},{9,8},{10,11... | collective-permute-start | bytes 1572872 | tf_op jit(solution)/shard_map/ppermute | solution.py:27
  98.5 17.9 %copy-start.2 = (bf16[2,64,2048]{2,1,0:T(8,128)(2,1)}, bf16[2,64,2048]{2,1,0:T(8,128)(2,1)S(1)}, u32[]{:S(2)}) copy-start(bf16[2,64,2048]{2,1,0:T(8,128)(2,1)S(1)} %collective-permute-done.2.refs_2_) | copy-start | bytes 1572868
  98.5 25.9 %collective-permute-start.25 = (bf16[2,64,2048]{2,1,0:T(8,128)(2,1)}, bf16[2,64,2048]{2,1,0:T(8,128)(2,1)}, u32[]{:S(2)}, u32[]{:S(2)}) collective-permute-start(bf16[2,64,2048]{2,1,0:T(8,128)(2,1)} %get-tuple-element.60), channel_id=1, source_target_pairs={{0,2},{1,3},{2,0},{3,1},{4,6},{5,7},{6,4},{7,5},{8,10},{9,11},{10,... | collective-permute-start | bytes 1572872 | tf_op jit(solution)/shard_map/ppermute | solution.py:27
  103.0 20.3 %copy-start.4 = (bf16[2,64,2048]{2,1,0:T(8,128)(2,1)}, bf16[2,64,2048]{2,1,0:T(8,128)(2,1)S(1)}, u32[]{:S(2)}) copy-start(bf16[2,64,2048]{2,1,0:T(8,128)(2,1)S(1)} %collective-permute-done.7.refs_1_.refs_5_) | copy-start | bytes 1572868
  103.0 23.9 %collective-permute-start.9 = (bf16[2,64,2048]{2,1,0:T(8,128)(2,1)S(1)}, bf16[2,64,2048]{2,1,0:T(8,128)(2,1)}, u32[]{:S(2)}, u32[]{:S(2)}) collective-permute-start(bf16[2,64,2048]{2,1,0:T(8,128)(2,1)S(1)} %collective-permute-done.7.refs_1_.refs_5_), channel_id=1, source_target_pairs={{0,1},{1,0},{2,3},{3,2},{4,5},{5,4},{6,7},{7,6},{8,9},{9,8},{10,11... | collective-permute-start | bytes 1572872 | tf_op jit(solution)/shard_map/ppermute | solution.py:27
  104.3 12.1 %copy-start.5 = (bf16[2,64,2048]{2,1,0:T(8,128)(2,1)}, bf16[2,64,2048]{2,1,0:T(8,128)(2,1)S(1)}, u32[]{:S(2)}) copy-start(bf16[2,64,2048]{2,1,0:T(8,128)(2,1)S(1)} %collective-permute-done.3.refs_3_) | copy-start | bytes 1572868
  104.3 33.7 %collective-permute-start.17 = (bf16[2,64,2048]{2,1,0:T(8,128)(2,1)S(1)}, bf16[2,64,2048]{2,1,0:T(8,128)(2,1)S(1)}, u32[]{:S(2)}, u32[]{:S(2)}) collective-permute-start(bf16[2,64,2048]{2,1,0:T(8,128)(2,1)S(1)} %copy-done.6), channel_id=1, source_target_pairs={{0,1},{1,0},{2,3},{3,2},{4,5},{5,4},{6,7},{7,6},{8,9},{9,8},{10,11... | collective-permute-start | bytes 1572872 | tf_op jit(solution)/shard_map/ppermute | solution.py:27
  114.3 35.0 %collective-permute-start.18 = (bf16[2,64,2048]{2,1,0:T(8,128)(2,1)}, bf16[2,64,2048]{2,1,0:T(8,128)(2,1)}, u32[]{:S(2)}, u32[]{:S(2)}) collective-permute-start(bf16[2,64,2048]{2,1,0:T(8,128)(2,1)} %collective-permute-done.16.refs_1_.refs_9_), channel_id=1, source_target_pairs={{0,1},{1,0},{2,3},{3,2},{4,5},{5,4},{6,7},{7,6},{8,9},{9,8},{10,11... | collective-permute-start | bytes 1572872 | tf_op jit(solution)/shard_map/ppermute | solution.py:27
  115.6 44.8 %collective-permute-start.23 = (bf16[2,64,2048]{2,1,0:T(8,128)(2,1)}, bf16[2,64,2048]{2,1,0:T(8,128)(2,1)S(1)}, u32[]{:S(2)}, u32[]{:S(2)}) collective-permute-start(bf16[2,64,2048]{2,1,0:T(8,128)(2,1)} %get-tuple-element.58.refs_0_.refs_12_), channel_id=1, source_target_pairs={{0,1},{1,0},{2,3},{3,2},{4,5},{5,4},{6,7},{7,6},{8,9},{9,8},{10,11... | collective-permute-start | bytes 1572872 | tf_op jit(solution)/shard_map/ppermute | solution.py:27
  124.4 43.7 %collective-permute-start.26 = (bf16[2,64,2048]{2,1,0:T(8,128)(2,1)}, bf16[2,64,2048]{2,1,0:T(8,128)(2,1)S(1)}, u32[]{:S(2)}, u32[]{:S(2)}) collective-permute-start(bf16[2,64,2048]{2,1,0:T(8,128)(2,1)} %collective-permute-done.25.refs_0_.refs_14_), channel_id=1, source_target_pairs={{0,1},{1,0},{2,3},{3,2},{4,5},{5,4},{6,7},{7,6},{8,9},{9,8},{10,11... | collective-permute-start | bytes 1572872 | tf_op jit(solution)/shard_map/ppermute | solution.py:27
  138.0 11.3 %copy-start.7 = (bf16[2,64,2048]{2,1,0:T(8,128)(2,1)}, bf16[2,64,2048]{2,1,0:T(8,128)(2,1)S(1)}, u32[]{:S(2)}) copy-start(bf16[2,64,2048]{2,1,0:T(8,128)(2,1)S(1)} %collective-permute-done.17.refs_2_.refs_10_) | copy-start | bytes 1572868
  168.1 11.8 %copy-start.17 = (f32[4,128]{1,0:T(4,128)S(1)}, f32[4,128]{1,0:T(4,128)}, u32[]{:S(2)}) copy-start(f32[4,128]{1,0:T(4,128)} %pad_maximum_fusion.1.code_ref.mine_ref) | copy-start | bytes 6148
  175.7 3.7 %collective-permute-start.30 = (f32[8,64]{1,0:T(8,128)S(1)}, f32[8,64]{1,0:T(8,128)S(1)}, u32[]{:S(2)}, u32[]{:S(2)}) collective-permute-start(f32[8,64]{1,0:T(8,128)S(1)} %stack.42), channel_id=1, source_target_pairs={{0,1},{1,0},{2,3},{3,2},{4,5},{5,4},{6,7},{7,6},{8,9},{9,8},{10,11... | collective-permute-start | bytes 6152 | tf_op jit(solution)/shard_map/ppermute | solution.py:27
  176.3 11.6 %collective-permute-start.4 = (bf16[2,64,2048]{2,1,0:T(8,128)(2,1)S(1)}, bf16[2,64,2048]{2,1,0:T(8,128)(2,1)S(1)}, u32[]{:S(2)}, u32[]{:S(2)}) collective-permute-start(bf16[2,64,2048]{2,1,0:T(8,128)(2,1)S(1)} %copy-done.24), channel_id=1, source_target_pairs={{16,18},{17,19},{18,16},{19,17},{20,22},{21,23},{22,20},{23,21},{2... | collective-permute-start | bytes 1572872 | tf_op jit(solution)/shard_map/ppermute | solution.py:27
  177.0 11.7 %collective-permute-start.10 = (bf16[2,64,2048]{2,1,0:T(8,128)(2,1)}, bf16[2,64,2048]{2,1,0:T(8,128)(2,1)S(1)}, u32[]{:S(2)}, u32[]{:S(2)}) collective-permute-start(bf16[2,64,2048]{2,1,0:T(8,128)(2,1)} %get-tuple-element.52), channel_id=1, source_target_pairs={{16,20},{17,21},{18,22},{19,23},{20,16},{21,17},{22,18},{23,19},{2... | collective-permute-start | bytes 1572872 | tf_op jit(solution)/shard_map/ppermute | solution.py:27
  179.4 3.7 %collective-permute-start.31 = (f32[4,64]{1,0:T(4,128)S(1)}, f32[4,64]{1,0:T(4,128)S(1)}, u32[]{:S(2)}, u32[]{:S(2)}) collective-permute-start(f32[4,64]{1,0:T(4,128)S(1)} %pad_maximum_fusion.2), channel_id=1, source_target_pairs={{0,2},{1,3},{2,0},{3,1},{4,6},{5,7},{6,4},{7,5},{8,10},{9,11},{10,... | collective-permute-start | bytes 3080 | tf_op jit(solution)/shard_map/ppermute | solution.py:27
  180.0 7.2 %collective-permute-start = (f32[4,128]{1,0:T(4,128)S(1)}, f32[4,128]{1,0:T(4,128)S(1)}, u32[]{:S(2)}, u32[]{:S(2)}) collective-permute-start(f32[4,128]{1,0:T(4,128)S(1)} %copy-done.17), channel_id=1, source_target_pairs={{0,1},{1,0},{2,3},{3,2},{4,5},{5,4},{6,7},{7,6},{8,9},{9,8},{10,11... | collective-permute-start | bytes 6152 | tf_op jit(solution)/shard_map/ppermute | solution.py:27
  183.1 6.3 %collective-permute-start.32 = (f32[4,64]{1,0:T(4,128)S(1)}, f32[4,64]{1,0:T(4,128)S(1)}, u32[]{:S(2)}, u32[]{:S(2)}) collective-permute-start(f32[4,64]{1,0:T(4,128)S(1)} %pad_maximum_fusion.3), channel_id=1, source_target_pairs={{0,4},{1,5},{2,6},{3,7},{4,0},{5,1},{6,2},{7,3},{8,12},{9,13},{10,... | collective-permute-start | bytes 3080 | tf_op jit(solution)/shard_map/ppermute | solution.py:27
  186.5 4.5 %collective-permute-start.11 = (bf16[2,64,2048]{2,1,0:T(8,128)(2,1)}, bf16[2,64,2048]{2,1,0:T(8,128)(2,1)S(1)}, u32[]{:S(2)}, u32[]{:S(2)}) collective-permute-start(bf16[2,64,2048]{2,1,0:T(8,128)(2,1)} %get-tuple-element.53), channel_id=1, source_target_pairs={{16,22},{17,23},{18,20},{19,21},{20,18},{21,19},{22,16},{23,17},{2... | collective-permute-start | bytes 1572872 | tf_op jit(solution)/shard_map/ppermute | solution.py:27
  187.2 14.4 %copy-start.18 = (f32[4,128]{1,0:T(4,128)}, f32[4,128]{1,0:T(4,128)S(1)}, u32[]{:S(2)}) copy-start(f32[4,128]{1,0:T(4,128)S(1)} %collective-permute-done.other_ref) | copy-start | bytes 6148
  187.2 14.5 %collective-permute-start.19 = (bf16[2,64,2048]{2,1,0:T(8,128)(2,1)}, bf16[2,64,2048]{2,1,0:T(8,128)(2,1)S(1)}, u32[]{:S(2)}, u32[]{:S(2)}) collective-permute-start(bf16[2,64,2048]{2,1,0:T(8,128)(2,1)} %get-tuple-element.56), channel_id=1, source_target_pairs={{16,24},{17,25},{18,26},{19,27},{20,28},{21,29},{22,30},{23,31},{2... | collective-permute-start | bytes 1572872 | tf_op jit(solution)/shard_map/ppermute | solution.py:27
  188.0 13.7 %copy-start.11 = (bf16[2,64,2048]{2,1,0:T(8,128)(2,1)}, bf16[2,64,2048]{2,1,0:T(8,128)(2,1)S(1)}, u32[]{:S(2)}) copy-start(bf16[2,64,2048]{2,1,0:T(8,128)(2,1)S(1)} %collective-permute-done.4.refs_1_) | copy-start | bytes 1572868
  188.0 13.8 %collective-permute-start.20 = (bf16[2,64,2048]{2,1,0:T(8,128)(2,1)}, bf16[2,64,2048]{2,1,0:T(8,128)(2,1)S(1)}, u32[]{:S(2)}, u32[]{:S(2)}) collective-permute-start(bf16[2,64,2048]{2,1,0:T(8,128)(2,1)} %get-tuple-element.57), channel_id=1, source_target_pairs={{16,26},{17,27},{18,24},{19,25},{20,30},{21,31},{22,28},{23,29},{2... | collective-permute-start | bytes 1572872 | tf_op jit(solution)/shard_map/ppermute | solution.py:27
  188.7 13.0 %copy-start.12 = (bf16[2,64,2048]{2,1,0:T(8,128)(2,1)}, bf16[2,64,2048]{2,1,0:T(8,128)(2,1)S(1)}, u32[]{:S(2)}) copy-start(bf16[2,64,2048]{2,1,0:T(8,128)(2,1)S(1)} %collective-permute-done.10.refs_2_) | copy-start | bytes 1572868
  188.7 13.0 %collective-permute-start.24 = (bf16[2,64,2048]{2,1,0:T(8,128)(2,1)}, bf16[2,64,2048]{2,1,0:T(8,128)(2,1)S(1)}, u32[]{:S(2)}, u32[]{:S(2)}) collective-permute-start(bf16[2,64,2048]{2,1,0:T(8,128)(2,1)} %get-tuple-element.59), channel_id=1, source_target_pairs={{16,28},{17,29},{18,30},{19,31},{20,24},{21,25},{22,26},{23,27},{2... | collective-permute-start | bytes 1572872 | tf_op jit(solution)/shard_map/ppermute | solution.py:27
  189.4 12.4 %collective-permute-start.27 = (bf16[2,64,2048]{2,1,0:T(8,128)(2,1)}, bf16[2,64,2048]{2,1,0:T(8,128)(2,1)}, u32[]{:S(2)}, u32[]{:S(2)}) collective-permute-start(bf16[2,64,2048]{2,1,0:T(8,128)(2,1)} %get-tuple-element.61), channel_id=1, source_target_pairs={{16,30},{17,31},{18,28},{19,29},{20,26},{21,27},{22,24},{23,25},{2... | collective-permute-start | bytes 1572872 | tf_op jit(solution)/shard_map/ppermute | solution.py:27
  191.0 10.6 %copy-start.13 = (bf16[2,64,2048]{2,1,0:T(8,128)(2,1)}, bf16[2,64,2048]{2,1,0:T(8,128)(2,1)S(1)}, u32[]{:S(2)}) copy-start(bf16[2,64,2048]{2,1,0:T(8,128)(2,1)S(1)} %collective-permute-done.11.refs_3_) | copy-start | bytes 1572868
  191.1 18.5 %collective-permute-start.33 = (f32[4,64]{1,0:T(4,128)S(1)}, f32[4,64]{1,0:T(4,128)S(1)}, u32[]{:S(2)}, u32[]{:S(2)}) collective-permute-start(f32[4,64]{1,0:T(4,128)S(1)} %pad_maximum_fusion.4), channel_id=1, source_target_pairs={{0,8},{1,9},{2,10},{3,11},{4,12},{5,13},{6,14},{7,15},{8,0},{9,1},... | collective-permute-start | bytes 3080 | tf_op jit(solution)/shard_map/ppermute | solution.py:27
  207.0 45.7 %collective-permute-start.29 = (bf16[128,2048]{1,0:T(8,128)(2,1)}, bf16[128,2048]{1,0:T(8,128)(2,1)S(1)}, u32[]{:S(2)}, u32[]{:S(2)}) collective-permute-start(bf16[128,2048]{1,0:T(8,128)(2,1)} %get-tuple-element.63), channel_id=1, source_target_pairs={{16,1},{17,0},{18,3},{19,2},{20,5},{21,4},{22,7},{23,6},{24,9},{25... | collective-permute-start | bytes 1572872 | tf_op jit(solution)/shard_map/ppermute | solution.py:27
  208.3 44.4 %collective-permute-start.28 = (bf16[128,2048]{1,0:T(8,128)(2,1)}, bf16[128,2048]{1,0:T(8,128)(2,1)S(1)}, u32[]{:S(2)}, u32[]{:S(2)}) collective-permute-start(bf16[128,2048]{1,0:T(8,128)(2,1)} %get-tuple-element.62), channel_id=1, source_target_pairs={{16,0},{17,1},{18,2},{19,3},{20,4},{21,5},{22,6},{23,7},{24,8},{25... | collective-permute-start | bytes 1572872 | tf_op jit(solution)/shard_map/ppermute | solution.py:27
  (11 other events, 45.3 us)
where the time goes:
time: 254 us
  waiting for transfers between devices  136 us (54%)
  Pallas kernels  59.6 us (23%)
  starting transfers between devices  43.5 us (17%)
  local copies, waits for them, and re-layouts  7.08 us (3%)
  other arithmetic  6.44 us (3%)
    ppermute x34, waiting for transfers between devices, moved(): return lax.ppermute(value, AXES, pairs)  136 us
    ppermute x34, starting transfers between devices, moved(): return lax.ppermute(value, AXES, pairs)  43.5 us
    pallas_call x5, Pallas kernels, phase(): pl.pallas_call(functools.partial(phase_kernel, size), out_shape=[flat, fl...  32.7 us
    pallas_call x4, Pallas kernels, select(): pl.pallas_call(functools.partial(select_kernel, len(sources), ring, cap),...  12.7 us
    pallas_call x1, Pallas kernels, grads(): pl.pallas_call(functools.partial(grads_kernel, len(blocks), len(das)), gr...  10.1 us
  transfers between devices with their start and end apart: 34, of which 15 were waited for; matrix products, arithmetic and copies ran while one was open for 3% of the time, Pallas kernels for 21%

commit v1 on v0

v1 whole, which is shorter than its diff:
```python
import functools

import jax
import jax.numpy as jnp
from jax import lax
from jax.experimental import pallas as pl
from jax.experimental.pallas import tpu as pltpu
from jax.sharding import PartitionSpec as P


AXES = ("section", "expert")
HALF, FULL = jnp.bfloat16, jnp.float32
LINE = 4
VMEM = pl.BlockSpec(memory_space=pltpu.VMEM)
ANY = pl.BlockSpec(memory_space=pl.ANY)
ROOM = pltpu.CompilerParams(vmem_limit_bytes=28 << 20)


def moved(value, target, first=0, down=0):
    sections, units = lax.axis_size("section"), lax.axis_size("expert")
    pairs = [
        (s * units + i, (s - down) * units + target(i))
        for s in range(first, sections)
        for i in range(units)
        if target(i) is not None
    ]
    return lax.ppermute(value, AXES, pairs)


def shifted(value, mask, first=0, down=0):
    return moved(value, lambda i: i ^ mask, first, down)


def groups_of(experts):
    ring = experts // LINE
    head = [list(range(2 * ring)), list(range(2 * ring, experts - 2))]
    return [group for group in head if group] + [[experts - 2], [experts - 1]]


def kept(shape, kind):
    return pltpu.VMEM(shape, kind)


def position(experts):
    home = lax.axis_index("expert") // 2
    line = home // (experts // LINE)
    return home, jnp.logical_or(line == 1, line == 2)


def dot(a, b, ca, cb):
    return lax.dot_general(a, b, (((ca,), (cb,)), ((), ())), preferred_element_type=FULL)


def picks(code, home, offsets, cap):
    top, rows = code.shape[0] // 2, code.shape[1]
    near = [code[k : k + 1].astype(jnp.int32) ^ home for k in range(top)]
    hits = [[n == o for n in near] for o in offsets]
    named = jnp.concatenate(
        [functools.reduce(jnp.logical_or, h).astype(FULL) for h in hits], axis=0
    )
    weight = [
        functools.reduce(
            jnp.add, [jnp.where(h[k], code[top + k : top + k + 1], 0.0) for k in range(top)]
        )
        for h in hits
    ]
    earlier = (
        lax.broadcasted_iota(jnp.int32, (rows, rows), 0)
        < lax.broadcasted_iota(jnp.int32, (rows, rows), 1)
    )
    place = dot(named.astype(HALF), earlier.astype(FULL).astype(HALF), 1, 0)
    place = jnp.where(named > 0, place, -1.0)
    slot = lax.broadcasted_iota(jnp.int32, (cap, rows), 0).astype(FULL)
    return [slot == place[i : i + 1] for i in range(len(offsets))], weight


def load_kernel(*refs):
    count, sem = len(refs) // 2, refs[-1]
    copies = [pltpu.make_async_copy(refs[i], refs[count + i], sem.at[i]) for i in range(count)]
    for copy in copies:
        copy.start()
    for copy in copies:
        copy.wait()


def load(*arrays):
    return pl.pallas_call(
        load_kernel,
        out_shape=[kept(v.shape, v.dtype) for v in arrays],
        in_specs=[ANY] * len(arrays),
        out_specs=[VMEM] * len(arrays),
        scratch_shapes=[pltpu.SemaphoreType.DMA((len(arrays),))],
        name="load",
        compiler_params=ROOM,
    )(*arrays)


def select_kernel(sources, experts, cap, code_ref, *refs):
    ring = experts // LINE
    home, inner = position(experts)
    from_x, from_g = refs[:sources], refs[sources : 2 * sources]
    out, (x_held, g_held, sem) = refs[2 * sources : 2 * sources + ring], refs[-3:]

    def fetch(i):
        pltpu.make_async_copy(from_x[i], x_held, sem.at[0]).start()
        pltpu.make_async_copy(from_g[i], g_held, sem.at[1]).start()

    if sources == 1:
        fetch(0)
    else:
        pl.when(inner)(lambda: fetch(0))
        pl.when(jnp.logical_not(inner))(lambda: fetch(1))
    pick, weight = picks(code_ref[...], home, range(ring), cap)
    rows_x = jnp.concatenate([jnp.where(p, 1.0, 0.0) for p in pick], axis=0).astype(HALF)
    rows_g = jnp.concatenate([jnp.where(p, w, 0.0) for p, w in zip(pick, weight)], axis=0)
    pltpu.make_async_copy(from_x[0], x_held, sem.at[0]).wait()
    x = dot(rows_x, x_held[...], 1, 0).astype(HALF)
    for d in range(ring):
        out[d][0] = x[d * cap : (d + 1) * cap]
    pltpu.make_async_copy(from_g[0], g_held, sem.at[1]).wait()
    g = dot(rows_g.astype(HALF), g_held[...], 1, 0).astype(HALF)
    for d in range(ring):
        out[d][1] = g[d * cap : (d + 1) * cap]


def select(code, from_x, from_g, experts, cap):
    rows, width = from_x[0].shape
    ring = experts // LINE
    return pl.pallas_call(
        functools.partial(select_kernel, len(from_x), experts, cap),
        out_shape=[kept((2, cap, width), HALF)] * ring,
        in_specs=[VMEM] + [ANY] * (2 * len(from_x)),
        out_specs=[VMEM] * ring,
        scratch_shapes=[pltpu.VMEM((rows, width), HALF)] * 2 + [pltpu.SemaphoreType.DMA((2,))],
        name="select",
        compiler_params=ROOM,
    )(code, *from_x, *from_g)


def phase_kernel(size, reduced, *refs):
    near, far, (wg, wu, wd) = refs[:size], refs[size : 2 * size], refs[2 * size : 2 * size + 3]
    x_ref, g_ref, da_ref, db_ref, h_ref, rg_ref, *parts, sem = refs[2 * size + 3 :]
    cap = near[0].shape[1]
    for which, held in enumerate((x_ref, g_ref)):
        for i, ref in enumerate(near + far):
            rows = held.at[pl.ds(i * cap, cap)]
            pltpu.make_async_copy(ref.at[which], rows, sem.at[which]).start()
    pltpu.make_async_copy(x_ref, x_ref, sem.at[0]).wait()
    a = dot(x_ref[...], wg[...], 1, 0)
    b = dot(x_ref[...], wu[...], 1, 0)
    pltpu.make_async_copy(g_ref, g_ref, sem.at[1]).wait()
    q = dot(g_ref[...], wd[...], 1, 1)
    sig = jax.nn.sigmoid(a)
    act = a * sig
    h = (act * b).astype(HALF)
    da = (q * b * sig * (1.0 + a * (1.0 - sig))).astype(HALF)
    db = (q * act).astype(HALF)
    h_ref[...], da_ref[...], db_ref[...] = h, da, db
    rg_ref[...] = jnp.sum((q * h.astype(FULL)).reshape(2 * size, cap, -1), axis=2)
    part = dot(da, wg[...], 1, 1) + dot(db, wu[...], 1, 1)
    for i in range(size):
        for side in range(2):
            start = (side * size + i) * cap
            piece = part[start : start + cap]
            if reduced:
                parts[2 * i + side][...] = piece if side == 0 else piece.astype(HALF)
            else:
                parts[i][side] = piece.astype(HALF)


def phase(near, far, wg, wu, wd, reduced):
    size = len(near)
    _, cap, width = near[0].shape
    rows, hidden = 2 * size * cap, wg.shape[1]
    if reduced:
        parts = [kept((cap, width), t) for t in (FULL, HALF)] * size
    else:
        parts = [kept((2, cap, width), HALF)] * size
    out = pl.pallas_call(
        functools.partial(phase_kernel, size, reduced),
        out_shape=[kept((rows, width), HALF)] * 2
        + [kept((rows, hidden), HALF)] * 3
        + [kept((2 * size, cap), FULL)]
        + parts,
        in_specs=[ANY] * (2 * size) + [VMEM] * 3,
        out_specs=[VMEM] * (6 + len(parts)),
        scratch_shapes=[pltpu.SemaphoreType.DMA((2,))],
        name="phase",
        compiler_params=ROOM,
    )(*near, *far, wg, wu, wd)
    return out[:5], out[5], out[6:]


def grads_kernel(count, begun, last, tile, *refs):
    xs, gs, das, dbs, hs = (refs[i * count : (i + 1) * count] for i in range(5))
    olds, outs = refs[5 * count : -3], refs[-3:]
    start = pl.multiple_of(pl.program_id(0) * tile, tile)
    cols = pl.ds(start, tile)
    x = jnp.concatenate([r[:, cols] for r in xs], axis=0)
    g = jnp.concatenate([r[:, cols] for r in gs], axis=0)
    da, db, h = (jnp.concatenate([r[...] for r in v], axis=0) for v in (das, dbs, hs))
    sums = [dot(da, x, 0, 0), dot(db, x, 0, 0), dot(h, g, 0, 0)]
    for i, (out, value) in enumerate(zip(outs, sums)):
        value = value + olds[i][:, cols] if begun else value
        if not last:
            out[:, cols] = value
        else:
            out[...] = value.astype(HALF).T if i < 2 else value.astype(HALF)


def grads(chunks, olds=(), last=True, tile=512):
    width, hidden = chunks[0][0].shape[1], chunks[0][2].shape[1]
    if last:
        shapes = [(width, hidden), (width, hidden), (hidden, width)]
        out_shape = [jax.ShapeDtypeStruct(s, HALF) for s in shapes]
        out_specs = [pl.BlockSpec((tile, hidden), lambda i: (i, 0))] * 2
        out_specs += [pl.BlockSpec((hidden, tile), lambda i: (0, i))]
    else:
        out_shape, out_specs = [kept((hidden, width), FULL)] * 3, [VMEM] * 3
    return pl.pallas_call(
        functools.partial(grads_kernel, len(chunks), bool(olds), last, tile),
        grid=(width // tile,),
        out_shape=out_shape,
        in_specs=[VMEM] * (5 * len(chunks) + len(olds)),
        out_specs=out_specs,
        name="grads",
        compiler_params=ROOM,
    )(*[c[i] for i in range(5) for c in chunks], *olds)


def combine_kernel(experts, count, mine_ref, other_ref, *refs):
    got, outs = refs[:count], refs[count:]
    home, _ = position(experts)
    cap = got[0].shape[1]
    for side, code_ref in enumerate((mine_ref, other_ref)):
        pick, _ = picks(code_ref[...], home, range(count), cap)
        rows = jnp.concatenate([jnp.where(p, 1.0, 0.0).astype(HALF) for p in pick], axis=0)
        back = jnp.concatenate([r[side] for r in got], axis=0)
        outs[side][...] = dot(rows, back, 0, 0).astype(HALF)


def combine(mine, other, got, experts):
    width, rows = got[0].shape[2], mine.shape[1]
    return pl.pallas_call(
        functools.partial(combine_kernel, experts, len(got)),
        out_shape=[kept((rows, width), HALF)] * 2,
        in_specs=[VMEM] * (2 + len(got)),
        out_specs=[VMEM] * 2,
        name="combine",
        compiler_params=ROOM,
    )(mine, other, *got)


def final_kernel(experts, offsets, code_ref, near_ref, far_ref, *refs):
    got, out = refs[:-1], refs[-1]
    home, _ = position(experts)
    pick, _ = picks(code_ref[...], home, offsets, got[0].shape[0])
    rows = jnp.concatenate([jnp.where(p, 1.0, 0.0).astype(HALF) for p in pick], axis=0)
    back = jnp.concatenate([r[...] for r in got], axis=0)
    total = near_ref[...].astype(FULL) + far_ref[...].astype(FULL) + dot(rows, back, 0, 0)
    out[0] = total.astype(HALF)


def final(code, near, far, offsets, got, experts):
    rows, width = near.shape
    return pl.pallas_call(
        functools.partial(final_kernel, experts, offsets),
        out_shape=jax.ShapeDtypeStruct((1, rows, width), HALF),
        in_specs=[VMEM] * (3 + len(got)),
        out_specs=VMEM,
        name="final",
        compiler_params=ROOM,
    )(code, near, far, *got)


def route_kernel(experts, code_ref, slots_ref, *refs):
    ends, out = refs[:-1], refs[-1]
    home, _ = position(experts)
    code = code_ref[...]
    top, cap = code.shape[0] // 2, slots_ref.shape[1]
    pick, _ = picks(code, home, range(experts), cap)
    values = [slots_ref[o : o + 1] for o in range(slots_ref.shape[0])]
    values += [ends[i][...] + ends[i + 1][...] for i in range(0, len(ends), 2)]
    named = [
        lax.dot_general(
            jnp.broadcast_to(v, (8, cap)),
            jnp.where(p, 1.0, 0.0),
            (((1,), (0,)), ((), ())),
            precision=lax.Precision.HIGHEST,
            preferred_element_type=FULL,
        )[:1]
        for p, v in zip(pick, values)
    ]
    for k in range(top):
        near = code[k : k + 1].astype(jnp.int32) ^ home
        chosen = [jnp.where(near == o, named[o], 0.0) for o in range(experts)]
        total = functools.reduce(jnp.add, chosen) / code[top + k : top + k + 1]
        out[k : k + 1] = total.astype(HALF)


def route(code, slots, ends, experts):
    return pl.pallas_call(
        functools.partial(route_kernel, experts),
        out_shape=jax.ShapeDtypeStruct((code.shape[0] // 2, code.shape[1]), HALF),
        in_specs=[VMEM] * (2 + len(ends)),
        out_specs=VMEM,
        name="route",
        compiler_params=ROOM,
    )(code, slots, *ends)


def body(tokens, routes, probs, cotangent, w_gate, w_up, w_down):
    units = lax.axis_size("expert")
    experts = units // 2
    ring = experts // LINE
    rows, top = routes.shape[1:]
    cap = 2 * rows * top // experts
    wg, wu, wd = load(w_gate[0], w_up[0], w_down[0])

    def along(value, hops):
        step = 2 * ring

        def target(i):
            return hops[i // step] * step + i % step if i // step in hops else None

        return moved(value, target)

    code = jnp.concatenate([routes[0].astype(FULL).T, probs[0].astype(FULL).T], axis=0)
    sides = []
    for own in (tokens[0], cotangent[0]):
        side1 = along(own, {0: 1, 1: 0, 2: 3, 3: 2})
        side2 = along(own, {1: 2, 2: 1})
        side3 = along(side1, {1: 2, 2: 1})
        side4 = along(side2, {1: 0, 2: 3})
        side5 = along(side3, {1: 0, 2: 3})
        sides.append([[own], [side1], [side3, side4], [side2, side5]])
    codes = [code] + [shifted(code, 2 * ring * j) for j in range(1, LINE)]
    mirror = shifted(code, 1, 1)
    lower = shifted(code, 0, 1, 1)

    near, far = {}, {}
    for j in range(LINE):
        picked = select(codes[j], sides[0][j], sides[1][j], experts, cap)
        for d, block in enumerate(picked):
            o = j * ring + d
            near[o] = block if d == 0 else shifted(block, 2 * d)
            far[o] = shifted(near[o], 1)

    groups = groups_of(experts)
    last = list(range(experts - 2, experts))
    chunks, near_rg, far_rg, got = [], {}, {}, {}
    for group in groups:
        near_group, far_group = [near[o] for o in group], [far[o] for o in group]
        reduced = group[0] in last
        chunk, rg, parts = phase(near_group, far_group, wg, wu, wd, reduced)
        chunks.append(chunk)
        for i, o in enumerate(group):
            near_rg[o], far_rg[o] = rg[i], rg[len(group) + i]
            if reduced:
                partner = shifted(parts[1], 1, 1)
                total = (parts[0] + partner.astype(FULL)).astype(HALF)
                got[o] = shifted(total, 2 * o, 1, 1)
            else:
                got[o] = parts[i] if o == 0 else shifted(parts[i], 2 * o, 1)

    begun = grads(chunks[:1], last=False)
    g_gate, g_up, g_down = grads(chunks[1:], begun)

    early = [o for o in range(experts) if o not in last]
    slots = jnp.stack([near_rg[o] for o in early])
    slots += shifted(jnp.stack([far_rg[o] for o in early]), 1)
    for bit in range(experts.bit_length() - 1):
        high = [o for o in early if o >> bit & 1]
        taken = shifted(jnp.stack([slots[o] for o in high]), 2 << bit)
        slots = jnp.stack([taken[high.index(o)] if o in high else slots[o] for o in early])
    ends = [
        shifted(rg[None], 2 * o + side)
        for o in last
        for side, rg in enumerate((near_rg[o], far_rg[o]))
    ]
    route_grad = route(code, slots, ends, experts).T

    dx_near, dx_far = combine(code, mirror, [got[o] for o in early], experts)
    below = shifted(dx_near, 0, 1, 1)
    across = shifted(dx_far, 1, 1, 1)
    upstream = final(lower, below, across, last, [got[o] for o in last], experts)
    return (upstream, route_grad[None], g_gate[None], g_up[None], g_down[None])


def solution(mesh):
    rows, columns = P("section", "expert", None), P("section", None, "expert")
    in_specs = (rows, rows, rows, rows, columns, columns, rows)
    out_specs = (rows, rows, columns, columns, rows)

    return jax.shard_map(body, mesh=mesh, in_specs=in_specs, out_specs=out_specs, check_vma=False)
```

time: 254 us -> 210 us (0.83)
  the two profiles are of different devices: /device:TPU:10 before, /device:TPU:9 now
where the time goes in v1:
time: 210 us; the launch traced here: 209 us
  waiting for transfers between devices  95.3 us (45%)
  starting transfers between devices  78.3 us (37%)
  Pallas kernels  29.5 us (14%)
  local copies, waits for them, and re-layouts  3.53 us (2%)
    ppermute x46, waiting for transfers between devices, moved(): return lax.ppermute(value, AXES, pairs)  95.3 us
    ppermute x46, starting transfers between devices, moved(): return lax.ppermute(value, AXES, pairs)  78.3 us
    pallas_call x4, Pallas kernels, phase(): pl.pallas_call(functools.partial(phase_kernel, size, reduced), out_shape=...  15 us
    pallas_call x2, Pallas kernels, grads(): pl.pallas_call(functools.partial(grads_kernel, len(chunks), bool(olds), l...  7.6 us
  transfers between devices with their start and end apart: 46, of which 17 were waited for; matrix products, arithmetic and copies ran while one was open for 1% of the time, Pallas kernels for 14%

profile of v1, /device:TPU:9, one launch (start us, length us, event | category | flops | bytes accessed | tf_op | source)
XLA Modules:
  0.0 209.4 jit_solution(17674256616799122237)
XLA Ops:
  0.7 4.5 %collective-permute-start.16 = (bf16[128,2048]{1,0:T(8,128)(2,1)}, bf16[128,2048]{1,0:T(8,128)(2,1)S(1)}, u32[]{:S(2)}, u32[]{:S(2)}) collective-permute-start(bf16[128,2048]{1,0:T(8,128)(2,1)} %bitcast.24), channel_id=1, source_target_pairs={{4,8},{5,9},{6,10},{7,11},{8,4},{9,5},{10,6},{11,7},{20,24},{21,25... | collective-permute-start | bytes 1572872 | tf_op jit(solution)/shard_map/ppermute | solution.py:27
  5.3 1.9 collective-permute-start.19
  7.9 5.8 %collective-permute-done.4.refs_0_ = bf16[128,2048]{1,0:T(8,128)(2,1)S(1)} collective-permute-done((bf16[128,2048]{1,0:T(8,128)(2,1)}, bf16[128,2048]{1,0:T(8,128)(2,1)S(1)}, u32[]{:S(2)}, u32[]{:S(2)}) %collective-permute-start.4) | collective-permute-done | bytes 524320 | tf_op jit(solution)/shard_map/ppermute | solution.py:27
  13.7 3.2 %collective-permute-start.15 = (bf16[128,2048]{1,0:T(8,128)(2,1)S(1)}, bf16[128,2048]{1,0:T(8,128)(2,1)S(1)}, u32[]{:S(2)}, u32[]{:S(2)}) collective-permute-start(bf16[128,2048]{1,0:T(8,128)(2,1)S(1)} %collective-permute-done.4.refs_0_), channel_id=1, source_target_pairs={{4,8},{5,9},{6,10},{7,11},{8,4},{9,5},{10,6},{11,7},{20,24},{21,25... | collective-permute-start | bytes 1572872 | tf_op jit(solution)/shard_map/ppermute | solution.py:27
  16.9 1.3 collective-permute-start.17
  18.3 6.7 %collective-permute-done.5.refs_1_ = bf16[128,2048]{1,0:T(8,128)(2,1)S(1)} collective-permute-done((bf16[128,2048]{1,0:T(8,128)(2,1)}, bf16[128,2048]{1,0:T(8,128)(2,1)S(1)}, u32[]{:S(2)}, u32[]{:S(2)}) %collective-permute-start.5) | collective-permute-done | bytes 524320 | tf_op jit(solution)/shard_map/ppermute | solution.py:27
  25.0 3.2 %collective-permute-start.18 = (bf16[128,2048]{1,0:T(8,128)(2,1)S(1)}, bf16[128,2048]{1,0:T(8,128)(2,1)S(1)}, u32[]{:S(2)}, u32[]{:S(2)}) collective-permute-start(bf16[128,2048]{1,0:T(8,128)(2,1)S(1)} %collective-permute-done.5.refs_1_), channel_id=1, source_target_pairs={{4,8},{5,9},{6,10},{7,11},{8,4},{9,5},{10,6},{11,7},{20,24},{21,25... | collective-permute-start | bytes 1572872 | tf_op jit(solution)/shard_map/ppermute | solution.py:27
  28.2 1.3 collective-permute-start.20
  30.2 15.3 %collective-permute-done.3.code_ref = f32[4,128]{1,0:T(4,128)S(1)} collective-permute-done((f32[4,128]{1,0:T(4,128)S(1)}, f32[4,128]{1,0:T(4,128)S(1)}, u32[]{:S(2)}, u32[]{:S(2)}) %collective-permute-start.3) | collective-permute-done | bytes 2080 | tf_op jit(solution)/shard_map/ppermute | solution.py:27
  45.6 4.2 %collective-permute-start.14 = (f32[4,128]{1,0:T(4,128)S(1)}, f32[4,128]{1,0:T(4,128)S(1)}, u32[]{:S(2)}, u32[]{:S(2)}) collective-permute-start(f32[4,128]{1,0:T(4,128)S(1)} %pad_maximum_fusion.2.code_ref.mine_ref), channel_id=1, source_target_pairs={{0,8},{1,9},{2,10},{3,11},{4,12},{5,13},{6,14},{7,15},{8,0},{9,1},... | collective-permute-start | bytes 6152 | tf_op jit(solution)/shard_map/ppermute | solution.py:27
  52.7 1.3 collective-permute-start.2
  57.2 1.3 collective-permute-start.21
  58.5 2.7 %collective-permute-done.28.code_ref = f32[4,128]{1,0:T(4,128)S(1)} collective-permute-done((f32[4,128]{1,0:T(4,128)S(1)}, f32[4,128]{1,0:T(4,128)S(1)}, u32[]{:S(2)}, u32[]{:S(2)}) %collective-permute-start.28) | collective-permute-done | bytes 2080 | tf_op jit(solution)/shard_map/ppermute | solution.py:27
  61.2 2.7 %collective-permute-start.29 = (bf16[128,2048]{1,0:T(8,128)(2,1)S(1)}, bf16[128,2048]{1,0:T(8,128)(2,1)S(1)}, u32[]{:S(2)}, u32[]{:S(2)}) collective-permute-start(bf16[128,2048]{1,0:T(8,128)(2,1)S(1)} %collective-permute-done.15.refs_0_), channel_id=1, source_target_pairs={{4,0},{5,1},{6,2},{7,3},{8,12},{9,13},{10,14},{11,15},{20,16},{21,... | collective-permute-start | bytes 1572872 | tf_op jit(solution)/shard_map/ppermute | solution.py:27
  64.5 1.3 collective-permute-start.30
  67.5 8.2 %collective-permute-done.6.refs_3_ = bf16[2,64,2048]{2,1,0:T(8,128)(2,1)S(1)} collective-permute-done((bf16[2,64,2048]{2,1,0:T(8,128)(2,1)S(1)}, bf16[2,64,2048]{2,1,0:T(8,128)(2,1)S(1)}, u32[]{:S(2)}, u32[]{:S(2)}) %collective-permute-start.6) | collective-permute-done | bytes 524320 | tf_op jit(solution)/shard_map/ppermute | solution.py:27
  76.9 10.0 %collective-permute-done.21.refs_1_ = bf16[2,64,2048]{2,1,0:T(8,128)(2,1)S(1)} collective-permute-done((bf16[2,64,2048]{2,1,0:T(8,128)(2,1)S(1)}, bf16[2,64,2048]{2,1,0:T(8,128)(2,1)S(1)}, u32[]{:S(2)}, u32[]{:S(2)}) %collective-permute-start.21) | collective-permute-done | bytes 524320 | tf_op jit(solution)/shard_map/ppermute | solution.py:27
  89.6 1.4 copy-done.2
  93.8 7.1 %collective-permute-done.10.refs_7_ = bf16[2,64,2048]{2,1,0:T(8,128)(2,1)S(1)} collective-permute-done((bf16[2,64,2048]{2,1,0:T(8,128)(2,1)S(1)}, bf16[2,64,2048]{2,1,0:T(8,128)(2,1)S(1)}, u32[]{:S(2)}, u32[]{:S(2)}) %collective-permute-start.10) | collective-permute-done | bytes 524320 | tf_op jit(solution)/shard_map/ppermute | solution.py:27
  100.9 6.4 %phase.4 = (bf16[512,2048]{1,0:T(8,128)(2,1)S(1)}, bf16[512,2048]{1,0:T(8,128)(2,1)S(1)}, bf16[512,384]{1,0:T(8,128)(2,1)S(1)}, bf16[512,384]{1,0:T(8,128)(2,1)S...) custom-call(bf16[2,64,2048]{2,1,0:T(8,128)(2,1)S(1)} %get-tuple-elem, ...), custom_call_target="tpu_custom_call" | custom-call | tf_op jit(solution)/shard_map/phase/pallas_call | solution.py:179
  107.3 4.8 %collective-permute-done.22.refs_2_ = bf16[2,64,2048]{2,1,0:T(8,128)(2,1)S(1)} collective-permute-done((bf16[2,64,2048]{2,1,0:T(8,128)(2,1)S(1)}, bf16[2,64,2048]{2,1,0:T(8,128)(2,1)S(1)}, u32[]{:S(2)}, u32[]{:S(2)}) %collective-permute-start.22) | collective-permute-done | bytes 524320 | tf_op jit(solution)/shard_map/ppermute | solution.py:27
  112.1 11.2 %collective-permute-done.23.refs_3_ = bf16[2,64,2048]{2,1,0:T(8,128)(2,1)S(1)} collective-permute-done((bf16[2,64,2048]{2,1,0:T(8,128)(2,1)S(1)}, bf16[2,64,2048]{2,1,0:T(8,128)(2,1)S(1)}, u32[]{:S(2)}, u32[]{:S(2)}) %collective-permute-start.23) | collective-permute-done | bytes 524320 | tf_op jit(solution)/shard_map/ppermute | solution.py:27
  123.3 3.5 %phase.5 = (bf16[256,2048]{1,0:T(8,128)(2,1)S(1)}, bf16[256,2048]{1,0:T(8,128)(2,1)S(1)}, bf16[256,384]{1,0:T(8,128)(2,1)S(1)}, bf16[256,384]{1,0:T(8,128)(2,1)S...) custom-call(bf16[2,64,2048]{2,1,0:T(8,128)(2,1)S(1)} %get-tuple-elem, ...), custom_call_target="tpu_custom_call" | custom-call | tf_op jit(solution)/shard_map/phase/pallas_call | solution.py:179
  128.1 2.4 %collective-permute-start.1 = (f32[4,128]{1,0:T(4,128)S(1)}, f32[4,128]{1,0:T(4,128)S(1)}, u32[]{:S(2)}, u32[]{:S(2)}) collective-permute-start(f32[4,128]{1,0:T(4,128)S(1)} %pad_maximum_fusion.2.code_ref.mine_ref), channel_id=1, source_target_pairs={{16,17},{17,16},{18,19},{19,18},{20,21},{21,20},{22,23},{23,22},{2... | collective-permute-start | bytes 6152 | tf_op jit(solution)/shard_map/ppermute | solution.py:27
  130.5 2.8 %collective-permute-start.11 = (bf16[2,64,2048]{2,1,0:T(8,128)(2,1)S(1)}, bf16[2,64,2048]{2,1,0:T(8,128)(2,1)S(1)}, u32[]{:S(2)}, u32[]{:S(2)}) collective-permute-start(bf16[2,64,2048]{2,1,0:T(8,128)(2,1)S(1)} %get-tuple-element.66), channel_id=1, source_target_pairs={{16,18},{17,19},{18,16},{19,17},{20,22},{21,23},{22,20},{23,21},{2... | collective-permute-start | bytes 1572872 | tf_op jit(solution)/shard_map/ppermute | solution.py:27
  133.3 1.3 collective-permute-done.31.refs_1_
  134.6 1.9 collective-permute-start.12
  136.5 2.6 %phase.6 = (bf16[128,2048]{1,0:T(8,128)(2,1)S(1)}, bf16[128,2048]{1,0:T(8,128)(2,1)S(1)}, bf16[128,384]{1,0:T(8,128)(2,1)S(1)}, bf16[128,384]{1,0:T(8,128)(2,1)S...) custom-call(bf16[2,64,2048]{2,1,0:T(8,128)(2,1)S(1)} %get-tuple-elem, ...), custom_call_target="tpu_custom_call" | custom-call | tf_op jit(solution)/shard_map/phase/pallas_call | solution.py:179
  141.4 1.5 collective-permute-done.39
  142.9 2.2 %collective-permute-start.32 = (bf16[64,2048]{1,0:T(8,128)(2,1)S(1)}, bf16[64,2048]{1,0:T(8,128)(2,1)S(1)}, u32[]{:S(2)}, u32[]{:S(2)}) collective-permute-start(bf16[64,2048]{1,0:T(8,128)(2,1)S(1)} %get-tuple-element.77), channel_id=1, source_target_pairs={{16,17},{17,16},{18,19},{19,18},{20,21},{21,20},{22,23},{23,22},{2... | collective-permute-start | bytes 786440 | tf_op jit(solution)/shard_map/ppermute | solution.py:27
  145.1 4.3 %collective-permute-start.13 = (bf16[2,64,2048]{2,1,0:T(8,128)(2,1)S(1)}, bf16[2,64,2048]{2,1,0:T(8,128)(2,1)S(1)}, u32[]{:S(2)}, u32[]{:S(2)}) collective-permute-start(bf16[2,64,2048]{2,1,0:T(8,128)(2,1)S(1)} %get-tuple-element.68), channel_id=1, source_target_pairs={{16,22},{17,23},{18,20},{19,21},{20,18},{21,19},{22,16},{23,17},{2... | collective-permute-start | bytes 1572872 | tf_op jit(solution)/shard_map/ppermute | solution.py:27
  149.4 1.9 collective-permute-start.24
  151.6 4.3 %collective-permute-start.25 = (bf16[2,64,2048]{2,1,0:T(8,128)(2,1)S(1)}, bf16[2,64,2048]{2,1,0:T(8,128)(2,1)S(1)}, u32[]{:S(2)}, u32[]{:S(2)}) collective-permute-start(bf16[2,64,2048]{2,1,0:T(8,128)(2,1)S(1)} %get-tuple-element.72), channel_id=1, source_target_pairs={{16,26},{17,27},{18,24},{19,25},{20,30},{21,31},{22,28},{23,29},{2... | collective-permute-start | bytes 1572872 | tf_op jit(solution)/shard_map/ppermute | solution.py:27
  155.9 2.6 %phase.7 = (bf16[128,2048]{1,0:T(8,128)(2,1)S(1)}, bf16[128,2048]{1,0:T(8,128)(2,1)S(1)}, bf16[128,384]{1,0:T(8,128)(2,1)S(1)}, bf16[128,384]{1,0:T(8,128)(2,1)S...) custom-call(bf16[2,64,2048]{2,1,0:T(8,128)(2,1)S(1)} %collective-per, ...), custom_call_target="tpu_custom_call" | custom-call | tf_op jit(solution)/shard_map/phase/pallas_call | solution.py:179
  158.5 3.1 %collective-permute-start.36 = (bf16[64,2048]{1,0:T(8,128)(2,1)S(1)}, bf16[64,2048]{1,0:T(8,128)(2,1)S(1)}, u32[]{:S(2)}, u32[]{:S(2)}) collective-permute-start(bf16[64,2048]{1,0:T(8,128)(2,1)S(1)} %get-tuple-element.80), channel_id=1, source_target_pairs={{16,17},{17,16},{18,19},{19,18},{20,21},{21,20},{22,23},{23,22},{2... | collective-permute-start | bytes 786440 | tf_op jit(solution)/shard_map/ppermute | solution.py:27
  161.7 1.3 collective-permute-start.42
  163.2 5.6 %collective-permute-done.24.refs_4_ = bf16[2,64,2048]{2,1,0:T(8,128)(2,1)S(1)} collective-permute-done((bf16[2,64,2048]{2,1,0:T(8,128)(2,1)S(1)}, bf16[2,64,2048]{2,1,0:T(8,128)(2,1)S(1)}, u32[]{:S(2)}, u32[]{:S(2)}) %collective-permute-start.24) | collective-permute-done | bytes 524320 | tf_op jit(solution)/shard_map/ppermute | solution.py:27
  168.8 2.8 %collective-permute-start.41 = (f32[2,64]{1,0:T(2,128)S(1)}, f32[2,64]{1,0:T(2,128)S(1)}, u32[]{:S(2)}, u32[]{:S(2)}) collective-permute-start(f32[2,64]{1,0:T(2,128)S(1)} %pad_maximum_fusion.5), channel_id=1, source_target_pairs={{0,8},{1,9},{2,10},{3,11},{4,12},{5,13},{6,14},{7,15},{8,0},{9,1},... | collective-permute-start | bytes 1544 | tf_op jit(solution)/shard_map/ppermute | solution.py:27
  171.6 2.8 %collective-permute-done.25.refs_5_ = bf16[2,64,2048]{2,1,0:T(8,128)(2,1)S(1)} collective-permute-done((bf16[2,64,2048]{2,1,0:T(8,128)(2,1)S(1)}, bf16[2,64,2048]{2,1,0:T(8,128)(2,1)S(1)}, u32[]{:S(2)}, u32[]{:S(2)}) %collective-permute-start.25) | collective-permute-done | bytes 524320 | tf_op jit(solution)/shard_map/ppermute | solution.py:27
  175.5 1.3 collective-permute-start.26
  176.8 1.3 collective-permute-start.27
  178.2 2.9 %collective-permute-start.40 = (f32[2,64]{1,0:T(2,128)S(1)}, f32[2,64]{1,0:T(2,128)S(1)}, u32[]{:S(2)}, u32[]{:S(2)}) collective-permute-start(f32[2,64]{1,0:T(2,128)S(1)} %pad_maximum_fusion.4), channel_id=1, source_target_pairs={{0,4},{1,5},{2,6},{3,7},{4,0},{5,1},{6,2},{7,3},{8,12},{9,13},{10,... | collective-permute-start | bytes 1544 | tf_op jit(solution)/shard_map/ppermute | solution.py:27
  181.1 1.3 collective-permute-start.33
  182.4 1.3 collective-permute-start.37
  185.0 10.8 %collective-permute-done.44.refs_2_ = f32[1,64]{1,0:T(1,128)S(1)} collective-permute-done((f32[1,64]{1,0:T(1,128)S(1)}, f32[1,64]{1,0:T(1,128)S(1)}, u32[]{:S(2)}, u32[]{:S(2)}) %collective-permute-start.44) | collective-permute-done | bytes 288 | tf_op jit(solution)/shard_map/ppermute | solution.py:27
  195.8 2.4 %collective-permute-start.45 = (f32[1,64]{1,0:T(1,128)S(1)}, f32[1,64]{1,0:T(1,128)S(1)}, u32[]{:S(2)}, u32[]{:S(2)}) collective-permute-start(f32[1,64]{1,0:T(1,128)S(1)} %get-tuple-element.124), channel_id=1, source_target_pairs={{0,15},{1,14},{2,13},{3,12},{4,11},{5,10},{6,9},{7,8},{8,7},{9,6},... | collective-permute-start | bytes 776 | tf_op jit(solution)/shard_map/ppermute | solution.py:27
  198.2 3.3 %grads.2 = (f32[384,2048]{1,0:T(8,128)S(1)}, f32[384,2048]{1,0:T(8,128)S(1)}, f32[384,2048]{1,0:T(8,128)S(1)}) custom-call(bf16[512,2048]{1,0:T(8,128)(2,1)S(1)} %get-tuple-element.100.refs_0_, bf16[512,2048]{1,0:T(8,128)(2,1)S(1)} %get-tuple-element.101.refs_1_, bf16[512,384]{1,0:T(8,128)(2,1)S(1)} %get-tuple-element.102.refs_2_, ...), custom_call_target="tpu_custom_call" | custom-call | tf_op jit(solution)/shard_map/grads/pallas_call | solution.py:220
  202.8 4.3 %grads.3 = (bf16[2048,384]{1,0:T(8,128)(2,1)}, bf16[2048,384]{1,0:T(8,128)(2,1)}, bf16[384,2048]{1,0:T(8,128)(2,1)}) custom-call(bf16[256,2048]{1,0:T(8,128)(2,1)S(1)} %get-tuple-element.85.refs_0_, bf16[128,2048]{1,0:T(8,128)(2,1)S(1)} %get-tuple-element.86.refs_1_, bf16[128,2048]{1,0:T(8,128)(2,1)S(1)} %get-tuple-element.87.refs_2_, ...), custom_call_target="tpu_custom_call" | custom-call | tf_op jit(solution)/shard_map/grads/pallas_call | solution.py:220
  (85 shorter events, 26.5 us)
Async XLA Ops:
  0.6 13.1 %collective-permute-start.4 = (bf16[128,2048]{1,0:T(8,128)(2,1)}, bf16[128,2048]{1,0:T(8,128)(2,1)S(1)}, u32[]{:S(2)}, u32[]{:S(2)}) collective-permute-start(bf16[128,2048]{1,0:T(8,128)(2,1)} %bitcast.23), channel_id=1, source_target_pairs={{0,4},{1,5},{2,6},{3,7},{4,0},{5,1},{6,2},{7,3},{8,12},{9,13},{10,... | collective-permute-start | bytes 1572872 | tf_op jit(solution)/shard_map/ppermute | solution.py:27
  0.7 16.2 %collective-permute-start.16 = (bf16[128,2048]{1,0:T(8,128)(2,1)}, bf16[128,2048]{1,0:T(8,128)(2,1)S(1)}, u32[]{:S(2)}, u32[]{:S(2)}) collective-permute-start(bf16[128,2048]{1,0:T(8,128)(2,1)} %bitcast.24), channel_id=1, source_target_pairs={{4,8},{5,9},{6,10},{7,11},{8,4},{9,5},{10,6},{11,7},{20,24},{21,25... | collective-permute-start | bytes 1572872 | tf_op jit(solution)/shard_map/ppermute | solution.py:27
  5.2 19.8 %collective-permute-start.5 = (bf16[128,2048]{1,0:T(8,128)(2,1)}, bf16[128,2048]{1,0:T(8,128)(2,1)S(1)}, u32[]{:S(2)}, u32[]{:S(2)}) collective-permute-start(bf16[128,2048]{1,0:T(8,128)(2,1)} %bitcast.26), channel_id=1, source_target_pairs={{0,4},{1,5},{2,6},{3,7},{4,0},{5,1},{6,2},{7,3},{8,12},{9,13},{10,... | collective-permute-start | bytes 1572872 | tf_op jit(solution)/shard_map/ppermute | solution.py:27
  5.3 22.9 %collective-permute-start.19 = (bf16[128,2048]{1,0:T(8,128)(2,1)}, bf16[128,2048]{1,0:T(8,128)(2,1)S(1)}, u32[]{:S(2)}, u32[]{:S(2)}) collective-permute-start(bf16[128,2048]{1,0:T(8,128)(2,1)} %bitcast.27), channel_id=1, source_target_pairs={{4,8},{5,9},{6,10},{7,11},{8,4},{9,5},{10,6},{11,7},{20,24},{21,25... | collective-permute-start | bytes 1572872 | tf_op jit(solution)/shard_map/ppermute | solution.py:27
  13.7 41.1 %collective-permute-start.15 = (bf16[128,2048]{1,0:T(8,128)(2,1)S(1)}, bf16[128,2048]{1,0:T(8,128)(2,1)S(1)}, u32[]{:S(2)}, u32[]{:S(2)}) collective-permute-start(bf16[128,2048]{1,0:T(8,128)(2,1)S(1)} %collective-permute-done.4.refs_0_), channel_id=1, source_target_pairs={{4,8},{5,9},{6,10},{7,11},{8,4},{9,5},{10,6},{11,7},{20,24},{21,25... | collective-permute-start | bytes 1572872 | tf_op jit(solution)/shard_map/ppermute | solution.py:27
  16.9 39.2 %collective-permute-start.17 = (bf16[128,2048]{1,0:T(8,128)(2,1)S(1)}, bf16[128,2048]{1,0:T(8,128)(2,1)S(1)}, u32[]{:S(2)}, u32[]{:S(2)}) collective-permute-start(bf16[128,2048]{1,0:T(8,128)(2,1)S(1)} %collective-permute-done.16.refs_0_), channel_id=1, source_target_pairs={{4,0},{5,1},{6,2},{7,3},{8,12},{9,13},{10,14},{11,15},{20,16},{21,... | collective-permute-start | bytes 1572872 | tf_op jit(solution)/shard_map/ppermute | solution.py:27
  25.0 31.4 %collective-permute-start.18 = (bf16[128,2048]{1,0:T(8,128)(2,1)S(1)}, bf16[128,2048]{1,0:T(8,128)(2,1)S(1)}, u32[]{:S(2)}, u32[]{:S(2)}) collective-permute-start(bf16[128,2048]{1,0:T(8,128)(2,1)S(1)} %collective-permute-done.5.refs_1_), channel_id=1, source_target_pairs={{4,8},{5,9},{6,10},{7,11},{8,4},{9,5},{10,6},{11,7},{20,24},{21,25... | collective-permute-start | bytes 1572872 | tf_op jit(solution)/shard_map/ppermute | solution.py:27
  28.2 28.2 %collective-permute-start.20 = (bf16[128,2048]{1,0:T(8,128)(2,1)S(1)}, bf16[128,2048]{1,0:T(8,128)(2,1)S(1)}, u32[]{:S(2)}, u32[]{:S(2)}) collective-permute-start(bf16[128,2048]{1,0:T(8,128)(2,1)S(1)} %collective-permute-done.19.refs_2_), channel_id=1, source_target_pairs={{4,0},{5,1},{6,2},{7,3},{8,12},{9,13},{10,14},{11,15},{20,16},{21,... | collective-permute-start | bytes 1572872 | tf_op jit(solution)/shard_map/ppermute | solution.py:27
  30.2 15.4 %collective-permute-start.3 = (f32[4,128]{1,0:T(4,128)S(1)}, f32[4,128]{1,0:T(4,128)S(1)}, u32[]{:S(2)}, u32[]{:S(2)}) collective-permute-start(f32[4,128]{1,0:T(4,128)S(1)} %pad_maximum_fusion.2.code_ref.mine_ref), channel_id=1, source_target_pairs={{0,4},{1,5},{2,6},{3,7},{4,0},{5,1},{6,2},{7,3},{8,12},{9,13},{10,... | collective-permute-start | bytes 6152 | tf_op jit(solution)/shard_map/ppermute | solution.py:27
  45.6 7.1 %collective-permute-start.14 = (f32[4,128]{1,0:T(4,128)S(1)}, f32[4,128]{1,0:T(4,128)S(1)}, u32[]{:S(2)}, u32[]{:S(2)}) collective-permute-start(f32[4,128]{1,0:T(4,128)S(1)} %pad_maximum_fusion.2.code_ref.mine_ref), channel_id=1, source_target_pairs={{0,8},{1,9},{2,10},{3,11},{4,12},{5,13},{6,14},{7,15},{8,0},{9,1},... | collective-permute-start | bytes 6152 | tf_op jit(solution)/shard_map/ppermute | solution.py:27
  52.7 36.9 %copy-start = (bf16[1,2048,384]{2,1,0:T(8,128)(2,1)S(1)}, bf16[1,2048,384]{2,1,0:T(8,128)(2,1)}, u32[]{:S(2)}) copy-start(bf16[1,2048,384]{2,1,0:T(8,128)(2,1)} %param.11) | copy-start | bytes 4718596
  52.7 36.9 %copy-start.1 = (bf16[1,2048,384]{2,1,0:T(8,128)(2,1)S(1)}, bf16[1,2048,384]{2,1,0:T(8,128)(2,1)}, u32[]{:S(2)}) copy-start(bf16[1,2048,384]{2,1,0:T(8,128)(2,1)} %param.12) | copy-start | bytes 4718596
  52.7 11.7 %collective-permute-start.2 = (bf16[2,64,2048]{2,1,0:T(8,128)(2,1)S(1)}, bf16[2,64,2048]{2,1,0:T(8,128)(2,1)S(1)}, u32[]{:S(2)}, u32[]{:S(2)}) collective-permute-start(bf16[2,64,2048]{2,1,0:T(8,128)(2,1)S(1)} %get-tuple-element.59), channel_id=1, source_target_pairs={{0,2},{1,3},{2,0},{3,1},{4,6},{5,7},{6,4},{7,5},{8,10},{9,11},{10,... | collective-permute-start | bytes 1572872 | tf_op jit(solution)/shard_map/ppermute | solution.py:27
  54.8 11.5 %collective-permute-start.7 = (bf16[2,64,2048]{2,1,0:T(8,128)(2,1)S(1)}, bf16[2,64,2048]{2,1,0:T(8,128)(2,1)S(1)}, u32[]{:S(2)}, u32[]{:S(2)}) collective-permute-start(bf16[2,64,2048]{2,1,0:T(8,128)(2,1)S(1)} %get-tuple-element.58.refs_0_), channel_id=1, source_target_pairs={{0,1},{1,0},{2,3},{3,2},{4,5},{5,4},{6,7},{7,6},{8,9},{9,8},{10,11... | collective-permute-start | bytes 1572872 | tf_op jit(solution)/shard_map/ppermute | solution.py:27
  56.1 19.6 %collective-permute-start.6 = (bf16[2,64,2048]{2,1,0:T(8,128)(2,1)S(1)}, bf16[2,64,2048]{2,1,0:T(8,128)(2,1)S(1)}, u32[]{:S(2)}, u32[]{:S(2)}) collective-permute-start(bf16[2,64,2048]{2,1,0:T(8,128)(2,1)S(1)} %get-tuple-element.61), channel_id=1, source_target_pairs={{0,2},{1,3},{2,0},{3,1},{4,6},{5,7},{6,4},{7,5},{8,10},{9,11},{10,... | collective-permute-start | bytes 1572872 | tf_op jit(solution)/shard_map/ppermute | solution.py:27
  57.2 29.7 %collective-permute-start.21 = (bf16[2,64,2048]{2,1,0:T(8,128)(2,1)S(1)}, bf16[2,64,2048]{2,1,0:T(8,128)(2,1)S(1)}, u32[]{:S(2)}, u32[]{:S(2)}) collective-permute-start(bf16[2,64,2048]{2,1,0:T(8,128)(2,1)S(1)} %get-tuple-element.70), channel_id=1, source_target_pairs={{0,2},{1,3},{2,0},{3,1},{4,6},{5,7},{6,4},{7,5},{8,10},{9,11},{10,... | collective-permute-start | bytes 1572872 | tf_op jit(solution)/shard_map/ppermute | solution.py:27
  58.5 2.7 %collective-permute-start.28 = (f32[4,128]{1,0:T(4,128)S(1)}, f32[4,128]{1,0:T(4,128)S(1)}, u32[]{:S(2)}, u32[]{:S(2)}) collective-permute-start(f32[4,128]{1,0:T(4,128)S(1)} %pad_maximum_fusion.2.code_ref.mine_ref), channel_id=1, source_target_pairs={{0,12},{1,13},{2,14},{3,15},{4,8},{5,9},{6,10},{7,11},{8,4},{9,5},... | collective-permute-start | bytes 6152 | tf_op jit(solution)/shard_map/ppermute | solution.py:27
  61.2 26.9 %collective-permute-start.29 = (bf16[128,2048]{1,0:T(8,128)(2,1)S(1)}, bf16[128,2048]{1,0:T(8,128)(2,1)S(1)}, u32[]{:S(2)}, u32[]{:S(2)}) collective-permute-start(bf16[128,2048]{1,0:T(8,128)(2,1)S(1)} %collective-permute-done.15.refs_0_), channel_id=1, source_target_pairs={{4,0},{5,1},{6,2},{7,3},{8,12},{9,13},{10,14},{11,15},{20,16},{21,... | collective-permute-start | bytes 1572872 | tf_op jit(solution)/shard_map/ppermute | solution.py:27
  64.5 23.9 %collective-permute-start.30 = (bf16[128,2048]{1,0:T(8,128)(2,1)S(1)}, bf16[128,2048]{1,0:T(8,128)(2,1)S(1)}, u32[]{:S(2)}, u32[]{:S(2)}) collective-permute-start(bf16[128,2048]{1,0:T(8,128)(2,1)S(1)} %collective-permute-done.18.refs_2_), channel_id=1, source_target_pairs={{4,0},{5,1},{6,2},{7,3},{8,12},{9,13},{10,14},{11,15},{20,16},{21,... | collective-permute-start | bytes 1572872 | tf_op jit(solution)/shard_map/ppermute | solution.py:27
  66.3 25.9 %collective-permute-start.8 = (bf16[2,64,2048]{2,1,0:T(8,128)(2,1)S(1)}, bf16[2,64,2048]{2,1,0:T(8,128)(2,1)S(1)}, u32[]{:S(2)}, u32[]{:S(2)}) collective-permute-start(bf16[2,64,2048]{2,1,0:T(8,128)(2,1)S(1)} %collective-permute-done.2.refs_1_), channel_id=1, source_target_pairs={{0,1},{1,0},{2,3},{3,2},{4,5},{5,4},{6,7},{7,6},{8,9},{9,8},{10,11... | collective-permute-start | bytes 1572872 | tf_op jit(solution)/shard_map/ppermute | solution.py:27
  75.7 16.9 %collective-permute-start.9 = (bf16[2,64,2048]{2,1,0:T(8,128)(2,1)S(1)}, bf16[2,64,2048]{2,1,0:T(8,128)(2,1)S(1)}, u32[]{:S(2)}, u32[]{:S(2)}) collective-permute-start(bf16[2,64,2048]{2,1,0:T(8,128)(2,1)S(1)} %get-tuple-element.60.refs_2_), channel_id=1, source_target_pairs={{0,1},{1,0},{2,3},{3,2},{4,5},{5,4},{6,7},{7,6},{8,9},{9,8},{10,11... | collective-permute-start | bytes 1572872 | tf_op jit(solution)/shard_map/ppermute | solution.py:27
  86.9 13.9 %collective-permute-start.10 = (bf16[2,64,2048]{2,1,0:T(8,128)(2,1)S(1)}, bf16[2,64,2048]{2,1,0:T(8,128)(2,1)S(1)}, u32[]{:S(2)}, u32[]{:S(2)}) collective-permute-start(bf16[2,64,2048]{2,1,0:T(8,128)(2,1)S(1)} %collective-permute-done.6.refs_3_), channel_id=1, source_target_pairs={{0,1},{1,0},{2,3},{3,2},{4,5},{5,4},{6,7},{7,6},{8,9},{9,8},{10,11... | collective-permute-start | bytes 1572872 | tf_op jit(solution)/shard_map/ppermute | solution.py:27
  88.1 24.0 %collective-permute-start.22 = (bf16[2,64,2048]{2,1,0:T(8,128)(2,1)S(1)}, bf16[2,64,2048]{2,1,0:T(8,128)(2,1)S(1)}, u32[]{:S(2)}, u32[]{:S(2)}) collective-permute-start(bf16[2,64,2048]{2,1,0:T(8,128)(2,1)S(1)} %get-tuple-element.69.refs_0_), channel_id=1, source_target_pairs={{0,1},{1,0},{2,3},{3,2},{4,5},{5,4},{6,7},{7,6},{8,9},{9,8},{10,11... | collective-permute-start | bytes 1572872 | tf_op jit(solution)/shard_map/ppermute | solution.py:27
  88.4 34.9 %collective-permute-start.23 = (bf16[2,64,2048]{2,1,0:T(8,128)(2,1)S(1)}, bf16[2,64,2048]{2,1,0:T(8,128)(2,1)S(1)}, u32[]{:S(2)}, u32[]{:S(2)}) collective-permute-start(bf16[2,64,2048]{2,1,0:T(8,128)(2,1)S(1)} %collective-permute-done.21.refs_1_), channel_id=1, source_target_pairs={{0,1},{1,0},{2,3},{3,2},{4,5},{5,4},{6,7},{7,6},{8,9},{9,8},{10,11... | collective-permute-start | bytes 1572872 | tf_op jit(solution)/shard_map/ppermute | solution.py:27
  92.2 42.3 %collective-permute-start.31 = (bf16[2,64,2048]{2,1,0:T(8,128)(2,1)S(1)}, bf16[2,64,2048]{2,1,0:T(8,128)(2,1)S(1)}, u32[]{:S(2)}, u32[]{:S(2)}) collective-permute-start(bf16[2,64,2048]{2,1,0:T(8,128)(2,1)S(1)} %get-tuple-element.75.refs_0_), channel_id=1, source_target_pairs={{0,1},{1,0},{2,3},{3,2},{4,5},{5,4},{6,7},{7,6},{8,9},{9,8},{10,11... | collective-permute-start | bytes 1572872 | tf_op jit(solution)/shard_map/ppermute | solution.py:27
  92.6 46.5 %collective-permute-start.34 = (bf16[2,64,2048]{2,1,0:T(8,128)(2,1)S(1)}, bf16[2,64,2048]{2,1,0:T(8,128)(2,1)S(1)}, u32[]{:S(2)}, u32[]{:S(2)}) collective-permute-start(bf16[2,64,2048]{2,1,0:T(8,128)(2,1)S(1)} %get-tuple-element.78), channel_id=1, source_target_pairs={{0,2},{1,3},{2,0},{3,1},{4,6},{5,7},{6,4},{7,5},{8,10},{9,11},{10,... | collective-permute-start | bytes 1572872 | tf_op jit(solution)/shard_map/ppermute | solution.py:27
  126.9 13.5 %collective-permute-start.38 = (f32[6,64]{1,0:T(8,128)S(1)}, f32[6,64]{1,0:T(8,128)S(1)}, u32[]{:S(2)}, u32[]{:S(2)}) collective-permute-start(f32[6,64]{1,0:T(8,128)S(1)} %pad_maximum_fusion), channel_id=1, source_target_pairs={{0,1},{1,0},{2,3},{3,2},{4,5},{5,4},{6,7},{7,6},{8,9},{9,8},{10,11... | collective-permute-start | bytes 4616 | tf_op jit(solution)/shard_map/ppermute | solution.py:27
  128.1 17.0 %collective-permute-start.1 = (f32[4,128]{1,0:T(4,128)S(1)}, f32[4,128]{1,0:T(4,128)S(1)}, u32[]{:S(2)}, u32[]{:S(2)}) collective-permute-start(f32[4,128]{1,0:T(4,128)S(1)} %pad_maximum_fusion.2.code_ref.mine_ref), channel_id=1, source_target_pairs={{16,17},{17,16},{18,19},{19,18},{20,21},{21,20},{22,23},{23,22},{2... | collective-permute-start | bytes 6152 | tf_op jit(solution)/shard_map/ppermute | solution.py:27
  130.5 18.9 %collective-permute-start.11 = (bf16[2,64,2048]{2,1,0:T(8,128)(2,1)S(1)}, bf16[2,64,2048]{2,1,0:T(8,128)(2,1)S(1)}, u32[]{:S(2)}, u32[]{:S(2)}) collective-permute-start(bf16[2,64,2048]{2,1,0:T(8,128)(2,1)S(1)} %get-tuple-element.66), channel_id=1, source_target_pairs={{16,18},{17,19},{18,16},{19,17},{20,22},{21,23},{22,20},{23,21},{2... | collective-permute-start | bytes 1572872 | tf_op jit(solution)/shard_map/ppermute | solution.py:27
  134.6 27.1 %collective-permute-start.12 = (bf16[2,64,2048]{2,1,0:T(8,128)(2,1)S(1)}, bf16[2,64,2048]{2,1,0:T(8,128)(2,1)S(1)}, u32[]{:S(2)}, u32[]{:S(2)}) collective-permute-start(bf16[2,64,2048]{2,1,0:T(8,128)(2,1)S(1)} %get-tuple-element.67), channel_id=1, source_target_pairs={{16,20},{17,21},{18,22},{19,23},{20,16},{21,17},{22,18},{23,19},{2... | collective-permute-start | bytes 1572872 | tf_op jit(solution)/shard_map/ppermute | solution.py:27
  139.1 12.5 %collective-permute-start.35 = (bf16[2,64,2048]{2,1,0:T(8,128)(2,1)S(1)}, bf16[2,64,2048]{2,1,0:T(8,128)(2,1)S(1)}, u32[]{:S(2)}, u32[]{:S(2)}) collective-permute-start(bf16[2,64,2048]{2,1,0:T(8,128)(2,1)S(1)} %collective-permute-done.34.refs_0_), channel_id=1, source_target_pairs={{0,1},{1,0},{2,3},{3,2},{4,5},{5,4},{6,7},{7,6},{8,9},{9,8},{10,11... | collective-permute-start | bytes 1572872 | tf_op jit(solution)/shard_map/ppermute | solution.py:27
  140.4 2.5 %collective-permute-start.39 = (f32[3,64]{1,0:T(4,128)S(1)}, f32[3,64]{1,0:T(4,128)S(1)}, u32[]{:S(2)}, u32[]{:S(2)}) collective-permute-start(f32[3,64]{1,0:T(4,128)S(1)} %pad_maximum_fusion.3), channel_id=1, source_target_pairs={{0,2},{1,3},{2,0},{3,1},{4,6},{5,7},{6,4},{7,5},{8,10},{9,11},{10,... | collective-permute-start | bytes 2312 | tf_op jit(solution)/shard_map/ppermute | solution.py:27
  142.9 15.6 %collective-permute-start.32 = (bf16[64,2048]{1,0:T(8,128)(2,1)S(1)}, bf16[64,2048]{1,0:T(8,128)(2,1)S(1)}, u32[]{:S(2)}, u32[]{:S(2)}) collective-permute-start(bf16[64,2048]{1,0:T(8,128)(2,1)S(1)} %get-tuple-element.77), channel_id=1, source_target_pairs={{16,17},{17,16},{18,19},{19,18},{20,21},{21,20},{22,23},{23,22},{2... | collective-permute-start | bytes 786440 | tf_op jit(solution)/shard_map/ppermute | solution.py:27
  145.1 17.9 %collective-permute-start.13 = (bf16[2,64,2048]{2,1,0:T(8,128)(2,1)S(1)}, bf16[2,64,2048]{2,1,0:T(8,128)(2,1)S(1)}, u32[]{:S(2)}, u32[]{:S(2)}) collective-permute-start(bf16[2,64,2048]{2,1,0:T(8,128)(2,1)S(1)} %get-tuple-element.68), channel_id=1, source_target_pairs={{16,22},{17,23},{18,20},{19,21},{20,18},{21,19},{22,16},{23,17},{2... | collective-permute-start | bytes 1572872 | tf_op jit(solution)/shard_map/ppermute | solution.py:27
  149.4 19.4 %collective-permute-start.24 = (bf16[2,64,2048]{2,1,0:T(8,128)(2,1)S(1)}, bf16[2,64,2048]{2,1,0:T(8,128)(2,1)S(1)}, u32[]{:S(2)}, u32[]{:S(2)}) collective-permute-start(bf16[2,64,2048]{2,1,0:T(8,128)(2,1)S(1)} %get-tuple-element.71), channel_id=1, source_target_pairs={{16,24},{17,25},{18,26},{19,27},{20,28},{21,29},{22,30},{23,31},{2... | collective-permute-start | bytes 1572872 | tf_op jit(solution)/shard_map/ppermute | solution.py:27
  151.6 22.8 %collective-permute-start.25 = (bf16[2,64,2048]{2,1,0:T(8,128)(2,1)S(1)}, bf16[2,64,2048]{2,1,0:T(8,128)(2,1)S(1)}, u32[]{:S(2)}, u32[]{:S(2)}) collective-permute-start(bf16[2,64,2048]{2,1,0:T(8,128)(2,1)S(1)} %get-tuple-element.72), channel_id=1, source_target_pairs={{16,26},{17,27},{18,24},{19,25},{20,30},{21,31},{22,28},{23,29},{2... | collective-permute-start | bytes 1572872 | tf_op jit(solution)/shard_map/ppermute | solution.py:27
  158.5 18.3 %collective-permute-start.36 = (bf16[64,2048]{1,0:T(8,128)(2,1)S(1)}, bf16[64,2048]{1,0:T(8,128)(2,1)S(1)}, u32[]{:S(2)}, u32[]{:S(2)}) collective-permute-start(bf16[64,2048]{1,0:T(8,128)(2,1)S(1)} %get-tuple-element.80), channel_id=1, source_target_pairs={{16,17},{17,16},{18,19},{19,18},{20,21},{21,20},{22,23},{23,22},{2... | collective-permute-start | bytes 786440 | tf_op jit(solution)/shard_map/ppermute | solution.py:27
  161.7 16.5 %collective-permute-start.42 = (f32[1,64]{1,0:T(1,128)S(1)}, f32[1,64]{1,0:T(1,128)S(1)}, u32[]{:S(2)}, u32[]{:S(2)}) collective-permute-start(f32[1,64]{1,0:T(1,128)S(1)} %get-tuple-element.127), channel_id=1, source_target_pairs={{0,12},{1,13},{2,14},{3,15},{4,8},{5,9},{6,10},{7,11},{8,4},{9,5},... | collective-permute-start | bytes 776 | tf_op jit(solution)/shard_map/ppermute | solution.py:27
  163.0 18.1 %collective-permute-start.43 = (f32[1,64]{1,0:T(1,128)S(1)}, f32[1,64]{1,0:T(1,128)S(1)}, u32[]{:S(2)}, u32[]{:S(2)}) collective-permute-start(f32[1,64]{1,0:T(1,128)S(1)} %get-tuple-element.126), channel_id=1, source_target_pairs={{0,13},{1,12},{2,15},{3,14},{4,9},{5,8},{6,11},{7,10},{8,5},{9,4},... | collective-permute-start | bytes 776 | tf_op jit(solution)/shard_map/ppermute | solution.py:27
  168.8 13.6 %collective-permute-start.41 = (f32[2,64]{1,0:T(2,128)S(1)}, f32[2,64]{1,0:T(2,128)S(1)}, u32[]{:S(2)}, u32[]{:S(2)}) collective-permute-start(f32[2,64]{1,0:T(2,128)S(1)} %pad_maximum_fusion.5), channel_id=1, source_target_pairs={{0,8},{1,9},{2,10},{3,11},{4,12},{5,13},{6,14},{7,15},{8,0},{9,1},... | collective-permute-start | bytes 1544 | tf_op jit(solution)/shard_map/ppermute | solution.py:27
  175.5 32.7 %collective-permute-start.26 = (bf16[128,2048]{1,0:T(8,128)(2,1)S(1)}, bf16[128,2048]{1,0:T(8,128)(2,1)S(1)}, u32[]{:S(2)}, u32[]{:S(2)}) collective-permute-start(bf16[128,2048]{1,0:T(8,128)(2,1)S(1)} %get-tuple-element.73), channel_id=1, source_target_pairs={{16,0},{17,1},{18,2},{19,3},{20,4},{21,5},{22,6},{23,7},{24,8},{25... | collective-permute-start | bytes 1572872 | tf_op jit(solution)/shard_map/ppermute | solution.py:27
  176.8 31.3 %collective-permute-start.27 = (bf16[128,2048]{1,0:T(8,128)(2,1)S(1)}, bf16[128,2048]{1,0:T(8,128)(2,1)S(1)}, u32[]{:S(2)}, u32[]{:S(2)}) collective-permute-start(bf16[128,2048]{1,0:T(8,128)(2,1)S(1)} %get-tuple-element.74), channel_id=1, source_target_pairs={{16,1},{17,0},{18,3},{19,2},{20,5},{21,4},{22,7},{23,6},{24,9},{25... | collective-permute-start | bytes 1572872 | tf_op jit(solution)/shard_map/ppermute | solution.py:27
  178.2 5.5 %collective-permute-start.40 = (f32[2,64]{1,0:T(2,128)S(1)}, f32[2,64]{1,0:T(2,128)S(1)}, u32[]{:S(2)}, u32[]{:S(2)}) collective-permute-start(f32[2,64]{1,0:T(2,128)S(1)} %pad_maximum_fusion.4), channel_id=1, source_target_pairs={{0,4},{1,5},{2,6},{3,7},{4,0},{5,1},{6,2},{7,3},{8,12},{9,13},{10,... | collective-permute-start | bytes 1544 | tf_op jit(solution)/shard_map/ppermute | solution.py:27
  181.1 27.0 %collective-permute-start.33 = (bf16[64,2048]{1,0:T(8,128)(2,1)S(1)}, bf16[64,2048]{1,0:T(8,128)(2,1)S(1)}, u32[]{:S(2)}, u32[]{:S(2)}) collective-permute-start(bf16[64,2048]{1,0:T(8,128)(2,1)S(1)} %add_convert_fusion.1), channel_id=1, source_target_pairs={{16,12},{17,13},{18,14},{19,15},{20,8},{21,9},{22,10},{23,11},{24,... | collective-permute-start | bytes 786440 | tf_op jit(solution)/shard_map/ppermute | solution.py:27
  182.4 25.7 %collective-permute-start.37 = (bf16[64,2048]{1,0:T(8,128)(2,1)S(1)}, bf16[64,2048]{1,0:T(8,128)(2,1)S(1)}, u32[]{:S(2)}, u32[]{:S(2)}) collective-permute-start(bf16[64,2048]{1,0:T(8,128)(2,1)S(1)} %add_convert_fusion), channel_id=1, source_target_pairs={{16,14},{17,15},{18,12},{19,13},{20,10},{21,11},{22,8},{23,9},{24,... | collective-permute-start | bytes 786440 | tf_op jit(solution)/shard_map/ppermute | solution.py:27
  183.7 12.0 %collective-permute-start.44 = (f32[1,64]{1,0:T(1,128)S(1)}, f32[1,64]{1,0:T(1,128)S(1)}, u32[]{:S(2)}, u32[]{:S(2)}) collective-permute-start(f32[1,64]{1,0:T(1,128)S(1)} %get-tuple-element.125), channel_id=1, source_target_pairs={{0,14},{1,15},{2,12},{3,13},{4,10},{5,11},{6,8},{7,9},{8,6},{9,7},... | collective-permute-start | bytes 776 | tf_op jit(solution)/shard_map/ppermute | solution.py:27
  195.8 5.7 %collective-permute-start.45 = (f32[1,64]{1,0:T(1,128)S(1)}, f32[1,64]{1,0:T(1,128)S(1)}, u32[]{:S(2)}, u32[]{:S(2)}) collective-permute-start(f32[1,64]{1,0:T(1,128)S(1)} %get-tuple-element.124), channel_id=1, source_target_pairs={{0,15},{1,14},{2,13},{3,12},{4,11},{5,10},{6,9},{7,8},{8,7},{9,6},... | collective-permute-start | bytes 776 | tf_op jit(solution)/shard_map/ppermute | solution.py:27
  201.5 6.6 %collective-permute-start = (f32[4,128]{1,0:T(4,128)S(1)}, f32[4,128]{1,0:T(4,128)S(1)}, u32[]{:S(2)}, u32[]{:S(2)}) collective-permute-start(f32[4,128]{1,0:T(4,128)S(1)} %pad_maximum_fusion.2.code_ref.mine_ref), channel_id=1, source_target_pairs={{16,0},{17,1},{18,2},{19,3},{20,4},{21,5},{22,6},{23,7},{24,8},{25... | collective-permute-start | bytes 6152 | tf_op jit(solution)/shard_map/ppermute | solution.py:27
  (3 other events, 3.5 us)

commit v2 on v1

--- a/solution.py
+++ b/solution.py
@@ -33,8 +33,8 @@
 
 def groups_of(experts):
     ring = experts // LINE
-    head = [list(range(2 * ring)), list(range(2 * ring, experts - 2))]
-    return [group for group in head if group] + [[experts - 2], [experts - 1]]
+    head = [list(range(i, min(i + ring, experts - 2))) for i in range(0, experts - 2, ring)]
+    return head + [[experts - 2], [experts - 1]]
 
 
 def kept(shape, kind):
@@ -363,8 +363,8 @@
             else:
                 got[o] = parts[i] if o == 0 else shifted(parts[i], 2 * o, 1)
 
-    begun = grads(chunks[:1], last=False)
-    g_gate, g_up, g_down = grads(chunks[1:], begun)
+    begun = grads(chunks[:2], last=False)
+    g_gate, g_up, g_down = grads(chunks[2:], begun)
 
     early = [o for o in range(experts) if o not in last]
     slots = jnp.stack([near_rg[o] for o in early])

time: 210 us -> 195 us (0.929)
  waiting for transfers between devices: 95.3 us -> 83.9 us
  starting transfers between devices: 78.3 us -> 73.7 us
    ppermute x46, waiting for transfers between devices: 95.3 us -> 83.9 us  [moved(): return lax.ppermute(value, AXES, pairs)]
    ppermute x46, starting transfers between devices: 78.3 us -> 73.7 us  [moved(): return lax.ppermute(value, AXES, pairs)]
    pallas_call x4 -> x5, Pallas kernels: 15 us -> 15.5 us  [phase(): pl.pallas_call(functools.partial(phase_kernel, size, reduced), out_shape=...]
  transfers between devices with their start and end apart: 46 -> 46, of which waited for: 17 -> 16; matrix products, arithmetic and copies ran while one was open for 1% -> 1% of each run, Pallas kernels for 14% -> 15%
where the time goes in v2:
time: 195 us; the launch traced here: 194 us
  waiting for transfers between devices  83.9 us (43%)
  starting transfers between devices  73.7 us (38%)
  Pallas kernels  30.2 us (15%)
  local copies, waits for them, and re-layouts  3.53 us (2%)
    ppermute x46, waiting for transfers between devices, moved(): return lax.ppermute(value, AXES, pairs)  83.9 us
    ppermute x46, starting transfers between devices, moved(): return lax.ppermute(value, AXES, pairs)  73.7 us
    pallas_call x5, Pallas kernels, phase(): pl.pallas_call(functools.partial(phase_kernel, size, reduced), out_shape=...  15.5 us
    pallas_call x2, Pallas kernels, grads(): pl.pallas_call(functools.partial(grads_kernel, len(chunks), bool(olds), l...  7.6 us
  transfers between devices with their start and end apart: 46, of which 16 were waited for; matrix products, arithmetic and copies ran while one was open for 1% of the time, Pallas kernels for 15%

profile of v2, /device:TPU:9, one launch (start us, length us, event | category | flops | bytes accessed | tf_op | source)
XLA Modules:
  0.0 194.0 jit_solution(12435652443285992560)
XLA Ops:
  0.7 4.5 %collective-permute-start.16 = (bf16[128,2048]{1,0:T(8,128)(2,1)}, bf16[128,2048]{1,0:T(8,128)(2,1)S(1)}, u32[]{:S(2)}, u32[]{:S(2)}) collective-permute-start(bf16[128,2048]{1,0:T(8,128)(2,1)} %bitcast.24), channel_id=1, source_target_pairs={{4,8},{5,9},{6,10},{7,11},{8,4},{9,5},{10,6},{11,7},{20,24},{21,25... | collective-permute-start | bytes 1572872 | tf_op jit(solution)/shard_map/ppermute | solution.py:27
  5.3 1.9 collective-permute-start.19
  8.8 16.2 %collective-permute-done.6.code_ref = f32[4,128]{1,0:T(4,128)S(1)} collective-permute-done((f32[4,128]{1,0:T(4,128)S(1)}, f32[4,128]{1,0:T(4,128)S(1)}, u32[]{:S(2)}, u32[]{:S(2)}) %collective-permute-start.6) | collective-permute-done | bytes 2080 | tf_op jit(solution)/shard_map/ppermute | solution.py:27
  25.0 2.3 %collective-permute-start.14 = (f32[4,128]{1,0:T(4,128)S(1)}, f32[4,128]{1,0:T(4,128)S(1)}, u32[]{:S(2)}, u32[]{:S(2)}) collective-permute-start(f32[4,128]{1,0:T(4,128)S(1)} %pad_maximum_fusion.2.code_ref.mine_ref), channel_id=1, source_target_pairs={{0,8},{1,9},{2,10},{3,11},{4,12},{5,13},{6,14},{7,15},{8,0},{9,1},... | collective-permute-start | bytes 6152 | tf_op jit(solution)/shard_map/ppermute | solution.py:27
  30.2 1.3 collective-permute-start.2
  31.5 1.9 collective-permute-start.15
  33.5 1.3 collective-permute-start.17
  34.8 3.4 %collective-permute-start.18 = (bf16[128,2048]{1,0:T(8,128)(2,1)S(1)}, bf16[128,2048]{1,0:T(8,128)(2,1)S(1)}, u32[]{:S(2)}, u32[]{:S(2)}) collective-permute-start(bf16[128,2048]{1,0:T(8,128)(2,1)S(1)} %collective-permute-done.8.refs_1_), channel_id=1, source_target_pairs={{4,8},{5,9},{6,10},{7,11},{8,4},{9,5},{10,6},{11,7},{20,24},{21,25... | collective-permute-start | bytes 1572872 | tf_op jit(solution)/shard_map/ppermute | solution.py:27
  38.2 1.3 collective-permute-start.20
  39.5 2.4 %collective-permute-done.2.refs_1_ = bf16[2,64,2048]{2,1,0:T(8,128)(2,1)S(1)} collective-permute-done((bf16[2,64,2048]{2,1,0:T(8,128)(2,1)S(1)}, bf16[2,64,2048]{2,1,0:T(8,128)(2,1)S(1)}, u32[]{:S(2)}, u32[]{:S(2)}) %collective-permute-start.2) | collective-permute-done | bytes 524320 | tf_op jit(solution)/shard_map/ppermute | solution.py:27
  43.2 1.6 collective-permute-done.15.refs_0_
  47.1 8.9 %collective-permute-done.18.refs_2_ = bf16[128,2048]{1,0:T(8,128)(2,1)S(1)} collective-permute-done((bf16[128,2048]{1,0:T(8,128)(2,1)S(1)}, bf16[128,2048]{1,0:T(8,128)(2,1)S(1)}, u32[]{:S(2)}, u32[]{:S(2)}) %collective-permute-start.18) | collective-permute-done | bytes 524320 | tf_op jit(solution)/shard_map/ppermute | solution.py:27
  57.2 1.6 collective-permute-done.28.code_ref
  58.8 1.4 collective-permute-start.29
  60.2 1.3 collective-permute-start.30
  61.6 2.4 %collective-permute-done.4.refs_3_ = bf16[2,64,2048]{2,1,0:T(8,128)(2,1)S(1)} collective-permute-done((bf16[2,64,2048]{2,1,0:T(8,128)(2,1)S(1)}, bf16[2,64,2048]{2,1,0:T(8,128)(2,1)S(1)}, u32[]{:S(2)}, u32[]{:S(2)}) %collective-permute-start.4) | collective-permute-done | bytes 524320 | tf_op jit(solution)/shard_map/ppermute | solution.py:27
  65.5 5.4 %collective-permute-done.21.refs_1_ = bf16[2,64,2048]{2,1,0:T(8,128)(2,1)S(1)} collective-permute-done((bf16[2,64,2048]{2,1,0:T(8,128)(2,1)S(1)}, bf16[2,64,2048]{2,1,0:T(8,128)(2,1)S(1)}, u32[]{:S(2)}, u32[]{:S(2)}) %collective-permute-start.21) | collective-permute-done | bytes 524320 | tf_op jit(solution)/shard_map/ppermute | solution.py:27
  70.9 1.5 collective-permute-start.23
  72.4 1.4 copy-done.2
  74.1 3.5 %phase.5 = (bf16[256,2048]{1,0:T(8,128)(2,1)S(1)}, bf16[256,2048]{1,0:T(8,128)(2,1)S(1)}, bf16[256,384]{1,0:T(8,128)(2,1)S(1)}, bf16[256,384]{1,0:T(8,128)(2,1)S...) custom-call(bf16[2,64,2048]{2,1,0:T(8,128)(2,1)S(1)} %get-tuple-elem, ...), custom_call_target="tpu_custom_call" | custom-call | tf_op jit(solution)/shard_map/phase/pallas_call | solution.py:179
  77.6 1.7 collective-permute-done.30.refs_3_
  82.8 2.8 %collective-permute-done.11.refs_3_ = bf16[2,64,2048]{2,1,0:T(8,128)(2,1)S(1)} collective-permute-done((bf16[2,64,2048]{2,1,0:T(8,128)(2,1)S(1)}, bf16[2,64,2048]{2,1,0:T(8,128)(2,1)S(1)}, u32[]{:S(2)}, u32[]{:S(2)}) %collective-permute-start.11) | collective-permute-done | bytes 524320 | tf_op jit(solution)/shard_map/ppermute | solution.py:27
  85.6 3.5 %phase.6 = (bf16[256,2048]{1,0:T(8,128)(2,1)S(1)}, bf16[256,2048]{1,0:T(8,128)(2,1)S(1)}, bf16[256,384]{1,0:T(8,128)(2,1)S(1)}, bf16[256,384]{1,0:T(8,128)(2,1)S...) custom-call(bf16[2,64,2048]{2,1,0:T(8,128)(2,1)S(1)} %get-tuple-elem, ...), custom_call_target="tpu_custom_call" | custom-call | tf_op jit(solution)/shard_map/phase/pallas_call | solution.py:179
  89.1 7.8 %collective-permute-done.22.refs_2_ = bf16[2,64,2048]{2,1,0:T(8,128)(2,1)S(1)} collective-permute-done((bf16[2,64,2048]{2,1,0:T(8,128)(2,1)S(1)}, bf16[2,64,2048]{2,1,0:T(8,128)(2,1)S(1)}, u32[]{:S(2)}, u32[]{:S(2)}) %collective-permute-start.22) | collective-permute-done | bytes 524320 | tf_op jit(solution)/shard_map/ppermute | solution.py:27
  96.9 11.2 %collective-permute-done.23.refs_3_ = bf16[2,64,2048]{2,1,0:T(8,128)(2,1)S(1)} collective-permute-done((bf16[2,64,2048]{2,1,0:T(8,128)(2,1)S(1)}, bf16[2,64,2048]{2,1,0:T(8,128)(2,1)S(1)}, u32[]{:S(2)}, u32[]{:S(2)}) %collective-permute-start.23) | collective-permute-done | bytes 524320 | tf_op jit(solution)/shard_map/ppermute | solution.py:27
  108.1 3.4 %phase.7 = (bf16[256,2048]{1,0:T(8,128)(2,1)S(1)}, bf16[256,2048]{1,0:T(8,128)(2,1)S(1)}, bf16[256,384]{1,0:T(8,128)(2,1)S(1)}, bf16[256,384]{1,0:T(8,128)(2,1)S...) custom-call(bf16[2,64,2048]{2,1,0:T(8,128)(2,1)S(1)} %get-tuple-elem, ...), custom_call_target="tpu_custom_call" | custom-call | tf_op jit(solution)/shard_map/phase/pallas_call | solution.py:179
  112.9 2.1 %collective-permute-start.1 = (f32[4,128]{1,0:T(4,128)S(1)}, f32[4,128]{1,0:T(4,128)S(1)}, u32[]{:S(2)}, u32[]{:S(2)}) collective-permute-start(f32[4,128]{1,0:T(4,128)S(1)} %pad_maximum_fusion.2.code_ref.mine_ref), channel_id=1, source_target_pairs={{16,17},{17,16},{18,19},{19,18},{20,21},{21,20},{22,23},{23,22},{2... | collective-permute-start | bytes 6152 | tf_op jit(solution)/shard_map/ppermute | solution.py:27
  115.0 3.1 %collective-permute-start.5 = (bf16[2,64,2048]{2,1,0:T(8,128)(2,1)S(1)}, bf16[2,64,2048]{2,1,0:T(8,128)(2,1)S(1)}, u32[]{:S(2)}, u32[]{:S(2)}) collective-permute-start(bf16[2,64,2048]{2,1,0:T(8,128)(2,1)S(1)} %get-tuple-element.70), channel_id=1, source_target_pairs={{16,18},{17,19},{18,16},{19,17},{20,22},{21,23},{22,20},{23,21},{2... | collective-permute-start | bytes 1572872 | tf_op jit(solution)/shard_map/ppermute | solution.py:27
  119.3 2.1 %collective-permute-start.12 = (bf16[2,64,2048]{2,1,0:T(8,128)(2,1)S(1)}, bf16[2,64,2048]{2,1,0:T(8,128)(2,1)S(1)}, u32[]{:S(2)}, u32[]{:S(2)}) collective-permute-start(bf16[2,64,2048]{2,1,0:T(8,128)(2,1)S(1)} %get-tuple-element.73), channel_id=1, source_target_pairs={{16,20},{17,21},{18,22},{19,23},{20,16},{21,17},{22,18},{23,19},{2... | collective-permute-start | bytes 1572872 | tf_op jit(solution)/shard_map/ppermute | solution.py:27
  121.4 2.6 %phase.8 = (bf16[128,2048]{1,0:T(8,128)(2,1)S(1)}, bf16[128,2048]{1,0:T(8,128)(2,1)S(1)}, bf16[128,384]{1,0:T(8,128)(2,1)S(1)}, bf16[128,384]{1,0:T(8,128)(2,1)S...) custom-call(bf16[2,64,2048]{2,1,0:T(8,128)(2,1)S(1)} %get-tuple-elem, ...), custom_call_target="tpu_custom_call" | custom-call | tf_op jit(solution)/shard_map/phase/pallas_call | solution.py:179
  125.3 1.3 collective-permute-start.39
  127.8 2.1 %collective-permute-start.32 = (bf16[64,2048]{1,0:T(8,128)(2,1)S(1)}, bf16[64,2048]{1,0:T(8,128)(2,1)S(1)}, u32[]{:S(2)}, u32[]{:S(2)}) collective-permute-start(bf16[64,2048]{1,0:T(8,128)(2,1)S(1)} %get-tuple-element.83), channel_id=1, source_target_pairs={{16,17},{17,16},{18,19},{19,18},{20,21},{21,20},{22,23},{23,22},{2... | collective-permute-start | bytes 786440 | tf_op jit(solution)/shard_map/ppermute | solution.py:27
  130.0 4.2 %collective-permute-start.13 = (bf16[2,64,2048]{2,1,0:T(8,128)(2,1)S(1)}, bf16[2,64,2048]{2,1,0:T(8,128)(2,1)S(1)}, u32[]{:S(2)}, u32[]{:S(2)}) collective-permute-start(bf16[2,64,2048]{2,1,0:T(8,128)(2,1)S(1)} %get-tuple-element.74), channel_id=1, source_target_pairs={{16,22},{17,23},{18,20},{19,21},{20,18},{21,19},{22,16},{23,17},{2... | collective-permute-start | bytes 1572872 | tf_op jit(solution)/shard_map/ppermute | solution.py:27
  134.2 1.9 collective-permute-start.24
  136.1 4.2 %collective-permute-start.25 = (bf16[2,64,2048]{2,1,0:T(8,128)(2,1)S(1)}, bf16[2,64,2048]{2,1,0:T(8,128)(2,1)S(1)}, u32[]{:S(2)}, u32[]{:S(2)}) collective-permute-start(bf16[2,64,2048]{2,1,0:T(8,128)(2,1)S(1)} %get-tuple-element.78), channel_id=1, source_target_pairs={{16,26},{17,27},{18,24},{19,25},{20,30},{21,31},{22,28},{23,29},{2... | collective-permute-start | bytes 1572872 | tf_op jit(solution)/shard_map/ppermute | solution.py:27
  140.4 2.6 %phase.9 = (bf16[128,2048]{1,0:T(8,128)(2,1)S(1)}, bf16[128,2048]{1,0:T(8,128)(2,1)S(1)}, bf16[128,384]{1,0:T(8,128)(2,1)S(1)}, bf16[128,384]{1,0:T(8,128)(2,1)S...) custom-call(bf16[2,64,2048]{2,1,0:T(8,128)(2,1)S(1)} %collective-per, ...), custom_call_target="tpu_custom_call" | custom-call | tf_op jit(solution)/shard_map/phase/pallas_call | solution.py:179
  142.9 3.3 %collective-permute-start.36 = (bf16[64,2048]{1,0:T(8,128)(2,1)S(1)}, bf16[64,2048]{1,0:T(8,128)(2,1)S(1)}, u32[]{:S(2)}, u32[]{:S(2)}) collective-permute-start(bf16[64,2048]{1,0:T(8,128)(2,1)S(1)} %get-tuple-element.86), channel_id=1, source_target_pairs={{16,17},{17,16},{18,19},{19,18},{20,21},{21,20},{22,23},{23,22},{2... | collective-permute-start | bytes 786440 | tf_op jit(solution)/shard_map/ppermute | solution.py:27
  147.8 5.7 %collective-permute-done.24.refs_4_ = bf16[2,64,2048]{2,1,0:T(8,128)(2,1)S(1)} collective-permute-done((bf16[2,64,2048]{2,1,0:T(8,128)(2,1)S(1)}, bf16[2,64,2048]{2,1,0:T(8,128)(2,1)S(1)}, u32[]{:S(2)}, u32[]{:S(2)}) %collective-permute-start.24) | collective-permute-done | bytes 524320 | tf_op jit(solution)/shard_map/ppermute | solution.py:27
  153.6 2.8 %collective-permute-start.41 = (f32[2,64]{1,0:T(2,128)S(1)}, f32[2,64]{1,0:T(2,128)S(1)}, u32[]{:S(2)}, u32[]{:S(2)}) collective-permute-start(f32[2,64]{1,0:T(2,128)S(1)} %pad_maximum_fusion.5), channel_id=1, source_target_pairs={{0,8},{1,9},{2,10},{3,11},{4,12},{5,13},{6,14},{7,15},{8,0},{9,1},... | collective-permute-start | bytes 1544 | tf_op jit(solution)/shard_map/ppermute | solution.py:27
  156.4 2.8 %collective-permute-done.25.refs_5_ = bf16[2,64,2048]{2,1,0:T(8,128)(2,1)S(1)} collective-permute-done((bf16[2,64,2048]{2,1,0:T(8,128)(2,1)S(1)}, bf16[2,64,2048]{2,1,0:T(8,128)(2,1)S(1)}, u32[]{:S(2)}, u32[]{:S(2)}) %collective-permute-start.25) | collective-permute-done | bytes 524320 | tf_op jit(solution)/shard_map/ppermute | solution.py:27
  160.3 1.3 collective-permute-start.26
  161.6 1.3 collective-permute-start.27
  163.0 3.0 %collective-permute-start.40 = (f32[2,64]{1,0:T(2,128)S(1)}, f32[2,64]{1,0:T(2,128)S(1)}, u32[]{:S(2)}, u32[]{:S(2)}) collective-permute-start(f32[2,64]{1,0:T(2,128)S(1)} %pad_maximum_fusion.4), channel_id=1, source_target_pairs={{0,4},{1,5},{2,6},{3,7},{4,0},{5,1},{6,2},{7,3},{8,12},{9,13},{10,... | collective-permute-start | bytes 1544 | tf_op jit(solution)/shard_map/ppermute | solution.py:27
  167.3 1.3 collective-permute-start.37
  169.8 10.8 %collective-permute-done.44.refs_2_ = f32[1,64]{1,0:T(1,128)S(1)} collective-permute-done((f32[1,64]{1,0:T(1,128)S(1)}, f32[1,64]{1,0:T(1,128)S(1)}, u32[]{:S(2)}, u32[]{:S(2)}) %collective-permute-start.44) | collective-permute-done | bytes 288 | tf_op jit(solution)/shard_map/ppermute | solution.py:27
  180.6 2.2 %collective-permute-start.45 = (f32[1,64]{1,0:T(1,128)S(1)}, f32[1,64]{1,0:T(1,128)S(1)}, u32[]{:S(2)}, u32[]{:S(2)}) collective-permute-start(f32[1,64]{1,0:T(1,128)S(1)} %get-tuple-element.138), channel_id=1, source_target_pairs={{0,15},{1,14},{2,13},{3,12},{4,11},{5,10},{6,9},{7,8},{8,7},{9,6},... | collective-permute-start | bytes 776 | tf_op jit(solution)/shard_map/ppermute | solution.py:27
  182.8 3.2 %grads.2 = (f32[384,2048]{1,0:T(8,128)S(1)}, f32[384,2048]{1,0:T(8,128)S(1)}, f32[384,2048]{1,0:T(8,128)S(1)}) custom-call(bf16[256,2048]{1,0:T(8,128)(2,1)S(1)} %get-tuple-element.107.refs_0_, bf16[256,2048]{1,0:T(8,128)(2,1)S(1)} %get-tuple-element.108.refs_1_, bf16[256,2048]{1,0:T(8,128)(2,1)S(1)} %get-tuple-element.109.refs_2_, ...), custom_call_target="tpu_custom_call" | custom-call | tf_op jit(solution)/shard_map/grads/pallas_call | solution.py:220
  187.4 4.4 %grads.3 = (bf16[2048,384]{1,0:T(8,128)(2,1)}, bf16[2048,384]{1,0:T(8,128)(2,1)}, bf16[384,2048]{1,0:T(8,128)(2,1)}) custom-call(bf16[256,2048]{1,0:T(8,128)(2,1)S(1)} %get-tuple-element.92.refs_0_, bf16[128,2048]{1,0:T(8,128)(2,1)S(1)} %get-tuple-element.93.refs_1_, bf16[128,2048]{1,0:T(8,128)(2,1)S(1)} %get-tuple-element.94.refs_2_, ...), custom_call_target="tpu_custom_call" | custom-call | tf_op jit(solution)/shard_map/grads/pallas_call | solution.py:220
  (87 shorter events, 28.4 us)
Async XLA Ops:
  0.6 30.9 %collective-permute-start.7 = (bf16[128,2048]{1,0:T(8,128)(2,1)}, bf16[128,2048]{1,0:T(8,128)(2,1)S(1)}, u32[]{:S(2)}, u32[]{:S(2)}) collective-permute-start(bf16[128,2048]{1,0:T(8,128)(2,1)} %bitcast.23), channel_id=1, source_target_pairs={{0,4},{1,5},{2,6},{3,7},{4,0},{5,1},{6,2},{7,3},{8,12},{9,13},{10,... | collective-permute-start | bytes 1572872 | tf_op jit(solution)/shard_map/ppermute | solution.py:27
  0.7 32.7 %collective-permute-start.16 = (bf16[128,2048]{1,0:T(8,128)(2,1)}, bf16[128,2048]{1,0:T(8,128)(2,1)S(1)}, u32[]{:S(2)}, u32[]{:S(2)}) collective-permute-start(bf16[128,2048]{1,0:T(8,128)(2,1)} %bitcast.24), channel_id=1, source_target_pairs={{4,8},{5,9},{6,10},{7,11},{8,4},{9,5},{10,6},{11,7},{20,24},{21,25... | collective-permute-start | bytes 1572872 | tf_op jit(solution)/shard_map/ppermute | solution.py:27
  5.2 29.6 %collective-permute-start.8 = (bf16[128,2048]{1,0:T(8,128)(2,1)}, bf16[128,2048]{1,0:T(8,128)(2,1)S(1)}, u32[]{:S(2)}, u32[]{:S(2)}) collective-permute-start(bf16[128,2048]{1,0:T(8,128)(2,1)} %bitcast.26), channel_id=1, source_target_pairs={{0,4},{1,5},{2,6},{3,7},{4,0},{5,1},{6,2},{7,3},{8,12},{9,13},{10,... | collective-permute-start | bytes 1572872 | tf_op jit(solution)/shard_map/ppermute | solution.py:27
  5.3 32.9 %collective-permute-start.19 = (bf16[128,2048]{1,0:T(8,128)(2,1)}, bf16[128,2048]{1,0:T(8,128)(2,1)S(1)}, u32[]{:S(2)}, u32[]{:S(2)}) collective-permute-start(bf16[128,2048]{1,0:T(8,128)(2,1)} %bitcast.27), channel_id=1, source_target_pairs={{4,8},{5,9},{6,10},{7,11},{8,4},{9,5},{10,6},{11,7},{20,24},{21,25... | collective-permute-start | bytes 1572872 | tf_op jit(solution)/shard_map/ppermute | solution.py:27
  8.6 16.4 %collective-permute-start.6 = (f32[4,128]{1,0:T(4,128)S(1)}, f32[4,128]{1,0:T(4,128)S(1)}, u32[]{:S(2)}, u32[]{:S(2)}) collective-permute-start(f32[4,128]{1,0:T(4,128)S(1)} %pad_maximum_fusion.2.code_ref.mine_ref), channel_id=1, source_target_pairs={{0,4},{1,5},{2,6},{3,7},{4,0},{5,1},{6,2},{7,3},{8,12},{9,13},{10,... | collective-permute-start | bytes 6152 | tf_op jit(solution)/shard_map/ppermute | solution.py:27
  25.0 5.2 %collective-permute-start.14 = (f32[4,128]{1,0:T(4,128)S(1)}, f32[4,128]{1,0:T(4,128)S(1)}, u32[]{:S(2)}, u32[]{:S(2)}) collective-permute-start(f32[4,128]{1,0:T(4,128)S(1)} %pad_maximum_fusion.2.code_ref.mine_ref), channel_id=1, source_target_pairs={{0,8},{1,9},{2,10},{3,11},{4,12},{5,13},{6,14},{7,15},{8,0},{9,1},... | collective-permute-start | bytes 6152 | tf_op jit(solution)/shard_map/ppermute | solution.py:27
  30.2 11.7 %collective-permute-start.2 = (bf16[2,64,2048]{2,1,0:T(8,128)(2,1)S(1)}, bf16[2,64,2048]{2,1,0:T(8,128)(2,1)S(1)}, u32[]{:S(2)}, u32[]{:S(2)}) collective-permute-start(bf16[2,64,2048]{2,1,0:T(8,128)(2,1)S(1)} %get-tuple-element.65), channel_id=1, source_target_pairs={{0,2},{1,3},{2,0},{3,1},{4,6},{5,7},{6,4},{7,5},{8,10},{9,11},{10,... | collective-permute-start | bytes 1572872 | tf_op jit(solution)/shard_map/ppermute | solution.py:27
  31.5 13.3 %collective-permute-start.15 = (bf16[128,2048]{1,0:T(8,128)(2,1)S(1)}, bf16[128,2048]{1,0:T(8,128)(2,1)S(1)}, u32[]{:S(2)}, u32[]{:S(2)}) collective-permute-start(bf16[128,2048]{1,0:T(8,128)(2,1)S(1)} %collective-permute-done.7.refs_0_), channel_id=1, source_target_pairs={{4,8},{5,9},{6,10},{7,11},{8,4},{9,5},{10,6},{11,7},{20,24},{21,25... | collective-permute-start | bytes 1572872 | tf_op jit(solution)/shard_map/ppermute | solution.py:27
  33.5 13.4 %collective-permute-start.17 = (bf16[128,2048]{1,0:T(8,128)(2,1)S(1)}, bf16[128,2048]{1,0:T(8,128)(2,1)S(1)}, u32[]{:S(2)}, u32[]{:S(2)}) collective-permute-start(bf16[128,2048]{1,0:T(8,128)(2,1)S(1)} %collective-permute-done.16.refs_0_), channel_id=1, source_target_pairs={{4,0},{5,1},{6,2},{7,3},{8,12},{9,13},{10,14},{11,15},{20,16},{21,... | collective-permute-start | bytes 1572872 | tf_op jit(solution)/shard_map/ppermute | solution.py:27
  34.8 21.3 %collective-permute-start.18 = (bf16[128,2048]{1,0:T(8,128)(2,1)S(1)}, bf16[128,2048]{1,0:T(8,128)(2,1)S(1)}, u32[]{:S(2)}, u32[]{:S(2)}) collective-permute-start(bf16[128,2048]{1,0:T(8,128)(2,1)S(1)} %collective-permute-done.8.refs_1_), channel_id=1, source_target_pairs={{4,8},{5,9},{6,10},{7,11},{8,4},{9,5},{10,6},{11,7},{20,24},{21,25... | collective-permute-start | bytes 1572872 | tf_op jit(solution)/shard_map/ppermute | solution.py:27
  38.2 17.9 %collective-permute-start.20 = (bf16[128,2048]{1,0:T(8,128)(2,1)S(1)}, bf16[128,2048]{1,0:T(8,128)(2,1)S(1)}, u32[]{:S(2)}, u32[]{:S(2)}) collective-permute-start(bf16[128,2048]{1,0:T(8,128)(2,1)S(1)} %collective-permute-done.19.refs_2_), channel_id=1, source_target_pairs={{4,0},{5,1},{6,2},{7,3},{8,12},{9,13},{10,14},{11,15},{20,16},{21,... | collective-permute-start | bytes 1572872 | tf_op jit(solution)/shard_map/ppermute | solution.py:27
  42.0 30.4 %copy-start = (bf16[1,2048,384]{2,1,0:T(8,128)(2,1)S(1)}, bf16[1,2048,384]{2,1,0:T(8,128)(2,1)}, u32[]{:S(2)}) copy-start(bf16[1,2048,384]{2,1,0:T(8,128)(2,1)} %param.11) | copy-start | bytes 4718596
  42.0 30.4 %copy-start.1 = (bf16[1,2048,384]{2,1,0:T(8,128)(2,1)S(1)}, bf16[1,2048,384]{2,1,0:T(8,128)(2,1)}, u32[]{:S(2)}) copy-start(bf16[1,2048,384]{2,1,0:T(8,128)(2,1)} %param.12) | copy-start | bytes 4718596
  42.0 18.3 %collective-permute-start.3 = (bf16[2,64,2048]{2,1,0:T(8,128)(2,1)S(1)}, bf16[2,64,2048]{2,1,0:T(8,128)(2,1)S(1)}, u32[]{:S(2)}, u32[]{:S(2)}) collective-permute-start(bf16[2,64,2048]{2,1,0:T(8,128)(2,1)S(1)} %get-tuple-element.64.refs_0_), channel_id=1, source_target_pairs={{0,1},{1,0},{2,3},{3,2},{4,5},{5,4},{6,7},{7,6},{8,9},{9,8},{10,11... | collective-permute-start | bytes 1572872 | tf_op jit(solution)/shard_map/ppermute | solution.py:27
  44.8 19.2 %collective-permute-start.4 = (bf16[2,64,2048]{2,1,0:T(8,128)(2,1)S(1)}, bf16[2,64,2048]{2,1,0:T(8,128)(2,1)S(1)}, u32[]{:S(2)}, u32[]{:S(2)}) collective-permute-start(bf16[2,64,2048]{2,1,0:T(8,128)(2,1)S(1)} %collective-permute-done.2.refs_1_), channel_id=1, source_target_pairs={{0,1},{1,0},{2,3},{3,2},{4,5},{5,4},{6,7},{7,6},{8,9},{9,8},{10,11... | collective-permute-start | bytes 1572872 | tf_op jit(solution)/shard_map/ppermute | solution.py:27
  46.9 18.4 %collective-permute-start.9 = (bf16[2,64,2048]{2,1,0:T(8,128)(2,1)S(1)}, bf16[2,64,2048]{2,1,0:T(8,128)(2,1)S(1)}, u32[]{:S(2)}, u32[]{:S(2)}) collective-permute-start(bf16[2,64,2048]{2,1,0:T(8,128)(2,1)S(1)} %get-tuple-element.72), channel_id=1, source_target_pairs={{0,2},{1,3},{2,0},{3,1},{4,6},{5,7},{6,4},{7,5},{8,10},{9,11},{10,... | collective-permute-start | bytes 1572872 | tf_op jit(solution)/shard_map/ppermute | solution.py:27
  56.1 2.7 %collective-permute-start.28 = (f32[4,128]{1,0:T(4,128)S(1)}, f32[4,128]{1,0:T(4,128)S(1)}, u32[]{:S(2)}, u32[]{:S(2)}) collective-permute-start(f32[4,128]{1,0:T(4,128)S(1)} %pad_maximum_fusion.2.code_ref.mine_ref), channel_id=1, source_target_pairs={{0,12},{1,13},{2,14},{3,15},{4,8},{5,9},{6,10},{7,11},{8,4},{9,5},... | collective-permute-start | bytes 6152 | tf_op jit(solution)/shard_map/ppermute | solution.py:27
  56.9 14.0 %collective-permute-start.21 = (bf16[2,64,2048]{2,1,0:T(8,128)(2,1)S(1)}, bf16[2,64,2048]{2,1,0:T(8,128)(2,1)S(1)}, u32[]{:S(2)}, u32[]{:S(2)}) collective-permute-start(bf16[2,64,2048]{2,1,0:T(8,128)(2,1)S(1)} %get-tuple-element.76), channel_id=1, source_target_pairs={{0,2},{1,3},{2,0},{3,1},{4,6},{5,7},{6,4},{7,5},{8,10},{9,11},{10,... | collective-permute-start | bytes 1572872 | tf_op jit(solution)/shard_map/ppermute | solution.py:27
  58.8 12.1 %collective-permute-start.29 = (bf16[128,2048]{1,0:T(8,128)(2,1)S(1)}, bf16[128,2048]{1,0:T(8,128)(2,1)S(1)}, u32[]{:S(2)}, u32[]{:S(2)}) collective-permute-start(bf16[128,2048]{1,0:T(8,128)(2,1)S(1)} %collective-permute-done.15.refs_0_), channel_id=1, source_target_pairs={{4,0},{5,1},{6,2},{7,3},{8,12},{9,13},{10,14},{11,15},{20,16},{21,... | collective-permute-start | bytes 1572872 | tf_op jit(solution)/shard_map/ppermute | solution.py:27
  60.2 19.0 %collective-permute-start.30 = (bf16[128,2048]{1,0:T(8,128)(2,1)S(1)}, bf16[128,2048]{1,0:T(8,128)(2,1)S(1)}, u32[]{:S(2)}, u32[]{:S(2)}) collective-permute-start(bf16[128,2048]{1,0:T(8,128)(2,1)S(1)} %collective-permute-done.18.refs_2_), channel_id=1, source_target_pairs={{4,0},{5,1},{6,2},{7,3},{8,12},{9,13},{10,14},{11,15},{20,16},{21,... | collective-permute-start | bytes 1572872 | tf_op jit(solution)/shard_map/ppermute | solution.py:27
  64.0 17.5 %collective-permute-start.10 = (bf16[2,64,2048]{2,1,0:T(8,128)(2,1)S(1)}, bf16[2,64,2048]{2,1,0:T(8,128)(2,1)S(1)}, u32[]{:S(2)}, u32[]{:S(2)}) collective-permute-start(bf16[2,64,2048]{2,1,0:T(8,128)(2,1)S(1)} %get-tuple-element.71.refs_0_), channel_id=1, source_target_pairs={{0,1},{1,0},{2,3},{3,2},{4,5},{5,4},{6,7},{7,6},{8,9},{9,8},{10,11... | collective-permute-start | bytes 1572872 | tf_op jit(solution)/shard_map/ppermute | solution.py:27
  65.2 20.4 %collective-permute-start.11 = (bf16[2,64,2048]{2,1,0:T(8,128)(2,1)S(1)}, bf16[2,64,2048]{2,1,0:T(8,128)(2,1)S(1)}, u32[]{:S(2)}, u32[]{:S(2)}) collective-permute-start(bf16[2,64,2048]{2,1,0:T(8,128)(2,1)S(1)} %collective-permute-done.9.refs_1_), channel_id=1, source_target_pairs={{0,1},{1,0},{2,3},{3,2},{4,5},{5,4},{6,7},{7,6},{8,9},{9,8},{10,11... | collective-permute-start | bytes 1572872 | tf_op jit(solution)/shard_map/ppermute | solution.py:27
  70.9 26.0 %collective-permute-start.22 = (bf16[2,64,2048]{2,1,0:T(8,128)(2,1)S(1)}, bf16[2,64,2048]{2,1,0:T(8,128)(2,1)S(1)}, u32[]{:S(2)}, u32[]{:S(2)}) collective-permute-start(bf16[2,64,2048]{2,1,0:T(8,128)(2,1)S(1)} %get-tuple-element.75.refs_0_), channel_id=1, source_target_pairs={{0,1},{1,0},{2,3},{3,2},{4,5},{5,4},{6,7},{7,6},{8,9},{9,8},{10,11... | collective-permute-start | bytes 1572872 | tf_op jit(solution)/shard_map/ppermute | solution.py:27
  70.9 37.2 %collective-permute-start.23 = (bf16[2,64,2048]{2,1,0:T(8,128)(2,1)S(1)}, bf16[2,64,2048]{2,1,0:T(8,128)(2,1)S(1)}, u32[]{:S(2)}, u32[]{:S(2)}) collective-permute-start(bf16[2,64,2048]{2,1,0:T(8,128)(2,1)S(1)} %collective-permute-done.21.refs_1_), channel_id=1, source_target_pairs={{0,1},{1,0},{2,3},{3,2},{4,5},{5,4},{6,7},{7,6},{8,9},{9,8},{10,11... | collective-permute-start | bytes 1572872 | tf_op jit(solution)/shard_map/ppermute | solution.py:27
  80.3 39.1 %collective-permute-start.31 = (bf16[2,64,2048]{2,1,0:T(8,128)(2,1)S(1)}, bf16[2,64,2048]{2,1,0:T(8,128)(2,1)S(1)}, u32[]{:S(2)}, u32[]{:S(2)}) collective-permute-start(bf16[2,64,2048]{2,1,0:T(8,128)(2,1)S(1)} %get-tuple-element.81.refs_0_), channel_id=1, source_target_pairs={{0,1},{1,0},{2,3},{3,2},{4,5},{5,4},{6,7},{7,6},{8,9},{9,8},{10,11... | collective-permute-start | bytes 1572872 | tf_op jit(solution)/shard_map/ppermute | solution.py:27
  81.5 42.4 %collective-permute-start.34 = (bf16[2,64,2048]{2,1,0:T(8,128)(2,1)S(1)}, bf16[2,64,2048]{2,1,0:T(8,128)(2,1)S(1)}, u32[]{:S(2)}, u32[]{:S(2)}) collective-permute-start(bf16[2,64,2048]{2,1,0:T(8,128)(2,1)S(1)} %get-tuple-element.84), channel_id=1, source_target_pairs={{0,2},{1,3},{2,0},{3,1},{4,6},{5,7},{6,4},{7,5},{8,10},{9,11},{10,... | collective-permute-start | bytes 1572872 | tf_op jit(solution)/shard_map/ppermute | solution.py:27
  111.6 13.7 %collective-permute-start.38 = (f32[6,64]{1,0:T(8,128)S(1)}, f32[6,64]{1,0:T(8,128)S(1)}, u32[]{:S(2)}, u32[]{:S(2)}) collective-permute-start(f32[6,64]{1,0:T(8,128)S(1)} %pad_maximum_fusion), channel_id=1, source_target_pairs={{0,1},{1,0},{2,3},{3,2},{4,5},{5,4},{6,7},{7,6},{8,9},{9,8},{10,11... | collective-permute-start | bytes 4616 | tf_op jit(solution)/shard_map/ppermute | solution.py:27
  112.9 17.1 %collective-permute-start.1 = (f32[4,128]{1,0:T(4,128)S(1)}, f32[4,128]{1,0:T(4,128)S(1)}, u32[]{:S(2)}, u32[]{:S(2)}) collective-permute-start(f32[4,128]{1,0:T(4,128)S(1)} %pad_maximum_fusion.2.code_ref.mine_ref), channel_id=1, source_target_pairs={{16,17},{17,16},{18,19},{19,18},{20,21},{21,20},{22,23},{23,22},{2... | collective-permute-start | bytes 6152 | tf_op jit(solution)/shard_map/ppermute | solution.py:27
  115.0 19.2 %collective-permute-start.5 = (bf16[2,64,2048]{2,1,0:T(8,128)(2,1)S(1)}, bf16[2,64,2048]{2,1,0:T(8,128)(2,1)S(1)}, u32[]{:S(2)}, u32[]{:S(2)}) collective-permute-start(bf16[2,64,2048]{2,1,0:T(8,128)(2,1)S(1)} %get-tuple-element.70), channel_id=1, source_target_pairs={{16,18},{17,19},{18,16},{19,17},{20,22},{21,23},{22,20},{23,21},{2... | collective-permute-start | bytes 1572872 | tf_op jit(solution)/shard_map/ppermute | solution.py:27
  119.3 27.0 %collective-permute-start.12 = (bf16[2,64,2048]{2,1,0:T(8,128)(2,1)S(1)}, bf16[2,64,2048]{2,1,0:T(8,128)(2,1)S(1)}, u32[]{:S(2)}, u32[]{:S(2)}) collective-permute-start(bf16[2,64,2048]{2,1,0:T(8,128)(2,1)S(1)} %get-tuple-element.73), channel_id=1, source_target_pairs={{16,20},{17,21},{18,22},{19,23},{20,16},{21,17},{22,18},{23,19},{2... | collective-permute-start | bytes 1572872 | tf_op jit(solution)/shard_map/ppermute | solution.py:27
  124.0 12.1 %collective-permute-start.35 = (bf16[2,64,2048]{2,1,0:T(8,128)(2,1)S(1)}, bf16[2,64,2048]{2,1,0:T(8,128)(2,1)S(1)}, u32[]{:S(2)}, u32[]{:S(2)}) collective-permute-start(bf16[2,64,2048]{2,1,0:T(8,128)(2,1)S(1)} %collective-permute-done.34.refs_0_), channel_id=1, source_target_pairs={{0,1},{1,0},{2,3},{3,2},{4,5},{5,4},{6,7},{7,6},{8,9},{9,8},{10,11... | collective-permute-start | bytes 1572872 | tf_op jit(solution)/shard_map/ppermute | solution.py:27
  125.3 2.5 %collective-permute-start.39 = (f32[3,64]{1,0:T(4,128)S(1)}, f32[3,64]{1,0:T(4,128)S(1)}, u32[]{:S(2)}, u32[]{:S(2)}) collective-permute-start(f32[3,64]{1,0:T(4,128)S(1)} %pad_maximum_fusion.3), channel_id=1, source_target_pairs={{0,2},{1,3},{2,0},{3,1},{4,6},{5,7},{6,4},{7,5},{8,10},{9,11},{10,... | collective-permute-start | bytes 2312 | tf_op jit(solution)/shard_map/ppermute | solution.py:27
  127.8 15.1 %collective-permute-start.32 = (bf16[64,2048]{1,0:T(8,128)(2,1)S(1)}, bf16[64,2048]{1,0:T(8,128)(2,1)S(1)}, u32[]{:S(2)}, u32[]{:S(2)}) collective-permute-start(bf16[64,2048]{1,0:T(8,128)(2,1)S(1)} %get-tuple-element.83), channel_id=1, source_target_pairs={{16,17},{17,16},{18,19},{19,18},{20,21},{21,20},{22,23},{23,22},{2... | collective-permute-start | bytes 786440 | tf_op jit(solution)/shard_map/ppermute | solution.py:27
  130.0 17.0 %collective-permute-start.13 = (bf16[2,64,2048]{2,1,0:T(8,128)(2,1)S(1)}, bf16[2,64,2048]{2,1,0:T(8,128)(2,1)S(1)}, u32[]{:S(2)}, u32[]{:S(2)}) collective-permute-start(bf16[2,64,2048]{2,1,0:T(8,128)(2,1)S(1)} %get-tuple-element.74), channel_id=1, source_target_pairs={{16,22},{17,23},{18,20},{19,21},{20,18},{21,19},{22,16},{23,17},{2... | collective-permute-start | bytes 1572872 | tf_op jit(solution)/shard_map/ppermute | solution.py:27
  134.2 19.4 %collective-permute-start.24 = (bf16[2,64,2048]{2,1,0:T(8,128)(2,1)S(1)}, bf16[2,64,2048]{2,1,0:T(8,128)(2,1)S(1)}, u32[]{:S(2)}, u32[]{:S(2)}) collective-permute-start(bf16[2,64,2048]{2,1,0:T(8,128)(2,1)S(1)} %get-tuple-element.77), channel_id=1, source_target_pairs={{16,24},{17,25},{18,26},{19,27},{20,28},{21,29},{22,30},{23,31},{2... | collective-permute-start | bytes 1572872 | tf_op jit(solution)/shard_map/ppermute | solution.py:27
  136.1 23.1 %collective-permute-start.25 = (bf16[2,64,2048]{2,1,0:T(8,128)(2,1)S(1)}, bf16[2,64,2048]{2,1,0:T(8,128)(2,1)S(1)}, u32[]{:S(2)}, u32[]{:S(2)}) collective-permute-start(bf16[2,64,2048]{2,1,0:T(8,128)(2,1)S(1)} %get-tuple-element.78), channel_id=1, source_target_pairs={{16,26},{17,27},{18,24},{19,25},{20,30},{21,31},{22,28},{23,29},{2... | collective-permute-start | bytes 1572872 | tf_op jit(solution)/shard_map/ppermute | solution.py:27
  142.9 18.7 %collective-permute-start.36 = (bf16[64,2048]{1,0:T(8,128)(2,1)S(1)}, bf16[64,2048]{1,0:T(8,128)(2,1)S(1)}, u32[]{:S(2)}, u32[]{:S(2)}) collective-permute-start(bf16[64,2048]{1,0:T(8,128)(2,1)S(1)} %get-tuple-element.86), channel_id=1, source_target_pairs={{16,17},{17,16},{18,19},{19,18},{20,21},{21,20},{22,23},{23,22},{2... | collective-permute-start | bytes 786440 | tf_op jit(solution)/shard_map/ppermute | solution.py:27
  146.3 16.7 %collective-permute-start.42 = (f32[1,64]{1,0:T(1,128)S(1)}, f32[1,64]{1,0:T(1,128)S(1)}, u32[]{:S(2)}, u32[]{:S(2)}) collective-permute-start(f32[1,64]{1,0:T(1,128)S(1)} %get-tuple-element.141), channel_id=1, source_target_pairs={{0,12},{1,13},{2,14},{3,15},{4,8},{5,9},{6,10},{7,11},{8,4},{9,5},... | collective-permute-start | bytes 776 | tf_op jit(solution)/shard_map/ppermute | solution.py:27
  147.0 19.0 %collective-permute-start.43 = (f32[1,64]{1,0:T(1,128)S(1)}, f32[1,64]{1,0:T(1,128)S(1)}, u32[]{:S(2)}, u32[]{:S(2)}) collective-permute-start(f32[1,64]{1,0:T(1,128)S(1)} %get-tuple-element.140), channel_id=1, source_target_pairs={{0,13},{1,12},{2,15},{3,14},{4,9},{5,8},{6,11},{7,10},{8,5},{9,4},... | collective-permute-start | bytes 776 | tf_op jit(solution)/shard_map/ppermute | solution.py:27
  153.6 13.7 %collective-permute-start.41 = (f32[2,64]{1,0:T(2,128)S(1)}, f32[2,64]{1,0:T(2,128)S(1)}, u32[]{:S(2)}, u32[]{:S(2)}) collective-permute-start(f32[2,64]{1,0:T(2,128)S(1)} %pad_maximum_fusion.5), channel_id=1, source_target_pairs={{0,8},{1,9},{2,10},{3,11},{4,12},{5,13},{6,14},{7,15},{8,0},{9,1},... | collective-permute-start | bytes 1544 | tf_op jit(solution)/shard_map/ppermute | solution.py:27
  160.3 32.5 %collective-permute-start.26 = (bf16[128,2048]{1,0:T(8,128)(2,1)S(1)}, bf16[128,2048]{1,0:T(8,128)(2,1)S(1)}, u32[]{:S(2)}, u32[]{:S(2)}) collective-permute-start(bf16[128,2048]{1,0:T(8,128)(2,1)S(1)} %get-tuple-element.79), channel_id=1, source_target_pairs={{16,0},{17,1},{18,2},{19,3},{20,4},{21,5},{22,6},{23,7},{24,8},{25... | collective-permute-start | bytes 1572872 | tf_op jit(solution)/shard_map/ppermute | solution.py:27
  161.6 31.1 %collective-permute-start.27 = (bf16[128,2048]{1,0:T(8,128)(2,1)S(1)}, bf16[128,2048]{1,0:T(8,128)(2,1)S(1)}, u32[]{:S(2)}, u32[]{:S(2)}) collective-permute-start(bf16[128,2048]{1,0:T(8,128)(2,1)S(1)} %get-tuple-element.80), channel_id=1, source_target_pairs={{16,1},{17,0},{18,3},{19,2},{20,5},{21,4},{22,7},{23,6},{24,9},{25... | collective-permute-start | bytes 1572872 | tf_op jit(solution)/shard_map/ppermute | solution.py:27
  163.0 5.6 %collective-permute-start.40 = (f32[2,64]{1,0:T(2,128)S(1)}, f32[2,64]{1,0:T(2,128)S(1)}, u32[]{:S(2)}, u32[]{:S(2)}) collective-permute-start(f32[2,64]{1,0:T(2,128)S(1)} %pad_maximum_fusion.4), channel_id=1, source_target_pairs={{0,4},{1,5},{2,6},{3,7},{4,0},{5,1},{6,2},{7,3},{8,12},{9,13},{10,... | collective-permute-start | bytes 1544 | tf_op jit(solution)/shard_map/ppermute | solution.py:27
  166.0 26.7 %collective-permute-start.33 = (bf16[64,2048]{1,0:T(8,128)(2,1)S(1)}, bf16[64,2048]{1,0:T(8,128)(2,1)S(1)}, u32[]{:S(2)}, u32[]{:S(2)}) collective-permute-start(bf16[64,2048]{1,0:T(8,128)(2,1)S(1)} %add_convert_fusion.1), channel_id=1, source_target_pairs={{16,12},{17,13},{18,14},{19,15},{20,8},{21,9},{22,10},{23,11},{24,... | collective-permute-start | bytes 786440 | tf_op jit(solution)/shard_map/ppermute | solution.py:27
  167.3 25.4 %collective-permute-start.37 = (bf16[64,2048]{1,0:T(8,128)(2,1)S(1)}, bf16[64,2048]{1,0:T(8,128)(2,1)S(1)}, u32[]{:S(2)}, u32[]{:S(2)}) collective-permute-start(bf16[64,2048]{1,0:T(8,128)(2,1)S(1)} %add_convert_fusion), channel_id=1, source_target_pairs={{16,14},{17,15},{18,12},{19,13},{20,10},{21,11},{22,8},{23,9},{24,... | collective-permute-start | bytes 786440 | tf_op jit(solution)/shard_map/ppermute | solution.py:27
  168.6 11.9 %collective-permute-start.44 = (f32[1,64]{1,0:T(1,128)S(1)}, f32[1,64]{1,0:T(1,128)S(1)}, u32[]{:S(2)}, u32[]{:S(2)}) collective-permute-start(f32[1,64]{1,0:T(1,128)S(1)} %get-tuple-element.139), channel_id=1, source_target_pairs={{0,14},{1,15},{2,12},{3,13},{4,10},{5,11},{6,8},{7,9},{8,6},{9,7},... | collective-permute-start | bytes 776 | tf_op jit(solution)/shard_map/ppermute | solution.py:27
  180.6 5.5 %collective-permute-start.45 = (f32[1,64]{1,0:T(1,128)S(1)}, f32[1,64]{1,0:T(1,128)S(1)}, u32[]{:S(2)}, u32[]{:S(2)}) collective-permute-start(f32[1,64]{1,0:T(1,128)S(1)} %get-tuple-element.138), channel_id=1, source_target_pairs={{0,15},{1,14},{2,13},{3,12},{4,11},{5,10},{6,9},{7,8},{8,7},{9,6},... | collective-permute-start | bytes 776 | tf_op jit(solution)/shard_map/ppermute | solution.py:27
  186.1 6.7 %collective-permute-start = (f32[4,128]{1,0:T(4,128)S(1)}, f32[4,128]{1,0:T(4,128)S(1)}, u32[]{:S(2)}, u32[]{:S(2)}) collective-permute-start(f32[4,128]{1,0:T(4,128)S(1)} %pad_maximum_fusion.2.code_ref.mine_ref), channel_id=1, source_target_pairs={{16,0},{17,1},{18,2},{19,3},{20,4},{21,5},{22,6},{23,7},{24,8},{25... | collective-permute-start | bytes 6152 | tf_op jit(solution)/shard_map/ppermute | solution.py:27
  (3 other events, 3.5 us)

commit v3 on v2

--- a/solution.py
+++ b/solution.py
@@ -13,6 +13,7 @@
 LINE = 4
 VMEM = pl.BlockSpec(memory_space=pltpu.VMEM)
 ANY = pl.BlockSpec(memory_space=pl.ANY)
+HBM = pl.BlockSpec(memory_space=pltpu.HBM)
 ROOM = pltpu.CompilerParams(vmem_limit_bytes=28 << 20)
 
 
@@ -35,6 +36,10 @@
     ring = experts // LINE
     head = [list(range(i, min(i + ring, experts - 2))) for i in range(0, experts - 2, ring)]
     return head + [[experts - 2], [experts - 1]]
+
+
+def outside(*arrays):
+    return [pltpu.with_memory_space_constraint(v, pltpu.HBM) for v in arrays]
 
 
 def kept(shape, kind):
@@ -87,19 +92,77 @@
     return pl.pallas_call(
         load_kernel,
         out_shape=[kept(v.shape, v.dtype) for v in arrays],
-        in_specs=[ANY] * len(arrays),
+        in_specs=[HBM] * len(arrays),
         out_specs=[VMEM] * len(arrays),
         scratch_shapes=[pltpu.SemaphoreType.DMA((len(arrays),))],
         name="load",
         compiler_params=ROOM,
-    )(*arrays)
-
-
-def select_kernel(sources, experts, cap, code_ref, *refs):
+    )(*outside(*arrays))
+
+
+def choose(x_ref, g_ref, code, home, ring, cap, out):
+    rows = code.shape[1]
+    pick, weight = picks(code, home, range(ring), cap)
+    rows_x = jnp.concatenate([jnp.where(p, 1.0, 0.0) for p in pick], axis=0).astype(HALF)
+    rows_g = jnp.concatenate([jnp.where(p, w, 0.0) for p, w in zip(pick, weight)], axis=0)
+    x = dot(rows_x, x_ref[:rows], 1, 0).astype(HALF)
+    g = dot(rows_g.astype(HALF), g_ref[...], 1, 0).astype(HALF)
+    for d in range(ring):
+        out[d][0] = x[d * cap : (d + 1) * cap]
+        out[d][1] = g[d * cap : (d + 1) * cap]
+
+
+def start_kernel(experts, cap, routes_ref, probs_ref, x_ref, g_ref, *refs):
+    own, code_ref, out, (routes, probs, g_held, sem) = refs[0], refs[1], refs[2:-4], refs[-4:]
+    (top, rows), width = routes_ref.shape, x_ref.shape[1]
+    copies = [
+        pltpu.make_async_copy(routes_ref, routes, sem.at[0]),
+        pltpu.make_async_copy(probs_ref, probs, sem.at[1]),
+        pltpu.make_async_copy(x_ref, own.at[pl.ds(0, rows)], sem.at[2]),
+        pltpu.make_async_copy(g_ref, g_held, sem.at[3]),
+    ]
+    for copy in copies:
+        copy.start()
+    home, _ = position(experts)
+    copies[0].wait()
+    copies[1].wait()
+    code = jnp.concatenate([routes[...].astype(FULL), probs[...].astype(FULL)], axis=0)
+    code_ref[...] = code
+    spare = own.shape[0] - rows
+    lead = jnp.concatenate([code, jnp.zeros((spare - 2 * top, rows), FULL)], axis=0)
+    own[rows:, :rows] = lead.astype(HALF)
+    own[rows:, rows:] = jnp.zeros((spare, width - rows), HALF)
+    copies[2].wait()
+    copies[3].wait()
+    choose(own, g_held, code, home, experts // LINE, cap, out)
+
+
+def start(routes, probs, x, g, experts, cap):
+    (top, rows), width = routes.shape, x.shape[1]
     ring = experts // LINE
+    out = pl.pallas_call(
+        functools.partial(start_kernel, experts, cap),
+        out_shape=[kept((rows + 16, width), HALF), kept((2 * top, rows), FULL)]
+        + [kept((2, cap, width), HALF)] * ring,
+        in_specs=[HBM] * 4,
+        out_specs=[VMEM] * (2 + ring),
+        scratch_shapes=[
+            pltpu.VMEM(routes.shape, routes.dtype),
+            pltpu.VMEM(probs.shape, probs.dtype),
+            pltpu.VMEM((rows, width), HALF),
+            pltpu.SemaphoreType.DMA((4,)),
+        ],
+        name="start",
+        compiler_params=ROOM,
+    )(*outside(routes, probs, x, g))
+    return out[0], out[1], out[2:]
+
+
+def select_kernel(sources, experts, cap, top, *refs):
+    from_x, from_g, out = refs[:sources], refs[sources : 2 * sources], refs[2 * sources : -3]
+    x_held, g_held, sem = refs[-3:]
     home, inner = position(experts)
-    from_x, from_g = refs[:sources], refs[sources : 2 * sources]
-    out, (x_held, g_held, sem) = refs[2 * sources : 2 * sources + ring], refs[-3:]
+    rows = g_held.shape[0]
 
     def fetch(i):
         pltpu.make_async_copy(from_x[i], x_held, sem.at[0]).start()
@@ -110,36 +173,52 @@
     else:
         pl.when(inner)(lambda: fetch(0))
         pl.when(jnp.logical_not(inner))(lambda: fetch(1))
-    pick, weight = picks(code_ref[...], home, range(ring), cap)
-    rows_x = jnp.concatenate([jnp.where(p, 1.0, 0.0) for p in pick], axis=0).astype(HALF)
-    rows_g = jnp.concatenate([jnp.where(p, w, 0.0) for p, w in zip(pick, weight)], axis=0)
     pltpu.make_async_copy(from_x[0], x_held, sem.at[0]).wait()
-    x = dot(rows_x, x_held[...], 1, 0).astype(HALF)
-    for d in range(ring):
-        out[d][0] = x[d * cap : (d + 1) * cap]
     pltpu.make_async_copy(from_g[0], g_held, sem.at[1]).wait()
-    g = dot(rows_g.astype(HALF), g_held[...], 1, 0).astype(HALF)
-    for d in range(ring):
-        out[d][1] = g[d * cap : (d + 1) * cap]
-
-
-def select(code, from_x, from_g, experts, cap):
-    rows, width = from_x[0].shape
+    code = x_held[rows:, :rows].astype(FULL)[: 2 * top]
+    choose(x_held, g_held, code, home, experts // LINE, cap, out)
+
+
+def select(from_x, from_g, experts, cap, top):
+    rows, width = from_g[0].shape
     ring = experts // LINE
     return pl.pallas_call(
-        functools.partial(select_kernel, len(from_x), experts, cap),
+        functools.partial(select_kernel, len(from_x), experts, cap, top),
         out_shape=[kept((2, cap, width), HALF)] * ring,
-        in_specs=[VMEM] + [ANY] * (2 * len(from_x)),
+        in_specs=[ANY] * (2 * len(from_x)),
         out_specs=[VMEM] * ring,
-        scratch_shapes=[pltpu.VMEM((rows, width), HALF)] * 2 + [pltpu.SemaphoreType.DMA((2,))],
+        scratch_shapes=[
+            pltpu.VMEM(from_x[0].shape, HALF),
+            pltpu.VMEM((rows, width), HALF),
+            pltpu.SemaphoreType.DMA((2,)),
+        ],
         name="select",
         compiler_params=ROOM,
-    )(code, *from_x, *from_g)
+    )(*from_x, *from_g)
+
+
+def merge_kernel(plan, *refs):
+    ins, outs = refs[: -len(plan)], refs[-len(plan) :]
+    for out, rows in zip(outs, plan):
+        for i, terms in enumerate(rows):
+            parts = [ins[k][r : r + 1] for k, r in terms]
+            out[i : i + 1] = functools.reduce(jnp.add, parts)
+
+
+def merge(plan, *arrays):
+    return pl.pallas_call(
+        functools.partial(merge_kernel, plan),
+        out_shape=[kept((len(rows), arrays[0].shape[1]), FULL) for rows in plan],
+        in_specs=[VMEM] * len(arrays),
+        out_specs=[VMEM] * len(plan),
+        name="merge",
+        compiler_params=ROOM,
+    )(*arrays)
 
 
 def phase_kernel(size, reduced, *refs):
     near, far, (wg, wu, wd) = refs[:size], refs[size : 2 * size], refs[2 * size : 2 * size + 3]
-    x_ref, g_ref, da_ref, db_ref, h_ref, rg_ref, *parts, sem = refs[2 * size + 3 :]
+    x_ref, g_ref, da_ref, db_ref, h_ref, rg_near, rg_far, *parts, sem = refs[2 * size + 3 :]
     cap = near[0].shape[1]
     for which, held in enumerate((x_ref, g_ref)):
         for i, ref in enumerate(near + far):
@@ -156,7 +235,8 @@
     da = (q * b * sig * (1.0 + a * (1.0 - sig))).astype(HALF)
     db = (q * act).astype(HALF)
     h_ref[...], da_ref[...], db_ref[...] = h, da, db
-    rg_ref[...] = jnp.sum((q * h.astype(FULL)).reshape(2 * size, cap, -1), axis=2)
+    rg = jnp.sum((q * h.astype(FULL)).reshape(2 * size, cap, -1), axis=2)
+    rg_near[...], rg_far[...] = rg[:size], rg[size:]
     part = dot(da, wg[...], 1, 1) + dot(db, wu[...], 1, 1)
     for i in range(size):
         for side in range(2):
@@ -180,15 +260,15 @@
         functools.partial(phase_kernel, size, reduced),
         out_shape=[kept((rows, width), HALF)] * 2
         + [kept((rows, hidden), HALF)] * 3
-        + [kept((2 * size, cap), FULL)]
+        + [kept((size, cap), FULL)] * 2
         + parts,
         in_specs=[ANY] * (2 * size) + [VMEM] * 3,
-        out_specs=[VMEM] * (6 + len(parts)),
+        out_specs=[VMEM] * (7 + len(parts)),
         scratch_shapes=[pltpu.SemaphoreType.DMA((2,))],
         name="phase",
         compiler_params=ROOM,
     )(*near, *far, wg, wu, wd)
-    return out[:5], out[5], out[6:]
+    return out[:5], out[5:7], out[7:]
 
 
 def grads_kernel(count, begun, last, tile, *refs):
@@ -223,6 +303,7 @@
         out_shape=out_shape,
         in_specs=[VMEM] * (5 * len(chunks) + len(olds)),
         out_specs=out_specs,
+        input_output_aliases={} if last else {5 * len(chunks) + i: i for i in range(len(olds))},
         name="grads",
         compiler_params=ROOM,
     )(*[c[i] for i in range(5) for c in chunks], *olds)
@@ -273,23 +354,20 @@
     )(code, near, far, *got)
 
 
-def route_kernel(experts, code_ref, slots_ref, *refs):
-    ends, out = refs[:-1], refs[-1]
+def route_kernel(experts, code_ref, slots_ref, out):
     home, _ = position(experts)
     code = code_ref[...]
     top, cap = code.shape[0] // 2, slots_ref.shape[1]
     pick, _ = picks(code, home, range(experts), cap)
-    values = [slots_ref[o : o + 1] for o in range(slots_ref.shape[0])]
-    values += [ends[i][...] + ends[i + 1][...] for i in range(0, len(ends), 2)]
     named = [
         lax.dot_general(
-            jnp.broadcast_to(v, (8, cap)),
+            jnp.broadcast_to(slots_ref[o : o + 1], (8, cap)),
             jnp.where(p, 1.0, 0.0),
             (((1,), (0,)), ((), ())),
             precision=lax.Precision.HIGHEST,
             preferred_element_type=FULL,
         )[:1]
-        for p, v in zip(pick, values)
+        for o, p in enumerate(pick)
     ]
     for k in range(top):
         near = code[k : k + 1].astype(jnp.int32) ^ home
@@ -298,15 +376,15 @@
         out[k : k + 1] = total.astype(HALF)
 
 
-def route(code, slots, ends, experts):
+def route(code, slots, experts):
     return pl.pallas_call(
         functools.partial(route_kernel, experts),
         out_shape=jax.ShapeDtypeStruct((code.shape[0] // 2, code.shape[1]), HALF),
-        in_specs=[VMEM] * (2 + len(ends)),
+        in_specs=[VMEM] * 2,
         out_specs=VMEM,
         name="route",
         compiler_params=ROOM,
-    )(code, slots, *ends)
+    )(code, slots)
 
 
 def body(tokens, routes, probs, cotangent, w_gate, w_up, w_down):
@@ -325,22 +403,23 @@
 
         return moved(value, target)
 
-    code = jnp.concatenate([routes[0].astype(FULL).T, probs[0].astype(FULL).T], axis=0)
+    own, code, first = start(
+        routes[0].T, probs[0].T, tokens[0], cotangent[0], experts, cap
+    )
     sides = []
-    for own in (tokens[0], cotangent[0]):
-        side1 = along(own, {0: 1, 1: 0, 2: 3, 3: 2})
-        side2 = along(own, {1: 2, 2: 1})
+    for mine in (own, cotangent[0]):
+        side1 = along(mine, {0: 1, 1: 0, 2: 3, 3: 2})
+        side2 = along(mine, {1: 2, 2: 1})
         side3 = along(side1, {1: 2, 2: 1})
         side4 = along(side2, {1: 0, 2: 3})
         side5 = along(side3, {1: 0, 2: 3})
-        sides.append([[own], [side1], [side3, side4], [side2, side5]])
-    codes = [code] + [shifted(code, 2 * ring * j) for j in range(1, LINE)]
+        sides.append([[mine], [side1], [side3, side4], [side2, side5]])
     mirror = shifted(code, 1, 1)
     lower = shifted(code, 0, 1, 1)
 
     near, far = {}, {}
     for j in range(LINE):
-        picked = select(codes[j], sides[0][j], sides[1][j], experts, cap)
+        picked = select(sides[0][j], sides[1][j], experts, cap, top) if j else first
         for d, block in enumerate(picked):
             o = j * ring + d
             near[o] = block if d == 0 else shifted(block, 2 * d)
@@ -348,14 +427,15 @@
 
     groups = groups_of(experts)
     last = list(range(experts - 2, experts))
-    chunks, near_rg, far_rg, got = [], {}, {}, {}
-    for group in groups:
+    chunks, rgs, near_rg, far_rg, got = [], [], {}, {}, {}
+    for number, group in enumerate(groups):
         near_group, far_group = [near[o] for o in group], [far[o] for o in group]
         reduced = group[0] in last
         chunk, rg, parts = phase(near_group, far_group, wg, wu, wd, reduced)
         chunks.append(chunk)
+        rgs += rg
         for i, o in enumerate(group):
-            near_rg[o], far_rg[o] = rg[i], rg[len(group) + i]
+            near_rg[o], far_rg[o] = (2 * number, i), (2 * number + 1, i)
             if reduced:
                 partner = shifted(parts[1], 1, 1)
                 total = (parts[0] + partner.astype(FULL)).astype(HALF)
@@ -364,23 +444,25 @@
                 got[o] = parts[i] if o == 0 else shifted(parts[i], 2 * o, 1)
 
     begun = grads(chunks[:2], last=False)
-    g_gate, g_up, g_down = grads(chunks[2:], begun)
-
-    early = [o for o in range(experts) if o not in last]
-    slots = jnp.stack([near_rg[o] for o in early])
-    slots += shifted(jnp.stack([far_rg[o] for o in early]), 1)
-    for bit in range(experts.bit_length() - 1):
-        high = [o for o in early if o >> bit & 1]
-        taken = shifted(jnp.stack([slots[o] for o in high]), 2 << bit)
-        slots = jnp.stack([taken[high.index(o)] if o in high else slots[o] for o in early])
-    ends = [
-        shifted(rg[None], 2 * o + side)
-        for o in last
-        for side, rg in enumerate((near_rg[o], far_rg[o]))
-    ]
-    route_grad = route(code, slots, ends, experts).T
-
-    dx_near, dx_far = combine(code, mirror, [got[o] for o in early], experts)
+    begun = grads(chunks[2:-1], begun, last=False)
+    g_gate, g_up, g_down = grads(chunks[-1:], begun, tile=1024)
+
+    every = range(experts)
+    plan = [[[part[o]] for o in every] for part in (near_rg, far_rg)]
+    slots, sent = merge(plan, *rgs)
+    rows_in = [[(0, o), (1, o)] for o in every]
+    for bit in range(experts.bit_length()):
+        taken = shifted(sent, 1 << bit)
+        high = [o for o in every if o >> bit & 1]
+        more = bit + 1 < experts.bit_length()
+        slots, *sent = merge(
+            [rows_in] + ([[rows_in[o] for o in high]] if more else []), slots, taken
+        )
+        sent = sent[0] if more else None
+        rows_in = [[(1, high.index(o))] if o in high else [(0, o)] for o in every]
+    route_grad = route(code, slots, experts).T
+
+    dx_near, dx_far = combine(code, mirror, [got[o] for o in range(experts - 2)], experts)
     below = shifted(dx_near, 0, 1, 1)
     across = shifted(dx_far, 1, 1, 1)
     upstream = final(lower, below, across, last, [got[o] for o in last], experts)

time: 195 us -> 222 us (1.14)
  the two profiles are of different devices: /device:TPU:9 before, /device:TPU:1 now
where the time goes in v3:
time: 222 us
  waiting for transfers between devices  135 us (61%)
  starting transfers between devices  51.1 us (23%)
  Pallas kernels  34.8 us (16%)
    ppermute x39, waiting for transfers between devices, moved(): return lax.ppermute(value, AXES, pairs)  135 us
    ppermute x39, starting transfers between devices, moved(): return lax.ppermute(value, AXES, pairs)  51.1 us
    pallas_call x5, Pallas kernels, phase(): pl.pallas_call(functools.partial(phase_kernel, size, reduced), out_shape=...  15.5 us
    pallas_call x3, Pallas kernels, grads(): pl.pallas_call(functools.partial(grads_kernel, len(chunks), bool(olds), l...  9.63 us
  transfers between devices with their start and end apart: 39, of which 18 were waited for; matrix products, arithmetic and copies ran while one was open for 0% of the time, Pallas kernels for 14%

profile of v3, /device:TPU:1, one launch (start us, length us, event | category | flops | bytes accessed | tf_op | source)
XLA Modules:
  0.0 221.7 jit_solution(8336859349614535075)
XLA Ops:
  0.6 1.8 start.1
  2.5 2.2 collective-permute-start.6
  6.1 11.6 %collective-permute-done.6.refs_0_ = bf16[144,2048]{1,0:T(8,128)(2,1)S(1)} collective-permute-done((bf16[144,2048]{1,0:T(8,128)(2,1)S(1)}, bf16[144,2048]{1,0:T(8,128)(2,1)S(1)}, u32[]{:S(2)}, u32[]{:S(2)}) %collective-permute-start.6) | collective-permute-done | bytes 589856 | tf_op jit(solution)/shard_map/ppermute | solution.py:28
  18.4 10.5 %collective-permute-done.7.refs_1_ = bf16[128,2048]{1,0:T(8,128)(2,1)S(1)} collective-permute-done((bf16[128,2048]{1,0:T(8,128)(2,1)}, bf16[128,2048]{1,0:T(8,128)(2,1)S(1)}, u32[]{:S(2)}, u32[]{:S(2)}) %collective-permute-start.7) | collective-permute-done | bytes 524320 | tf_op jit(solution)/shard_map/ppermute | solution.py:28
  30.8 1.3 collective-permute-start.18
  32.1 1.3 collective-permute-start.15
  33.4 1.3 collective-permute-start.26
  34.7 1.3 collective-permute-start.27
  36.0 5.9 %collective-permute-done.2.refs_1_ = bf16[2,64,2048]{2,1,0:T(8,128)(2,1)S(1)} collective-permute-done((bf16[2,64,2048]{2,1,0:T(8,128)(2,1)S(1)}, bf16[2,64,2048]{2,1,0:T(8,128)(2,1)S(1)}, u32[]{:S(2)}, u32[]{:S(2)}) %collective-permute-start.2) | collective-permute-done | bytes 524320 | tf_op jit(solution)/shard_map/ppermute | solution.py:28
  42.7 3.4 %collective-permute-done.18.refs_3_ = bf16[128,2048]{1,0:T(8,128)(2,1)S(1)} collective-permute-done((bf16[128,2048]{1,0:T(8,128)(2,1)S(1)}, bf16[128,2048]{1,0:T(8,128)(2,1)S(1)}, u32[]{:S(2)}, u32[]{:S(2)}) %collective-permute-start.18) | collective-permute-done | bytes 524320 | tf_op jit(solution)/shard_map/ppermute | solution.py:28
  48.0 10.7 %collective-permute-done.15.refs_1_ = bf16[144,2048]{1,0:T(8,128)(2,1)S(1)} collective-permute-done((bf16[144,2048]{1,0:T(8,128)(2,1)S(1)}, bf16[144,2048]{1,0:T(8,128)(2,1)S(1)}, u32[]{:S(2)}, u32[]{:S(2)}) %collective-permute-start.15) | collective-permute-done | bytes 589856 | tf_op jit(solution)/shard_map/ppermute | solution.py:28
  58.9 23.6 %collective-permute-done.27.refs_3_ = bf16[128,2048]{1,0:T(8,128)(2,1)S(1)} collective-permute-done((bf16[128,2048]{1,0:T(8,128)(2,1)S(1)}, bf16[128,2048]{1,0:T(8,128)(2,1)S(1)}, u32[]{:S(2)}, u32[]{:S(2)}) %collective-permute-start.27) | collective-permute-done | bytes 524320 | tf_op jit(solution)/shard_map/ppermute | solution.py:28
  85.5 1.3 collective-permute-start.31
  88.3 5.1 %collective-permute-done.9.refs_2_ = bf16[2,64,2048]{2,1,0:T(8,128)(2,1)S(1)} collective-permute-done((bf16[2,64,2048]{2,1,0:T(8,128)(2,1)S(1)}, bf16[2,64,2048]{2,1,0:T(8,128)(2,1)S(1)}, u32[]{:S(2)}, u32[]{:S(2)}) %collective-permute-start.9) | collective-permute-done | bytes 524320 | tf_op jit(solution)/shard_map/ppermute | solution.py:28
  94.6 2.4 %load.1 = (bf16[2048,384]{1,0:T(8,128)(2,1)S(1)}, bf16[2048,384]{1,0:T(8,128)(2,1)S(1)}, bf16[384,2048]{1,0:T(8,128)(2,1)S(1)}) custom-call(bf16[2048,384]{1,0:T(8,128)(2,1)} %bitcast.17, bf16[2048,384]{1,0:T(8,128)(2,1)} %bitcast.18, bf16[384,2048]{1,0:T(8,128)(2,1)} %bitcast.19), custom_call_target="tpu_custom_call" | custom-call | tf_op jit(solution)/shard_map/load/pallas_call | solution.py:92
  97.3 3.4 %phase.5 = (bf16[256,2048]{1,0:T(8,128)(2,1)S(1)}, bf16[256,2048]{1,0:T(8,128)(2,1)S(1)}, bf16[256,384]{1,0:T(8,128)(2,1)S(1)}, bf16[256,384]{1,0:T(8,128)(2,1)S...) custom-call(bf16[2,64,2048]{2,1,0:T(8,128)(2,1)S(1)} %get-tuple-elem, ...), custom_call_target="tpu_custom_call" | custom-call | tf_op jit(solution)/shard_map/phase/pallas_call | solution.py:259
  100.8 5.6 %collective-permute-done.31.refs_0_ = bf16[2,64,2048]{2,1,0:T(8,128)(2,1)S(1)} collective-permute-done((bf16[2,64,2048]{2,1,0:T(8,128)(2,1)S(1)}, bf16[2,64,2048]{2,1,0:T(8,128)(2,1)S(1)}, u32[]{:S(2)}, u32[]{:S(2)}) %collective-permute-start.31) | collective-permute-done | bytes 524320 | tf_op jit(solution)/shard_map/ppermute | solution.py:28
  106.4 2.1 collective-permute-start.5
  108.8 2.5 %phase.8 = (bf16[128,2048]{1,0:T(8,128)(2,1)S(1)}, bf16[128,2048]{1,0:T(8,128)(2,1)S(1)}, bf16[128,384]{1,0:T(8,128)(2,1)S(1)}, bf16[128,384]{1,0:T(8,128)(2,1)S...) custom-call(bf16[2,64,2048]{2,1,0:T(8,128)(2,1)S(1)} %get-tuple-elem, ...), custom_call_target="tpu_custom_call" | custom-call | tf_op jit(solution)/shard_map/phase/pallas_call | solution.py:259
  111.4 4.5 %collective-permute-done.10.refs_3_ = bf16[2,64,2048]{2,1,0:T(8,128)(2,1)S(1)} collective-permute-done((bf16[2,64,2048]{2,1,0:T(8,128)(2,1)S(1)}, bf16[2,64,2048]{2,1,0:T(8,128)(2,1)S(1)}, u32[]{:S(2)}, u32[]{:S(2)}) %collective-permute-start.10) | collective-permute-done | bytes 524320 | tf_op jit(solution)/shard_map/ppermute | solution.py:28
  115.9 3.1 %collective-permute-start.29 = (bf16[64,2048]{1,0:T(8,128)(2,1)S(1)}, bf16[64,2048]{1,0:T(8,128)(2,1)S(1)}, u32[]{:S(2)}, u32[]{:S(2)}) collective-permute-start(bf16[64,2048]{1,0:T(8,128)(2,1)S(1)} %get-tuple-element.103), channel_id=1, source_target_pairs={{16,17},{17,16},{18,19},{19,18},{20,21},{21,20},{22,23},{23,22},{2... | collective-permute-start | bytes 786440 | tf_op jit(solution)/shard_map/ppermute | solution.py:28
  119.0 8.1 %collective-permute-done.20.refs_2_ = bf16[2,64,2048]{2,1,0:T(8,128)(2,1)S(1)} collective-permute-done((bf16[2,64,2048]{2,1,0:T(8,128)(2,1)S(1)}, bf16[2,64,2048]{2,1,0:T(8,128)(2,1)S(1)}, u32[]{:S(2)}, u32[]{:S(2)}) %collective-permute-start.20) | collective-permute-done | bytes 524320 | tf_op jit(solution)/shard_map/ppermute | solution.py:28
  127.1 3.3 %collective-permute-start.1 = (f32[4,128]{1,0:T(4,128)S(1)}, f32[4,128]{1,0:T(4,128)S(1)}, u32[]{:S(2)}, u32[]{:S(2)}) collective-permute-start(f32[4,128]{1,0:T(4,128)S(1)} %get-tuple-element.82.mine_ref.code_ref), channel_id=1, source_target_pairs={{16,17},{17,16},{18,19},{19,18},{20,21},{21,20},{22,23},{23,22},{2... | collective-permute-start | bytes 6152 | tf_op jit(solution)/shard_map/ppermute | solution.py:28
  130.4 3.5 %phase.6 = (bf16[256,2048]{1,0:T(8,128)(2,1)S(1)}, bf16[256,2048]{1,0:T(8,128)(2,1)S(1)}, bf16[256,384]{1,0:T(8,128)(2,1)S(1)}, bf16[256,384]{1,0:T(8,128)(2,1)S...) custom-call(bf16[2,64,2048]{2,1,0:T(8,128)(2,1)S(1)} %get-tuple-elem, ...), custom_call_target="tpu_custom_call" | custom-call | tf_op jit(solution)/shard_map/phase/pallas_call | solution.py:259
  133.9 4.5 %collective-permute-done.21.refs_3_ = bf16[2,64,2048]{2,1,0:T(8,128)(2,1)S(1)} collective-permute-done((bf16[2,64,2048]{2,1,0:T(8,128)(2,1)S(1)}, bf16[2,64,2048]{2,1,0:T(8,128)(2,1)S(1)}, u32[]{:S(2)}, u32[]{:S(2)}) %collective-permute-start.21) | collective-permute-done | bytes 524320 | tf_op jit(solution)/shard_map/ppermute | solution.py:28
  138.3 1.9 collective-permute-start.11
  140.3 3.5 %phase.7 = (bf16[256,2048]{1,0:T(8,128)(2,1)S(1)}, bf16[256,2048]{1,0:T(8,128)(2,1)S(1)}, bf16[256,384]{1,0:T(8,128)(2,1)S(1)}, bf16[256,384]{1,0:T(8,128)(2,1)S...) custom-call(bf16[2,64,2048]{2,1,0:T(8,128)(2,1)S(1)} %get-tuple-elem, ...), custom_call_target="tpu_custom_call" | custom-call | tf_op jit(solution)/shard_map/phase/pallas_call | solution.py:259
  143.7 11.5 %collective-permute-done.1.other_ref = f32[4,128]{1,0:T(4,128)S(1)} collective-permute-done((f32[4,128]{1,0:T(4,128)S(1)}, f32[4,128]{1,0:T(4,128)S(1)}, u32[]{:S(2)}, u32[]{:S(2)}) %collective-permute-start.1) | collective-permute-done | bytes 2080 | tf_op jit(solution)/shard_map/ppermute | solution.py:28
  155.2 1.9 collective-permute-start.12
  157.2 3.7 %collective-permute-start.22 = (bf16[2,64,2048]{2,1,0:T(8,128)(2,1)S(1)}, bf16[2,64,2048]{2,1,0:T(8,128)(2,1)S(1)}, u32[]{:S(2)}, u32[]{:S(2)}) collective-permute-start(bf16[2,64,2048]{2,1,0:T(8,128)(2,1)S(1)} %get-tuple-element.97), channel_id=1, source_target_pairs={{16,24},{17,25},{18,26},{19,27},{20,28},{21,29},{22,30},{23,31},{2... | collective-permute-start | bytes 1572872 | tf_op jit(solution)/shard_map/ppermute | solution.py:28
  160.9 2.9 %collective-permute-start.23 = (bf16[2,64,2048]{2,1,0:T(8,128)(2,1)S(1)}, bf16[2,64,2048]{2,1,0:T(8,128)(2,1)S(1)}, u32[]{:S(2)}, u32[]{:S(2)}) collective-permute-start(bf16[2,64,2048]{2,1,0:T(8,128)(2,1)S(1)} %get-tuple-element.98), channel_id=1, source_target_pairs={{16,26},{17,27},{18,24},{19,25},{20,30},{21,31},{22,28},{23,29},{2... | collective-permute-start | bytes 1572872 | tf_op jit(solution)/shard_map/ppermute | solution.py:28
  163.8 2.6 %phase.9 = (bf16[128,2048]{1,0:T(8,128)(2,1)S(1)}, bf16[128,2048]{1,0:T(8,128)(2,1)S(1)}, bf16[128,384]{1,0:T(8,128)(2,1)S(1)}, bf16[128,384]{1,0:T(8,128)(2,1)S...) custom-call(bf16[2,64,2048]{2,1,0:T(8,128)(2,1)S(1)} %collective-per, ...), custom_call_target="tpu_custom_call" | custom-call | tf_op jit(solution)/shard_map/phase/pallas_call | solution.py:259
  166.4 3.1 %collective-permute-start.33 = (bf16[64,2048]{1,0:T(8,128)(2,1)S(1)}, bf16[64,2048]{1,0:T(8,128)(2,1)S(1)}, u32[]{:S(2)}, u32[]{:S(2)}) collective-permute-start(bf16[64,2048]{1,0:T(8,128)(2,1)S(1)} %get-tuple-element.106), channel_id=1, source_target_pairs={{16,17},{17,16},{18,19},{19,18},{20,21},{21,20},{22,23},{23,22},{2... | collective-permute-start | bytes 786440 | tf_op jit(solution)/shard_map/ppermute | solution.py:28
  169.5 1.3 collective-permute-start.30
  170.9 11.3 %collective-permute-done.22.refs_4_ = bf16[2,64,2048]{2,1,0:T(8,128)(2,1)S(1)} collective-permute-done((bf16[2,64,2048]{2,1,0:T(8,128)(2,1)S(1)}, bf16[2,64,2048]{2,1,0:T(8,128)(2,1)S(1)}, u32[]{:S(2)}, u32[]{:S(2)}) %collective-permute-start.22) | collective-permute-done | bytes 524320 | tf_op jit(solution)/shard_map/ppermute | solution.py:28
  182.1 6.0 %collective-permute-done.23.refs_5_ = bf16[2,64,2048]{2,1,0:T(8,128)(2,1)S(1)} collective-permute-done((bf16[2,64,2048]{2,1,0:T(8,128)(2,1)S(1)}, bf16[2,64,2048]{2,1,0:T(8,128)(2,1)S(1)}, u32[]{:S(2)}, u32[]{:S(2)}) %collective-permute-start.23) | collective-permute-done | bytes 524320 | tf_op jit(solution)/shard_map/ppermute | solution.py:28
  189.2 1.3 collective-permute-start.24
  190.6 1.3 collective-permute-start.25
  192.0 1.3 collective-permute-start.34
  193.3 1.3 collective-permute-start.35
  194.6 5.3 %collective-permute-done.35.refs_1_ = f32[8,64]{1,0:T(8,128)S(1)} collective-permute-done((f32[8,64]{1,0:T(8,128)S(1)}, f32[8,64]{1,0:T(8,128)S(1)}, u32[]{:S(2)}, u32[]{:S(2)}) %collective-permute-start.35) | collective-permute-done | bytes 2080 | tf_op jit(solution)/shard_map/ppermute | solution.py:28
  200.8 1.7 collective-permute-done.36.refs_1_
  202.4 2.4 %collective-permute-done.37.refs_1_ = f32[4,64]{1,0:T(4,128)S(1)} collective-permute-done((f32[4,64]{1,0:T(4,128)S(1)}, f32[4,64]{1,0:T(4,128)S(1)}, u32[]{:S(2)}, u32[]{:S(2)}) %collective-permute-start.37) | collective-permute-done | bytes 1056 | tf_op jit(solution)/shard_map/ppermute | solution.py:28
  205.4 2.8 %collective-permute-done.38.refs_1_ = f32[4,64]{1,0:T(4,128)S(1)} collective-permute-done((f32[4,64]{1,0:T(4,128)S(1)}, f32[4,64]{1,0:T(4,128)S(1)}, u32[]{:S(2)}, u32[]{:S(2)}) %collective-permute-start.38) | collective-permute-done | bytes 1056 | tf_op jit(solution)/shard_map/ppermute | solution.py:28
  208.2 1.5 collective-permute-start
  209.7 3.3 %grads.3 = (f32[384,2048]{1,0:T(8,128)S(1)}, f32[384,2048]{1,0:T(8,128)S(1)}, f32[384,2048]{1,0:T(8,128)S(1)}) custom-call(bf16[256,2048]{1,0:T(8,128)(2,1)S(1)} %get-tuple-element.140.refs_0_, bf16[256,2048]{1,0:T(8,128)(2,1)S(1)} %get-tuple-element.141.refs_1_, bf16[256,2048]{1,0:T(8,128)(2,1)S(1)} %get-tuple-element.142.refs_2_, ...), custom_call_target="tpu_custom_call" | custom-call | tf_op jit(solution)/shard_map/grads/pallas_call | solution.py:300
  213.0 3.5 %grads.4 = (f32[384,2048]{1,0:T(8,128)S(1)}, f32[384,2048]{1,0:T(8,128)S(1)}, f32[384,2048]{1,0:T(8,128)S(1)}) custom-call(bf16[256,2048]{1,0:T(8,128)(2,1)S(1)} %get-tuple-element.130.refs_0_, bf16[128,2048]{1,0:T(8,128)(2,1)S(1)} %get-tuple-element.131.refs_1_, ...), custom_call_target="tpu_custom_call", output_to_operand_aliasing={{0}: (10, {}), {1}: (11, {}), {2}: (12, {})} | custom-call | tf_op jit(solution)/shard_map/grads/pallas_call | solution.py:300
  216.5 2.8 %grads.5 = (bf16[2048,384]{1,0:T(8,128)(2,1)}, bf16[2048,384]{1,0:T(8,128)(2,1)}, bf16[384,2048]{1,0:T(8,128)(2,1)}) custom-call(bf16[128,2048]{1,0:T(8,128)(2,1)S(1)} %get-tuple-element.125.refs_0_, bf16[128,2048]{1,0:T(8,128)(2,1)S(1)} %get-tuple-element.126.refs_1_, bf16[128,384]{1,0:T(8,128)(2,1)S(1)} %get-tuple-element.127.refs_2_, ...), custom_call_target="tpu_custom_call" | custom-call | tf_op jit(solution)/shard_map/grads/pallas_call | solution.py:300
  (53 shorter events, 18.1 us)
Async XLA Ops:
  2.5 15.2 %collective-permute-start.6 = (bf16[144,2048]{1,0:T(8,128)(2,1)S(1)}, bf16[144,2048]{1,0:T(8,128)(2,1)S(1)}, u32[]{:S(2)}, u32[]{:S(2)}) collective-permute-start(bf16[144,2048]{1,0:T(8,128)(2,1)S(1)} %get-tuple-element.90), channel_id=1, source_target_pairs={{0,4},{1,5},{2,6},{3,7},{4,0},{5,1},{6,2},{7,3},{8,12},{9,13},{10,... | collective-permute-start | bytes 1769480 | tf_op jit(solution)/shard_map/ppermute | solution.py:28
  4.6 24.3 %collective-permute-start.7 = (bf16[128,2048]{1,0:T(8,128)(2,1)}, bf16[128,2048]{1,0:T(8,128)(2,1)S(1)}, u32[]{:S(2)}, u32[]{:S(2)}) collective-permute-start(bf16[128,2048]{1,0:T(8,128)(2,1)} %bitcast.22), channel_id=1, source_target_pairs={{0,4},{1,5},{2,6},{3,7},{4,0},{5,1},{6,2},{7,3},{8,12},{9,13},{10,... | collective-permute-start | bytes 1572872 | tf_op jit(solution)/shard_map/ppermute | solution.py:28
  4.7 26.1 %collective-permute-start.17 = (bf16[128,2048]{1,0:T(8,128)(2,1)}, bf16[128,2048]{1,0:T(8,128)(2,1)S(1)}, u32[]{:S(2)}, u32[]{:S(2)}) collective-permute-start(bf16[128,2048]{1,0:T(8,128)(2,1)} %bitcast.23), channel_id=1, source_target_pairs={{4,8},{5,9},{6,10},{7,11},{8,4},{9,5},{10,6},{11,7},{20,24},{21,25... | collective-permute-start | bytes 1572872 | tf_op jit(solution)/shard_map/ppermute | solution.py:28
  5.4 26.7 %collective-permute-start.14 = (bf16[144,2048]{1,0:T(8,128)(2,1)S(1)}, bf16[144,2048]{1,0:T(8,128)(2,1)S(1)}, u32[]{:S(2)}, u32[]{:S(2)}) collective-permute-start(bf16[144,2048]{1,0:T(8,128)(2,1)S(1)} %get-tuple-element.90), channel_id=1, source_target_pairs={{4,8},{5,9},{6,10},{7,11},{8,4},{9,5},{10,6},{11,7},{20,24},{21,25... | collective-permute-start | bytes 1769480 | tf_op jit(solution)/shard_map/ppermute | solution.py:28
  17.7 15.7 %collective-permute-start.13 = (bf16[144,2048]{1,0:T(8,128)(2,1)S(1)}, bf16[144,2048]{1,0:T(8,128)(2,1)S(1)}, u32[]{:S(2)}, u32[]{:S(2)}) collective-permute-start(bf16[144,2048]{1,0:T(8,128)(2,1)S(1)} %collective-permute-done.6.refs_0_), channel_id=1, source_target_pairs={{4,8},{5,9},{6,10},{7,11},{8,4},{9,5},{10,6},{11,7},{20,24},{21,25... | collective-permute-start | bytes 1769480 | tf_op jit(solution)/shard_map/ppermute | solution.py:28
  28.9 5.8 %collective-permute-start.16 = (bf16[128,2048]{1,0:T(8,128)(2,1)S(1)}, bf16[128,2048]{1,0:T(8,128)(2,1)S(1)}, u32[]{:S(2)}, u32[]{:S(2)}) collective-permute-start(bf16[128,2048]{1,0:T(8,128)(2,1)S(1)} %collective-permute-done.7.refs_1_), channel_id=1, source_target_pairs={{4,8},{5,9},{6,10},{7,11},{8,4},{9,5},{10,6},{11,7},{20,24},{21,25... | collective-permute-start | bytes 1572872 | tf_op jit(solution)/shard_map/ppermute | solution.py:28
  29.6 12.3 %collective-permute-start.2 = (bf16[2,64,2048]{2,1,0:T(8,128)(2,1)S(1)}, bf16[2,64,2048]{2,1,0:T(8,128)(2,1)S(1)}, u32[]{:S(2)}, u32[]{:S(2)}) collective-permute-start(bf16[2,64,2048]{2,1,0:T(8,128)(2,1)S(1)} %get-tuple-element.84), channel_id=1, source_target_pairs={{0,2},{1,3},{2,0},{3,1},{4,6},{5,7},{6,4},{7,5},{8,10},{9,11},{10,... | collective-permute-start | bytes 1572872 | tf_op jit(solution)/shard_map/ppermute | solution.py:28
  30.8 15.3 %collective-permute-start.18 = (bf16[128,2048]{1,0:T(8,128)(2,1)S(1)}, bf16[128,2048]{1,0:T(8,128)(2,1)S(1)}, u32[]{:S(2)}, u32[]{:S(2)}) collective-permute-start(bf16[128,2048]{1,0:T(8,128)(2,1)S(1)} %collective-permute-done.17.refs_2_), channel_id=1, source_target_pairs={{4,0},{5,1},{6,2},{7,3},{8,12},{9,13},{10,14},{11,15},{20,16},{21,... | collective-permute-start | bytes 1572872 | tf_op jit(solution)/shard_map/ppermute | solution.py:28
  32.1 26.6 %collective-permute-start.15 = (bf16[144,2048]{1,0:T(8,128)(2,1)S(1)}, bf16[144,2048]{1,0:T(8,128)(2,1)S(1)}, u32[]{:S(2)}, u32[]{:S(2)}) collective-permute-start(bf16[144,2048]{1,0:T(8,128)(2,1)S(1)} %collective-permute-done.14.refs_0_), channel_id=1, source_target_pairs={{4,0},{5,1},{6,2},{7,3},{8,12},{9,13},{10,14},{11,15},{20,16},{21,... | collective-permute-start | bytes 1769480 | tf_op jit(solution)/shard_map/ppermute | solution.py:28
  33.4 51.1 %collective-permute-start.26 = (bf16[144,2048]{1,0:T(8,128)(2,1)S(1)}, bf16[144,2048]{1,0:T(8,128)(2,1)S(1)}, u32[]{:S(2)}, u32[]{:S(2)}) collective-permute-start(bf16[144,2048]{1,0:T(8,128)(2,1)S(1)} %collective-permute-done.13.refs_0_), channel_id=1, source_target_pairs={{4,0},{5,1},{6,2},{7,3},{8,12},{9,13},{10,14},{11,15},{20,16},{21,... | collective-permute-start | bytes 1769480 | tf_op jit(solution)/shard_map/ppermute | solution.py:28
  34.7 47.9 %collective-permute-start.27 = (bf16[128,2048]{1,0:T(8,128)(2,1)S(1)}, bf16[128,2048]{1,0:T(8,128)(2,1)S(1)}, u32[]{:S(2)}, u32[]{:S(2)}) collective-permute-start(bf16[128,2048]{1,0:T(8,128)(2,1)S(1)} %collective-permute-done.16.refs_2_), channel_id=1, source_target_pairs={{4,0},{5,1},{6,2},{7,3},{8,12},{9,13},{10,14},{11,15},{20,16},{21,... | collective-permute-start | bytes 1572872 | tf_op jit(solution)/shard_map/ppermute | solution.py:28
  41.9 43.7 %collective-permute-start.3 = (bf16[2,64,2048]{2,1,0:T(8,128)(2,1)S(1)}, bf16[2,64,2048]{2,1,0:T(8,128)(2,1)S(1)}, u32[]{:S(2)}, u32[]{:S(2)}) collective-permute-start(bf16[2,64,2048]{2,1,0:T(8,128)(2,1)S(1)} %get-tuple-element.83.refs_0_), channel_id=1, source_target_pairs={{0,1},{1,0},{2,3},{3,2},{4,5},{5,4},{6,7},{7,6},{8,9},{9,8},{10,11... | collective-permute-start | bytes 1572872 | tf_op jit(solution)/shard_map/ppermute | solution.py:28
  46.1 40.8 %collective-permute-start.4 = (bf16[2,64,2048]{2,1,0:T(8,128)(2,1)S(1)}, bf16[2,64,2048]{2,1,0:T(8,128)(2,1)S(1)}, u32[]{:S(2)}, u32[]{:S(2)}) collective-permute-start(bf16[2,64,2048]{2,1,0:T(8,128)(2,1)S(1)} %collective-permute-done.2.refs_1_), channel_id=1, source_target_pairs={{0,1},{1,0},{2,3},{3,2},{4,5},{5,4},{6,7},{7,6},{8,9},{9,8},{10,11... | collective-permute-start | bytes 1572872 | tf_op jit(solution)/shard_map/ppermute | solution.py:28
  58.7 28.4 %collective-permute-start.8 = (bf16[2,64,2048]{2,1,0:T(8,128)(2,1)S(1)}, bf16[2,64,2048]{2,1,0:T(8,128)(2,1)S(1)}, u32[]{:S(2)}, u32[]{:S(2)}) collective-permute-start(bf16[2,64,2048]{2,1,0:T(8,128)(2,1)S(1)} %get-tuple-element.92), channel_id=1, source_target_pairs={{0,2},{1,3},{2,0},{3,1},{4,6},{5,7},{6,4},{7,5},{8,10},{9,11},{10,... | collective-permute-start | bytes 1572872 | tf_op jit(solution)/shard_map/ppermute | solution.py:28
  82.6 10.8 %collective-permute-start.9 = (bf16[2,64,2048]{2,1,0:T(8,128)(2,1)S(1)}, bf16[2,64,2048]{2,1,0:T(8,128)(2,1)S(1)}, u32[]{:S(2)}, u32[]{:S(2)}) collective-permute-start(bf16[2,64,2048]{2,1,0:T(8,128)(2,1)S(1)} %get-tuple-element.91.refs_0_), channel_id=1, source_target_pairs={{0,1},{1,0},{2,3},{3,2},{4,5},{5,4},{6,7},{7,6},{8,9},{9,8},{10,11... | collective-permute-start | bytes 1572872 | tf_op jit(solution)/shard_map/ppermute | solution.py:28
  84.5 12.5 %collective-permute-start.19 = (bf16[2,64,2048]{2,1,0:T(8,128)(2,1)S(1)}, bf16[2,64,2048]{2,1,0:T(8,128)(2,1)S(1)}, u32[]{:S(2)}, u32[]{:S(2)}) collective-permute-start(bf16[2,64,2048]{2,1,0:T(8,128)(2,1)S(1)} %get-tuple-element.96), channel_id=1, source_target_pairs={{0,2},{1,3},{2,0},{3,1},{4,6},{5,7},{6,4},{7,5},{8,10},{9,11},{10,... | collective-permute-start | bytes 1572872 | tf_op jit(solution)/shard_map/ppermute | solution.py:28
  85.5 20.8 %collective-permute-start.31 = (bf16[2,64,2048]{2,1,0:T(8,128)(2,1)S(1)}, bf16[2,64,2048]{2,1,0:T(8,128)(2,1)S(1)}, u32[]{:S(2)}, u32[]{:S(2)}) collective-permute-start(bf16[2,64,2048]{2,1,0:T(8,128)(2,1)S(1)} %get-tuple-element.104), channel_id=1, source_target_pairs={{0,2},{1,3},{2,0},{3,1},{4,6},{5,7},{6,4},{7,5},{8,10},{9,11},{10,... | collective-permute-start | bytes 1572872 | tf_op jit(solution)/shard_map/ppermute | solution.py:28
  86.9 21.6 %collective-permute-start.28 = (bf16[2,64,2048]{2,1,0:T(8,128)(2,1)S(1)}, bf16[2,64,2048]{2,1,0:T(8,128)(2,1)S(1)}, u32[]{:S(2)}, u32[]{:S(2)}) collective-permute-start(bf16[2,64,2048]{2,1,0:T(8,128)(2,1)S(1)} %get-tuple-element.101.refs_0_), channel_id=1, source_target_pairs={{0,1},{1,0},{2,3},{3,2},{4,5},{5,4},{6,7},{7,6},{8,9},{9,8},{10,11... | collective-permute-start | bytes 1572872 | tf_op jit(solution)/shard_map/ppermute | solution.py:28
  87.1 28.7 %collective-permute-start.10 = (bf16[2,64,2048]{2,1,0:T(8,128)(2,1)S(1)}, bf16[2,64,2048]{2,1,0:T(8,128)(2,1)S(1)}, u32[]{:S(2)}, u32[]{:S(2)}) collective-permute-start(bf16[2,64,2048]{2,1,0:T(8,128)(2,1)S(1)} %collective-permute-done.8.refs_1_), channel_id=1, source_target_pairs={{0,1},{1,0},{2,3},{3,2},{4,5},{5,4},{6,7},{7,6},{8,9},{9,8},{10,11... | collective-permute-start | bytes 1572872 | tf_op jit(solution)/shard_map/ppermute | solution.py:28
  93.4 33.7 %collective-permute-start.20 = (bf16[2,64,2048]{2,1,0:T(8,128)(2,1)S(1)}, bf16[2,64,2048]{2,1,0:T(8,128)(2,1)S(1)}, u32[]{:S(2)}, u32[]{:S(2)}) collective-permute-start(bf16[2,64,2048]{2,1,0:T(8,128)(2,1)S(1)} %get-tuple-element.95.refs_0_), channel_id=1, source_target_pairs={{0,1},{1,0},{2,3},{3,2},{4,5},{5,4},{6,7},{7,6},{8,9},{9,8},{10,11... | collective-permute-start | bytes 1572872 | tf_op jit(solution)/shard_map/ppermute | solution.py:28
  97.0 41.3 %collective-permute-start.21 = (bf16[2,64,2048]{2,1,0:T(8,128)(2,1)S(1)}, bf16[2,64,2048]{2,1,0:T(8,128)(2,1)S(1)}, u32[]{:S(2)}, u32[]{:S(2)}) collective-permute-start(bf16[2,64,2048]{2,1,0:T(8,128)(2,1)S(1)} %collective-permute-done.19.refs_1_), channel_id=1, source_target_pairs={{0,1},{1,0},{2,3},{3,2},{4,5},{5,4},{6,7},{7,6},{8,9},{9,8},{10,11... | collective-permute-start | bytes 1572872 | tf_op jit(solution)/shard_map/ppermute | solution.py:28
  106.4 50.8 %collective-permute-start.5 = (bf16[2,64,2048]{2,1,0:T(8,128)(2,1)S(1)}, bf16[2,64,2048]{2,1,0:T(8,128)(2,1)S(1)}, u32[]{:S(2)}, u32[]{:S(2)}) collective-permute-start(bf16[2,64,2048]{2,1,0:T(8,128)(2,1)S(1)} %get-tuple-element.89), channel_id=1, source_target_pairs={{16,18},{17,19},{18,16},{19,17},{20,22},{21,23},{22,20},{23,21},{2... | collective-permute-start | bytes 1572872 | tf_op jit(solution)/shard_map/ppermute | solution.py:28
  108.5 52.4 %collective-permute-start.32 = (bf16[2,64,2048]{2,1,0:T(8,128)(2,1)S(1)}, bf16[2,64,2048]{2,1,0:T(8,128)(2,1)S(1)}, u32[]{:S(2)}, u32[]{:S(2)}) collective-permute-start(bf16[2,64,2048]{2,1,0:T(8,128)(2,1)S(1)} %collective-permute-done.31.refs_0_), channel_id=1, source_target_pairs={{0,1},{1,0},{2,3},{3,2},{4,5},{5,4},{6,7},{7,6},{8,9},{9,8},{10,11... | collective-permute-start | bytes 1572872 | tf_op jit(solution)/shard_map/ppermute | solution.py:28
  115.9 50.5 %collective-permute-start.29 = (bf16[64,2048]{1,0:T(8,128)(2,1)S(1)}, bf16[64,2048]{1,0:T(8,128)(2,1)S(1)}, u32[]{:S(2)}, u32[]{:S(2)}) collective-permute-start(bf16[64,2048]{1,0:T(8,128)(2,1)S(1)} %get-tuple-element.103), channel_id=1, source_target_pairs={{16,17},{17,16},{18,19},{19,18},{20,21},{21,20},{22,23},{23,22},{2... | collective-permute-start | bytes 786440 | tf_op jit(solution)/shard_map/ppermute | solution.py:28
  127.1 28.1 %collective-permute-start.1 = (f32[4,128]{1,0:T(4,128)S(1)}, f32[4,128]{1,0:T(4,128)S(1)}, u32[]{:S(2)}, u32[]{:S(2)}) collective-permute-start(f32[4,128]{1,0:T(4,128)S(1)} %get-tuple-element.82.mine_ref.code_ref), channel_id=1, source_target_pairs={{16,17},{17,16},{18,19},{19,18},{20,21},{21,20},{22,23},{23,22},{2... | collective-permute-start | bytes 6152 | tf_op jit(solution)/shard_map/ppermute | solution.py:28
  138.3 31.2 %collective-permute-start.11 = (bf16[2,64,2048]{2,1,0:T(8,128)(2,1)S(1)}, bf16[2,64,2048]{2,1,0:T(8,128)(2,1)S(1)}, u32[]{:S(2)}, u32[]{:S(2)}) collective-permute-start(bf16[2,64,2048]{2,1,0:T(8,128)(2,1)S(1)} %get-tuple-element.93), channel_id=1, source_target_pairs={{16,20},{17,21},{18,22},{19,23},{20,16},{21,17},{22,18},{23,19},{2... | collective-permute-start | bytes 1572872 | tf_op jit(solution)/shard_map/ppermute | solution.py:28
  155.2 15.6 %collective-permute-start.12 = (bf16[2,64,2048]{2,1,0:T(8,128)(2,1)S(1)}, bf16[2,64,2048]{2,1,0:T(8,128)(2,1)S(1)}, u32[]{:S(2)}, u32[]{:S(2)}) collective-permute-start(bf16[2,64,2048]{2,1,0:T(8,128)(2,1)S(1)} %get-tuple-element.94), channel_id=1, source_target_pairs={{16,22},{17,23},{18,20},{19,21},{20,18},{21,19},{22,16},{23,17},{2... | collective-permute-start | bytes 1572872 | tf_op jit(solution)/shard_map/ppermute | solution.py:28
  157.2 25.0 %collective-permute-start.22 = (bf16[2,64,2048]{2,1,0:T(8,128)(2,1)S(1)}, bf16[2,64,2048]{2,1,0:T(8,128)(2,1)S(1)}, u32[]{:S(2)}, u32[]{:S(2)}) collective-permute-start(bf16[2,64,2048]{2,1,0:T(8,128)(2,1)S(1)} %get-tuple-element.97), channel_id=1, source_target_pairs={{16,24},{17,25},{18,26},{19,27},{20,28},{21,29},{22,30},{23,31},{2... | collective-permute-start | bytes 1572872 | tf_op jit(solution)/shard_map/ppermute | solution.py:28
  160.9 27.3 %collective-permute-start.23 = (bf16[2,64,2048]{2,1,0:T(8,128)(2,1)S(1)}, bf16[2,64,2048]{2,1,0:T(8,128)(2,1)S(1)}, u32[]{:S(2)}, u32[]{:S(2)}) collective-permute-start(bf16[2,64,2048]{2,1,0:T(8,128)(2,1)S(1)} %get-tuple-element.98), channel_id=1, source_target_pairs={{16,26},{17,27},{18,24},{19,25},{20,30},{21,31},{22,28},{23,29},{2... | collective-permute-start | bytes 1572872 | tf_op jit(solution)/shard_map/ppermute | solution.py:28
  166.4 25.5 %collective-permute-start.33 = (bf16[64,2048]{1,0:T(8,128)(2,1)S(1)}, bf16[64,2048]{1,0:T(8,128)(2,1)S(1)}, u32[]{:S(2)}, u32[]{:S(2)}) collective-permute-start(bf16[64,2048]{1,0:T(8,128)(2,1)S(1)} %get-tuple-element.106), channel_id=1, source_target_pairs={{16,17},{17,16},{18,19},{19,18},{20,21},{21,20},{22,23},{23,22},{2... | collective-permute-start | bytes 786440 | tf_op jit(solution)/shard_map/ppermute | solution.py:28
  169.5 50.8 %collective-permute-start.30 = (bf16[64,2048]{1,0:T(8,128)(2,1)S(1)}, bf16[64,2048]{1,0:T(8,128)(2,1)S(1)}, u32[]{:S(2)}, u32[]{:S(2)}) collective-permute-start(bf16[64,2048]{1,0:T(8,128)(2,1)S(1)} %add_convert_fusion.1), channel_id=1, source_target_pairs={{16,12},{17,13},{18,14},{19,15},{20,8},{21,9},{22,10},{23,11},{24,... | collective-permute-start | bytes 786440 | tf_op jit(solution)/shard_map/ppermute | solution.py:28
  189.2 31.1 %collective-permute-start.24 = (bf16[128,2048]{1,0:T(8,128)(2,1)S(1)}, bf16[128,2048]{1,0:T(8,128)(2,1)S(1)}, u32[]{:S(2)}, u32[]{:S(2)}) collective-permute-start(bf16[128,2048]{1,0:T(8,128)(2,1)S(1)} %get-tuple-element.99), channel_id=1, source_target_pairs={{16,0},{17,1},{18,2},{19,3},{20,4},{21,5},{22,6},{23,7},{24,8},{25... | collective-permute-start | bytes 1572872 | tf_op jit(solution)/shard_map/ppermute | solution.py:28
  190.6 29.8 %collective-permute-start.25 = (bf16[128,2048]{1,0:T(8,128)(2,1)S(1)}, bf16[128,2048]{1,0:T(8,128)(2,1)S(1)}, u32[]{:S(2)}, u32[]{:S(2)}) collective-permute-start(bf16[128,2048]{1,0:T(8,128)(2,1)S(1)} %get-tuple-element.100), channel_id=1, source_target_pairs={{16,1},{17,0},{18,3},{19,2},{20,5},{21,4},{22,7},{23,6},{24,9},{25... | collective-permute-start | bytes 1572872 | tf_op jit(solution)/shard_map/ppermute | solution.py:28
  192.0 28.4 %collective-permute-start.34 = (bf16[64,2048]{1,0:T(8,128)(2,1)S(1)}, bf16[64,2048]{1,0:T(8,128)(2,1)S(1)}, u32[]{:S(2)}, u32[]{:S(2)}) collective-permute-start(bf16[64,2048]{1,0:T(8,128)(2,1)S(1)} %add_convert_fusion), channel_id=1, source_target_pairs={{16,14},{17,15},{18,12},{19,13},{20,10},{21,11},{22,8},{23,9},{24,... | collective-permute-start | bytes 786440 | tf_op jit(solution)/shard_map/ppermute | solution.py:28
  193.3 6.6 %collective-permute-start.35 = (f32[8,64]{1,0:T(8,128)S(1)}, f32[8,64]{1,0:T(8,128)S(1)}, u32[]{:S(2)}, u32[]{:S(2)}) collective-permute-start(f32[8,64]{1,0:T(8,128)S(1)} %get-tuple-element.118), channel_id=1, source_target_pairs={{0,1},{1,0},{2,3},{3,2},{4,5},{5,4},{6,7},{7,6},{8,9},{9,8},{10,11... | collective-permute-start | bytes 6152 | tf_op jit(solution)/shard_map/ppermute | solution.py:28
  199.9 2.5 %collective-permute-start.36 = (f32[4,64]{1,0:T(4,128)S(1)}, f32[4,64]{1,0:T(4,128)S(1)}, u32[]{:S(2)}, u32[]{:S(2)}) collective-permute-start(f32[4,64]{1,0:T(4,128)S(1)} %get-tuple-element.120), channel_id=1, source_target_pairs={{0,2},{1,3},{2,0},{3,1},{4,6},{5,7},{6,4},{7,5},{8,10},{9,11},{10,... | collective-permute-start | bytes 3080 | tf_op jit(solution)/shard_map/ppermute | solution.py:28
  202.4 2.4 %collective-permute-start.37 = (f32[4,64]{1,0:T(4,128)S(1)}, f32[4,64]{1,0:T(4,128)S(1)}, u32[]{:S(2)}, u32[]{:S(2)}) collective-permute-start(f32[4,64]{1,0:T(4,128)S(1)} %get-tuple-element.122), channel_id=1, source_target_pairs={{0,4},{1,5},{2,6},{3,7},{4,0},{5,1},{6,2},{7,3},{8,12},{9,13},{10,... | collective-permute-start | bytes 3080 | tf_op jit(solution)/shard_map/ppermute | solution.py:28
  204.9 3.3 %collective-permute-start.38 = (f32[4,64]{1,0:T(4,128)S(1)}, f32[4,64]{1,0:T(4,128)S(1)}, u32[]{:S(2)}, u32[]{:S(2)}) collective-permute-start(f32[4,64]{1,0:T(4,128)S(1)} %get-tuple-element.124), channel_id=1, source_target_pairs={{0,8},{1,9},{2,10},{3,11},{4,12},{5,13},{6,14},{7,15},{8,0},{9,1},... | collective-permute-start | bytes 3080 | tf_op jit(solution)/shard_map/ppermute | solution.py:28
  208.2 12.1 %collective-permute-start = (f32[4,128]{1,0:T(4,128)S(1)}, f32[4,128]{1,0:T(4,128)S(1)}, u32[]{:S(2)}, u32[]{:S(2)}) collective-permute-start(f32[4,128]{1,0:T(4,128)S(1)} %get-tuple-element.82.mine_ref.code_ref), channel_id=1, source_target_pairs={{16,0},{17,1},{18,2},{19,3},{20,4},{21,5},{22,6},{23,7},{24,8},{25... | collective-permute-start | bytes 6152 | tf_op jit(solution)/shard_map/ppermute | solution.py:28
